TPU v7x, 32 devices: a whole 2x2x4 slice. The times are simulated.
32 devices in a mesh: dp: 8 (over z, x), mp: 4 (over y, core).
Axes of the slice: x: 2, y: 2, z: 4, core: 2. Of those that a mesh axis runs over, the one named last changes fastest.
Arguments:
- hidden_in: bfloat16 [16, 1024, 768], P(None, 'dp'), may hold values from -12 to 12
- cotangent: bfloat16 [16, 1024, 768], P(None, 'dp'), may hold values from -6 to 6
- lengths: int32 [16], replicated, may hold values from 1 to 1024, 9830 in all
- labels: int32 [16], replicated, may hold values from 0 to 13
- qkv_weight: bfloat16 [3, 768, 768], P(None, 'dp', 'mp'), may hold values from -0.15625 to 0.15625
- qv_bias: bfloat16 [12, 128], P('mp', 'dp'), may hold values from -1.796875 to 1.796875
- out_weight: bfloat16 [768, 768], P('mp', 'dp'), may hold values from -1.25 to 1.25
- out_bias: bfloat16 [768], P('dp'), may hold values from -1.796875 to 1.796875
- norm1_gain: bfloat16 [768], P('dp'), may hold values from 0.5 to 1.5
- norm1_bias: bfloat16 [768], P('dp'), may hold values from -1.796875 to 1.796875
- up_weight: bfloat16 [768, 3072], P('dp', 'mp'), may hold values from -0.21875 to 0.21875
- up_bias: bfloat16 [48, 64], P('mp', 'dp'), may hold values from -1.796875 to 1.796875
- down_weight: bfloat16 [3072, 768], P('mp', 'dp'), may hold values from -0.15625 to 0.15625
- down_bias: bfloat16 [768], P('dp'), may hold values from -1.796875 to 1.796875
- norm2_gain: bfloat16 [768], P('dp'), may hold values from 0.5 to 1.5
- norm2_bias: bfloat16 [768], P('dp'), may hold values from -1.796875 to 1.796875
- student_weight: bfloat16 [768, 128], P('dp'), may hold values from -0.21875 to 0.21875
- student_bias: bfloat16 [128], P('dp'), may hold values from -3 to 3
- pool_query: bfloat16 [128], P('dp'), may hold values from -9 to 9
- pooler_weight: bfloat16 [128, 128], P('dp'), may hold values from -0.5 to 0.5
- pooler_bias: bfloat16 [128], P('dp'), may hold values from -1.796875 to 1.796875
- class_weight: bfloat16 [128, 14], P('dp'), may hold values from -1 to 1
- class_bias: bfloat16 [14], replicated, may hold values from -6 to 6
Outputs:
- hidden_out: bfloat16 [16, 1024, 768], P(None, 'dp')
- logits: float32 [16, 14], replicated
- input_grad: bfloat16 [16, 1024, 768], P(None, 'dp')
- qkv_weight_grad: float32 [3, 768, 768], P(None, 'dp', 'mp')
- qv_bias_grad: float32 [12, 128], P('mp', 'dp')
- out_weight_grad: float32 [768, 768], P('mp', 'dp')
- out_bias_grad: float32 [768], P('dp')
- norm1_gain_grad: float32 [768], P('dp')
- norm1_bias_grad: float32 [768], P('dp')
- up_weight_grad: float32 [768, 3072], P('dp', 'mp')
- up_bias_grad: float32 [48, 64], P('mp', 'dp')
- down_weight_grad: float32 [3072, 768], P('mp', 'dp')
- down_bias_grad: float32 [768], P('dp')
- norm2_gain_grad: float32 [768], P('dp')
- norm2_bias_grad: float32 [768], P('dp')
- student_weight_grad: float32 [768, 128], P('dp')
- student_bias_grad: float32 [128], P('dp')
- pool_query_grad: float32 [128], P('dp')
- pooler_weight_grad: float32 [128, 128], P('dp')
- pooler_bias_grad: float32 [128], P('dp')
- class_weight_grad: float32 [128, 14], P('dp')
- class_bias_grad: float32 [14], replicated
- rms_stats: float32 [4], replicated
Inputs may be any that keep to these rules, and one draw needn't show every extreme that they name: `lengths`: every sequence has at least one live position, and some sequence fills its whole slot of 1024 positions.
All inputs are finite; a program needn't handle non-finite values.
Results may differ from a plain program's by a relative error of at most 0.03.
Values may be sent and summed in bfloat16 or wider, within the bound.
No kernel may reach another device: no remote copies, remote signals or barrier semaphores. Data moves between devices by JAX's collectives and lax.ppermute only.
A program may use at most 192 MiB of HBM per device.

v0:
```python
import jax
import jax.numpy as jnp
from jax import lax
from jax.sharding import PartitionSpec as P

D = 768
CW = 128
PH = 2
CLASSES = 14
MICRO = 2
SEQ_MB = 1


EPSILON = 1e-06
NEGATIVE = -1e30
HIGHEST = lax.Precision.HIGHEST


def cut_along(shard, dim, size):
    before, after = (shard.shape[:dim], shard.shape[dim + 1 :])
    return jnp.moveaxis(shard.reshape(*before, size, -1, *after), dim, 0)


def sum_at_owner(shard, axis, dim):
    blocks = cut_along(shard, dim, lax.axis_size(axis))
    arrived = lax.all_to_all(blocks, axis, split_axis=0, concat_axis=0, tiled=True)
    return arrived.astype(jnp.float32).sum(axis=0)


def in_one_piece(arrays, axis, dim, along):
    ends, at = ([], 0)
    for a in arrays[:-1]:
        at += a.shape[along]
        ends.append(at)
    both = jnp.concatenate(arrays, axis=along)
    return tuple(jnp.split(sum_at_owner(both, axis, dim), ends, axis=along))


def gelu_exact(values):
    return jax.nn.gelu(values, approximate=False)


def norm_forward(values, gain, shift):
    center = values - jnp.mean(values, -1, keepdims=True)
    spread = jnp.mean(center * center, -1, keepdims=True)
    row_scale = lax.rsqrt(spread + EPSILON)
    normed = center * row_scale
    return (normed * gain + shift, normed, row_scale)


def norm_backward(upstream, normed, row_scale, gain):
    scaled = upstream * gain
    inner = (
        scaled
        - jnp.mean(scaled, -1, keepdims=True)
        - normed * jnp.mean(scaled * normed, -1, keepdims=True)
    )
    return (
        inner * row_scale,
        jnp.sum(upstream * normed, axis=(0, 1)),
        jnp.sum(upstream, axis=(0, 1)),
    )


def attend_forward(item):
    queries, key_rows, value_rows, seq_length = item
    head_count, head_width, slot_rows = queries.shape
    block_rows = min(512, slot_rows // 2)
    block_count = slot_rows // block_rows
    score_scale = head_width ** (-0.5)
    branch_index = jnp.clip((seq_length + block_rows - 1) // block_rows, 1, block_count) - 1

    def one_block(first_row):
        query_block = lax.dynamic_slice_in_dim(queries, first_row, block_rows, 2)

        def with_keys(number):

            def compute(query_piece):
                key_piece = key_rows[:, :, : number * block_rows]
                value_piece = value_rows[:, :, : number * block_rows]
                raw_scores = jnp.einsum(
                    "heq,hek->hqk", query_piece, key_piece, preferred_element_type=jnp.float32
                )
                live_keys = jnp.arange(number * block_rows) < seq_length
                scores = jnp.where(live_keys, raw_scores * score_scale, NEGATIVE)
                row_max = jnp.max(scores, -1, keepdims=True)
                exponent = jnp.exp(scores - row_max)
                row_sum = jnp.sum(exponent, -1, keepdims=True)
                weights_low = (exponent / row_sum).astype(jnp.bfloat16)
                context = jnp.einsum(
                    "hqk,hek->heq", weights_low, value_piece, preferred_element_type=jnp.float32
                )
                return (context, (row_max + jnp.log(row_sum))[:, :, 0])

            return compute

        return lax.switch(
            branch_index, [with_keys(number) for number in range(1, block_count + 1)], query_block
        )

    block_starts = jnp.arange(block_count, dtype=jnp.int32) * block_rows
    context, log_total = lax.map(one_block, block_starts)
    context = jnp.transpose(context, (1, 2, 0, 3)).reshape(head_count * head_width, slot_rows)
    log_total = jnp.transpose(log_total, (1, 0, 2)).reshape(head_count, slot_rows)
    return (context, log_total)


def attend_backward(item):
    queries, key_rows, value_rows, grad_context, log_total, seq_length = item
    head_count, head_width, slot_rows = queries.shape
    block_rows = min(512, slot_rows // 2)
    block_count = slot_rows // block_rows
    score_scale = head_width ** (-0.5)
    branch_index = jnp.clip((seq_length + block_rows - 1) // block_rows, 1, block_count) - 1

    def one_block(carry, first_row):
        key_grad, value_grad = carry
        query_block = lax.dynamic_slice_in_dim(queries, first_row, block_rows, 2)
        grad_block = lax.dynamic_slice_in_dim(grad_context, first_row, block_rows, 2)
        log_block = lax.dynamic_slice_in_dim(log_total, first_row, block_rows, 1)

        def with_keys(number):

            def compute(operands):
                query_piece, grad_piece, log_piece = operands
                key_piece = key_rows[:, :, : number * block_rows]
                value_piece = value_rows[:, :, : number * block_rows]
                raw_scores = jnp.einsum(
                    "heq,hek->hqk", query_piece, key_piece, preferred_element_type=jnp.float32
                )
                live_keys = jnp.arange(number * block_rows) < seq_length
                scores = jnp.where(live_keys, raw_scores * score_scale, NEGATIVE)
                weights_full = jnp.exp(scores - log_piece[:, :, None])
                weights_low = weights_full.astype(jnp.bfloat16)
                grad_weights = jnp.einsum(
                    "heq,hek->hqk", grad_piece, value_piece, preferred_element_type=jnp.float32
                )
                row_dot = jnp.sum(weights_full * grad_weights, -1, keepdims=True)
                grad_raw = (weights_full * (grad_weights - row_dot) * score_scale).astype(
                    jnp.bfloat16
                )
                grad_query = jnp.einsum(
                    "hqk,hek->heq", grad_raw, key_piece, preferred_element_type=jnp.float32
                )
                grad_key = jnp.einsum(
                    "hqk,heq->hek", grad_raw, query_piece, preferred_element_type=jnp.float32
                )
                grad_value = jnp.einsum(
                    "hqk,heq->hek", weights_low, grad_piece, preferred_element_type=jnp.float32
                )
                padding = ((0, 0), (0, 0), (0, slot_rows - number * block_rows))
                return (grad_query, jnp.pad(grad_key, padding), jnp.pad(grad_value, padding))

            return compute

        grad_query, grad_key, grad_value = lax.switch(
            branch_index,
            [with_keys(number) for number in range(1, block_count + 1)],
            (query_block, grad_block, log_block),
        )
        return ((key_grad + grad_key, value_grad + grad_value), grad_query)

    zero_grad = jnp.zeros((head_count, head_width, slot_rows), jnp.float32)
    block_starts = jnp.arange(block_count, dtype=jnp.int32) * block_rows
    (key_grad, value_grad), query_grad = lax.scan(one_block, (zero_grad, zero_grad), block_starts)
    query_grad = jnp.transpose(query_grad, (1, 2, 0, 3)).reshape(head_count * head_width, slot_rows)
    return (
        query_grad,
        key_grad.reshape(head_count * head_width, slot_rows),
        value_grad.reshape(head_count * head_width, slot_rows),
    )


def attention_back(
    grad_attn_low,
    context_low,
    out_full,
    qkv_full,
    tokens,
    queries,
    key_rows,
    value_rows,
    log_total,
    seq_lengths,
    head_shape,
):
    head_count, head_width = (head_shape[1], head_shape[2])
    grad_out = jnp.einsum(
        "set,std->ed", context_low, grad_attn_low, preferred_element_type=jnp.float32
    )
    grad_context = jnp.einsum(
        "std,ed->set", grad_attn_low, out_full, preferred_element_type=jnp.float32
    )
    grad_context = grad_context.astype(jnp.bfloat16).reshape(head_shape)
    grad_query, grad_key, grad_value = lax.map(
        attend_backward, (queries, key_rows, value_rows, grad_context, log_total, seq_lengths)
    )
    grad_proj = jnp.stack([grad_query, grad_key, grad_value]).astype(jnp.bfloat16)
    grad_proj_float = grad_proj.astype(jnp.float32)
    grad_qv = jnp.concatenate(
        [
            jnp.sum(grad_proj_float[0], axis=(0, 2)).reshape(head_count, head_width),
            jnp.sum(grad_proj_float[2], axis=(0, 2)).reshape(head_count, head_width),
        ],
        axis=1,
    )
    grad_qkv = jnp.einsum("cset,std->cde", grad_proj, tokens, preferred_element_type=jnp.float32)
    grad_token_part = jnp.einsum(
        "cset,cde->std", grad_proj, qkv_full, preferred_element_type=jnp.float32
    )
    return (grad_out, grad_qv, grad_qkv, grad_token_part)


def micro_step(held, class_bias, tokens, cot_rows, seq_lengths, seq_labels):
    (
        qkv_full,
        out_full,
        up_full,
        down_full,
        qv_full,
        up_bias_full,
        wide_full,
        student_full,
        pooler_full,
        class_full,
        narrow_full,
    ) = held
    seq_count, slot_rows, _ = tokens.shape
    head_count = qv_full.shape[0]
    head_width = qv_full.shape[1] // 2
    local_width = head_count * head_width
    wide_float = wide_full.astype(jnp.float32)
    narrow_float = narrow_full.astype(jnp.float32)
    out_bias, gain_one, shift_one = (wide_float[0], wide_float[1], wide_float[2])
    down_bias, gain_two, shift_two = (wide_float[3], wide_float[4], wide_float[5])
    student_bias, pool_query, pooler_bias = (narrow_float[0], narrow_float[1], narrow_float[2])
    pooler_float = pooler_full.astype(jnp.float32)
    class_float = class_full.astype(jnp.float32)
    pool_width = CW // PH
    pool_scale = pool_width ** (-0.5)
    query_bias = qv_full[:, :head_width].reshape(local_width).astype(jnp.float32)
    value_bias = qv_full[:, head_width:].reshape(local_width).astype(jnp.float32)
    token_float = tokens.astype(jnp.float32)
    projected = jnp.einsum("cde,std->cset", qkv_full, tokens, preferred_element_type=jnp.float32)
    head_shape = (seq_count, head_count, head_width, slot_rows)
    queries = (projected[0] + query_bias[None, :, None]).astype(jnp.bfloat16).reshape(head_shape)
    key_rows = projected[1].astype(jnp.bfloat16).reshape(head_shape)
    value_rows = (projected[2] + value_bias[None, :, None]).astype(jnp.bfloat16).reshape(head_shape)
    context, log_total = lax.map(attend_forward, (queries, key_rows, value_rows, seq_lengths))
    context_low = context.astype(jnp.bfloat16)
    partial_attn = jnp.einsum(
        "set,ed->std", context_low, out_full, preferred_element_type=jnp.float32
    )
    attention = lax.psum(partial_attn.astype(jnp.bfloat16), "mp").astype(jnp.float32) + out_bias
    first, normed_one, scale_one = norm_forward(token_float + attention, gain_one, shift_one)
    first_low = first.astype(jnp.bfloat16)
    before = jnp.einsum("std,df->stf", first_low, up_full, preferred_element_type=jnp.float32)
    before = before + up_bias_full.reshape(-1).astype(jnp.float32)
    active_low = gelu_exact(before).astype(jnp.bfloat16)
    partial_ffn = jnp.einsum(
        "stf,fd->std", active_low, down_full, preferred_element_type=jnp.float32
    )
    feed = lax.psum(partial_ffn.astype(jnp.bfloat16), "mp").astype(jnp.float32) + down_bias
    second, normed_two, scale_two = norm_forward(first + feed, gain_two, shift_two)
    second_low = second.astype(jnp.bfloat16)
    student = (
        jnp.einsum("std,dc->stc", second_low, student_full, preferred_element_type=jnp.float32)
        + student_bias
    )
    pool_heads = student.reshape(seq_count, slot_rows, PH, pool_width)
    query_pairs = pool_query.reshape(PH, pool_width)
    live_rows = jnp.arange(slot_rows)[None, :] < seq_lengths[:, None]
    pool_logit = jnp.einsum("sthe,he->sth", pool_heads, query_pairs, precision=HIGHEST) * pool_scale
    pool_logit = jnp.where(live_rows[:, :, None], pool_logit, NEGATIVE)
    pool_weights = jax.nn.softmax(pool_logit, axis=1)
    pooled = jnp.einsum("sth,sthe->she", pool_weights, pool_heads, precision=HIGHEST).reshape(
        seq_count, CW
    )
    hidden_cls = jnp.tanh(jnp.dot(pooled, pooler_float, precision=HIGHEST) + pooler_bias)
    logit_rows = jnp.dot(hidden_cls, class_float, precision=HIGHEST) + class_bias.astype(
        jnp.float32
    )
    live_float = live_rows.astype(jnp.float32)
    sums = jnp.stack(
        [
            jnp.sum(live_float * jnp.sum(stream * stream, -1))
            for stream in (token_float, attention, first, feed)
        ]
    )
    onehot = (jnp.arange(CLASSES)[None, :] == seq_labels[:, None]).astype(jnp.float32)
    grad_logits = jax.nn.softmax(logit_rows, axis=-1) - onehot
    grad_class_bias = jnp.sum(grad_logits, 0)
    grad_class = jnp.dot(hidden_cls.T, grad_logits, precision=HIGHEST)
    grad_hidden_cls = jnp.dot(grad_logits, class_float.T, precision=HIGHEST)
    grad_pre_cls = grad_hidden_cls * (1.0 - hidden_cls * hidden_cls)
    grad_pooler_bias = jnp.sum(grad_pre_cls, 0)
    grad_pooler = jnp.dot(pooled.T, grad_pre_cls, precision=HIGHEST)
    grad_pooled = jnp.dot(grad_pre_cls, pooler_float.T, precision=HIGHEST).reshape(
        seq_count, PH, pool_width
    )
    grad_pool_weights = jnp.einsum("she,sthe->sth", grad_pooled, pool_heads, precision=HIGHEST)
    grad_pool_logit = (
        pool_weights
        * (grad_pool_weights - jnp.sum(pool_weights * grad_pool_weights, axis=1, keepdims=True))
        * pool_scale
    )
    grad_pool_query = jnp.einsum(
        "sth,sthe->he", grad_pool_logit, pool_heads, precision=HIGHEST
    ).reshape(CW)
    grad_heads = jnp.einsum("sth,she->sthe", pool_weights, grad_pooled, precision=HIGHEST)
    grad_heads = grad_heads + jnp.einsum(
        "sth,he->sthe", grad_pool_logit, query_pairs, precision=HIGHEST
    )
    grad_student = grad_heads.reshape(seq_count, slot_rows, CW).astype(jnp.bfloat16)
    grad_student_bias = jnp.sum(grad_student.astype(jnp.float32), axis=(0, 1))
    grad_student_weight = jnp.einsum(
        "std,stc->dc", second_low, grad_student, preferred_element_type=jnp.float32
    )
    grad_second = jnp.einsum(
        "stc,dc->std", grad_student, student_full, preferred_element_type=jnp.float32
    )
    grad_second = grad_second + cot_rows.astype(jnp.float32)
    grad_sum_two, grad_gain_two, grad_shift_two = norm_backward(
        grad_second, normed_two, scale_two, gain_two
    )
    grad_down_bias = jnp.sum(grad_sum_two, axis=(0, 1))
    grad_feed_low = grad_sum_two.astype(jnp.bfloat16)
    grad_down = jnp.einsum(
        "stf,std->fd", active_low, grad_feed_low, preferred_element_type=jnp.float32
    )
    grad_active = jnp.einsum(
        "std,fd->stf", grad_feed_low, down_full, preferred_element_type=jnp.float32
    )
    grad_before = jax.vjp(gelu_exact, before)[1](grad_active)[0].astype(jnp.bfloat16)
    grad_up_bias = jnp.sum(grad_before.astype(jnp.float32), axis=(0, 1)).reshape(up_bias_full.shape)
    grad_up = jnp.einsum("std,stf->df", first_low, grad_before, preferred_element_type=jnp.float32)
    grad_first_part = jnp.einsum(
        "stf,df->std", grad_before, up_full, preferred_element_type=jnp.float32
    )
    grad_first = (
        lax.psum(grad_first_part.astype(jnp.bfloat16), "mp").astype(jnp.float32) + grad_sum_two
    )
    grad_sum_one, grad_gain_one, grad_shift_one = norm_backward(
        grad_first, normed_one, scale_one, gain_one
    )
    grad_out_bias = jnp.sum(grad_sum_one, axis=(0, 1))
    grad_attn_low = grad_sum_one.astype(jnp.bfloat16)
    grad_out, grad_qv, grad_qkv, grad_token_part = attention_back(
        grad_attn_low,
        context_low,
        out_full,
        qkv_full,
        tokens,
        queries,
        key_rows,
        value_rows,
        log_total,
        seq_lengths,
        head_shape,
    )
    grad_tokens = (
        lax.psum(grad_token_part.astype(jnp.bfloat16), "mp").astype(jnp.float32) + grad_sum_one
    )
    grad_wide = jnp.stack(
        [
            grad_out_bias,
            grad_gain_one,
            grad_shift_one,
            grad_down_bias,
            grad_gain_two,
            grad_shift_two,
        ]
    )
    grad_narrow = jnp.stack([grad_student_bias, grad_pool_query, grad_pooler_bias])
    grads = (
        grad_qkv,
        grad_out,
        grad_up,
        grad_down,
        grad_qv,
        grad_up_bias,
        grad_wide,
        grad_student_weight,
        grad_pooler,
        grad_class,
        grad_narrow,
    )
    return (second_low, grad_tokens.astype(jnp.bfloat16), logit_rows, sums, grad_class_bias, grads)


def body(
    hidden_in,
    cotangent,
    lengths,
    labels,
    qkv_weight,
    qv_bias,
    out_weight,
    out_bias,
    norm1_gain,
    norm1_bias,
    up_weight,
    up_bias,
    down_weight,
    down_bias,
    norm2_gain,
    norm2_bias,
    student_weight,
    student_bias,
    pool_query,
    pooler_weight,
    pooler_bias,
    class_weight,
    class_bias,
):
    data_count = lax.axis_size("dp")
    data_index = lax.axis_index("dp")
    total_seqs = hidden_in.shape[0]
    seq_dev = total_seqs // data_count
    seq_ids = jnp.arange(total_seqs, dtype=jnp.int32)
    inverse = jnp.sum(jnp.where(seq_ids[:, None] == seq_ids[None, :], seq_ids[:, None], 0), 0)
    mine = lax.dynamic_slice_in_dim(seq_ids, data_index * seq_dev, seq_dev)
    my_lengths = lengths[mine]
    my_labels = labels[mine]
    dealt_tokens, dealt_cot = (
        lax.all_to_all(hidden_in[seq_ids], "dp", split_axis=0, concat_axis=1, tiled=True),
        lax.all_to_all(cotangent[seq_ids], "dp", split_axis=0, concat_axis=1, tiled=True),
    )
    wide_vectors = jnp.stack([out_bias, norm1_gain, norm1_bias, down_bias, norm2_gain, norm2_bias])
    narrow_vectors = jnp.stack([student_bias, pool_query, pooler_bias])
    hidden_parts = []
    grad_parts = []
    logit_parts = []
    sums_total = jnp.zeros((4,), jnp.float32)
    class_bias_total = jnp.zeros((CLASSES,), jnp.float32)
    accumulated = None
    for micro in range(MICRO):
        held = (
            lax.all_gather(qkv_weight, "dp", axis=1, tiled=True),
            lax.all_gather(out_weight, "dp", axis=1, tiled=True),
            lax.all_gather(up_weight, "dp", axis=0, tiled=True),
            lax.all_gather(down_weight, "dp", axis=1, tiled=True),
            lax.all_gather(qv_bias, "dp", axis=1, tiled=True),
            lax.all_gather(up_bias, "dp", axis=1, tiled=True),
            lax.all_gather(wide_vectors, "dp", axis=1, tiled=True),
            lax.all_gather(student_weight, "dp", axis=0, tiled=True),
            lax.all_gather(pooler_weight, "dp", axis=0, tiled=True),
            lax.all_gather(class_weight, "dp", axis=0, tiled=True),
            lax.all_gather(narrow_vectors, "dp", axis=1, tiled=True),
        )
        lower = micro * SEQ_MB
        hidden_low, grad_low, logit_rows, sums, grad_class_bias, grads = micro_step(
            held,
            class_bias,
            dealt_tokens[lower : lower + SEQ_MB],
            dealt_cot[lower : lower + SEQ_MB],
            my_lengths[lower : lower + SEQ_MB],
            my_labels[lower : lower + SEQ_MB],
        )
        hidden_parts.append(hidden_low)
        grad_parts.append(grad_low)
        logit_parts.append(logit_rows)
        sums_total = sums_total + sums
        class_bias_total = class_bias_total + grad_class_bias
        if accumulated is None:
            accumulated = grads
        else:
            accumulated = jax.tree.map(lambda older, newer: older + newer, accumulated, grads)
    scattered = (
        sum_at_owner(accumulated[0].astype(jnp.bfloat16), "dp", 1),
        sum_at_owner(accumulated[1].astype(jnp.bfloat16), "dp", 1),
        sum_at_owner(accumulated[2].astype(jnp.bfloat16), "dp", 0),
        sum_at_owner(accumulated[3].astype(jnp.bfloat16), "dp", 1),
        sum_at_owner(accumulated[4].astype(jnp.bfloat16), "dp", 1),
        sum_at_owner(accumulated[5].astype(jnp.bfloat16), "dp", 1),
        sum_at_owner(accumulated[6].astype(jnp.bfloat16), "dp", 1),
        sum_at_owner(accumulated[7].astype(jnp.bfloat16), "dp", 0),
        *in_one_piece(
            (accumulated[8].astype(jnp.bfloat16), accumulated[9].astype(jnp.bfloat16)), "dp", 0, 1
        ),
        sum_at_owner(accumulated[10].astype(jnp.bfloat16), "dp", 1),
    )
    my_logits = jnp.concatenate(logit_parts, 0)
    owner = (seq_ids[:, None] == mine[None, :])[:, :, None]
    logit_table = jnp.sum(jnp.where(owner, my_logits[None, :, :], 0.0), 1)
    summed, class_bias_grad, logit_all = lax.psum((sums_total, class_bias_total, logit_table), "dp")
    rms_stats = jnp.sqrt(summed / (jnp.sum(lengths).astype(jnp.float32) * D))
    back_hidden, back_grad = (
        lax.all_to_all(
            jnp.concatenate(hidden_parts, 0), "dp", split_axis=1, concat_axis=0, tiled=True
        ),
        lax.all_to_all(
            jnp.concatenate(grad_parts, 0), "dp", split_axis=1, concat_axis=0, tiled=True
        ),
    )
    hidden_out = back_hidden[inverse]
    input_grad = back_grad[inverse]
    (
        grad_qkv,
        grad_out,
        grad_up,
        grad_down,
        grad_qv,
        grad_up_bias,
        grad_wide,
        grad_student_weight,
        grad_pooler,
        grad_class,
        grad_narrow,
    ) = scattered
    return (
        hidden_out,
        logit_all,
        input_grad,
        grad_qkv,
        grad_qv,
        grad_out,
        grad_wide[0],
        grad_wide[1],
        grad_wide[2],
        grad_up,
        grad_up_bias,
        grad_down,
        grad_wide[3],
        grad_wide[4],
        grad_wide[5],
        grad_student_weight,
        grad_narrow[0],
        grad_narrow[1],
        grad_pooler,
        grad_narrow[2],
        grad_class,
        class_bias_grad,
        rms_stats,
    )


def solution(mesh):
    placed = (
        P(None, "dp", None),
        P(None, "dp", None),
        P(),
        P(),
        P(None, "dp", "mp"),
        P("mp", "dp"),
        P("mp", "dp"),
        P("dp"),
        P("dp"),
        P("dp"),
        P("dp", "mp"),
        P("mp", "dp"),
        P("mp", "dp"),
        P("dp"),
        P("dp"),
        P("dp"),
        P("dp", None),
        P("dp"),
        P("dp"),
        P("dp", None),
        P("dp"),
        P("dp", None),
        P(),
    )
    return jax.shard_map(
        body,
        mesh=mesh,
        in_specs=placed,
        out_specs=(
            P(None, "dp", None),
            P(),
            P(None, "dp", None),
            P(None, "dp", "mp"),
            P("mp", "dp"),
            P("mp", "dp"),
            P("dp"),
            P("dp"),
            P("dp"),
            P("dp", "mp"),
            P("mp", "dp"),
            P("mp", "dp"),
            P("dp"),
            P("dp"),
            P("dp"),
            P("dp", None),
            P("dp"),
            P("dp"),
            P("dp", None),
            P("dp"),
            P("dp", None),
            P(),
            P(),
        ),
        check_vma=False,
    )
```

profile of v0, /device:TPU:0, one launch (start us, length us, event | category | flops | bytes accessed | tf_op | source)
XLA Modules:
  0.0 1219.6 jit_solution(4937769743754859489)
XLA Ops:
  12.3 7.4 all-to-all-start
  23.1 94.2 %all_gather.44 = bf16[3,768,192]{2,0,1:T(4,128)(2,1)S(1)} all-gather(bf16[3,96,192]{2,0,1:T(4,128)(2,1)S(1)} %copy.263), channel_id=1, replica_groups=mesh['dp'=8,'mp'=4] {'dp'}, dimensions={1}, use_global_device_ids=true | all-gather | bytes 995328 | tf_op jit(solution)/shard_map/all_gather | solution.py:439
  119.4 18.3 %all-gather = bf16[8,16,3]{1,2,0:T(4,128)(2,1)S(1)} all-gather(bf16[1,16,3]{1,2,0:T(4,128)(2,1)S(1)} %bitcast.777), channel_id=1, replica_groups=mesh['dp'=8,'mp'=4] {'dp'}, dimensions={0}, use_global_device_ids=true | all-gather | bytes 864 | tf_op jit(solution)/shard_map/all_gather | solution.py:443
  138.0 33.0 %all_gather.46 = bf16[192,768]{0,1:T(8,128)(2,1)} all-gather(bf16[192,96]{0,1:T(8,128)(2,1)S(1)} %copy.267), channel_id=1, replica_groups=mesh['dp'=8,'mp'=4] {'dp'}, dimensions={1}, use_global_device_ids=true | all-gather | bytes 331776 | tf_op jit(solution)/shard_map/all_gather | solution.py:440
  182.2 20.8 %while.103 = (s32[]{:T(128)}, bf16[2,3,64,512]{3,2,1,0:T(8,128)(2,1)}, f32[2,3,512]{2,1,0:T(4,128)}, s32[2]{0:T(128)S(1)}, bf16[3,64,1024]{2,1,0:T(8,128)(2,1)},...) while((s32[]{:T(128)}, ...), condition=%wide.region_21.22_spmd, body=%wide.region_14.21_spmd.sunk | while | flops 421527040 | bytes 22482200 | solution.py:102
  186.0 5.4 conditional.11
  196.3 5.4 conditional.11
  206.7 18.2 %while.102 = (s32[]{:T(128)}, bf16[2,3,64,512]{3,2,1,0:T(8,128)(2,1)}, f32[2,3,512]{2,1,0:T(4,128)}, s32[2]{0:T(128)S(1)}, bf16[3,64,1024]{2,1,0:T(8,128)(2,1)},...) while((s32[]{:T(128)}, ...), condition=%wide.region_7.8_spmd, body=%wide.region_0.7_spmd.sunk | while | flops 421527040 | bytes 22482200 | solution.py:102
  219.3 4.1 conditional.10
  232.0 4.4 gather_fusion.4
  236.5 5.2 all-to-all-start.2
  242.4 91.1 %all-gather.1 = bf16[8,96,6]{1,2,0:T(8,128)(2,1)S(1)} all-gather(bf16[1,96,6]{1,2,0:T(8,128)(2,1)S(1)} %bitcast.763), channel_id=1, replica_groups=mesh['dp'=8,'mp'=4] {'dp'}, dimensions={0}, use_global_device_ids=true | all-gather | bytes 10368 | tf_op jit(solution)/shard_map/all_gather | solution.py:445
  333.7 26.0 %all_gather.49 = bf16[12,64]{0,1:T(8,128)(2,1)S(1)} all-gather(bf16[12,8]{0,1:T(8,128)(2,1)S(1)} %copy-done.106), channel_id=1, replica_groups=mesh['dp'=8,'mp'=4] {'dp'}, dimensions={1}, use_global_device_ids=true | all-gather | bytes 1728 | tf_op jit(solution)/shard_map/all_gather | solution.py:444
  375.6 16.4 %multiply_convert_fusion.5 = (bf16[1024,768]{1,0:T(8,128)(2,1)}, f32[1024,768]{1,0:T(8,128)}, bf16[1024,768]{1,0:T(8,128)(2,1)}, f32[1024,768]{1,0:T(8,128)}, f32[1024,768]{1,0:T(8,128)}) fusion(f32[768]{0:T(1024)S(1)} %reshape.1390, f32[1024,768]{1,0:T(8,128)S(1)} %fusion.303, bf16[768,768]{1,0:T(8,128)(2,1)S(1)} %copy-done.119, ...), kind=kOutput, calls=%fused_computation.252 | convolution fusion | flops 1314127872 | bytes 20063232 | tf_op jit(solution)/shard_map/std,df->stf/dot_general | solution.py:257
  392.1 4.5 fusion.247
  399.9 16.3 %all-gather.2 = bf16[8,16,3]{1,2,0:T(4,128)(2,1)S(1)} all-gather(bf16[1,16,3]{1,2,0:T(4,128)(2,1)S(1)} %maximum_bitcast_fusion), channel_id=1, replica_groups=mesh['dp'=8,'mp'=4] {'dp'}, dimensions={0}, use_global_device_ids=true | all-gather | bytes 864 | tf_op jit(solution)/shard_map/all_gather | solution.py:449
  417.8 30.9 %all_gather.54 = bf16[128,14]{1,0:T(8,128)(2,1)S(1)} all-gather(bf16[16,14]{1,0:T(8,128)(2,1)S(1)} %copy-done.104), channel_id=1, replica_groups=mesh['dp'=8,'mp'=4] {'dp'}, dimensions={0}, use_global_device_ids=true | all-gather | bytes 4032 | tf_op jit(solution)/shard_map/all_gather | solution.py:448
  448.6 30.5 %all_gather.53 = bf16[128,128]{1,0:T(8,128)(2,1)S(1)} all-gather(bf16[16,128]{1,0:T(8,128)(2,1)S(1)} %copy-done.105), channel_id=1, replica_groups=mesh['dp'=8,'mp'=4] {'dp'}, dimensions={0}, use_global_device_ids=true | all-gather | bytes 36864 | tf_op jit(solution)/shard_map/all_gather | solution.py:447
  479.1 30.6 %all_gather.52 = bf16[768,128]{1,0:T(8,128)(2,1)S(1)} all-gather(bf16[96,128]{1,0:T(8,128)(2,1)S(1)} %copy-done.85), channel_id=1, replica_groups=mesh['dp'=8,'mp'=4] {'dp'}, dimensions={0}, use_global_device_ids=true | all-gather | bytes 221184 | tf_op jit(solution)/shard_map/all_gather | solution.py:446
  515.8 5.3 multiply_reduce_fusion.4
  533.3 4.4 fusion.358
  587.2 5.0 fusion.222
  592.2 50.9 %all-reduce.16.cloned.1.call-done = (bf16[1,1024,768]{2,1,0:T(8,128)(2,1)}, bf16[1,1024,768]{2,1,0:T(8,128)(2,1)}) async-done(((bf16[1,1024,768]{2,1,0:T(8,128)(2,1)}, bf16[1,1024,768]{2,1,0:T(8,128)(2,1)}), (bf16[1,1024,768]{2,1,0:T(8,128)(2,1)}, bf16[1,1024,768]{2,1,0:T(8,128)(2,1)})) %all-reduce.16.cloned.1.call-update) | async-done | bytes 3145744 | tf_op jit(solution)/shard_map/psum | solution.py:341
  643.2 7.2 multiply_reduce_fusion.12
  657.8 5.8 all-to-all-start.9
  664.4 52.5 %while.104 = (s32[]{:T(128)}, f32[3,64,1024]{2,1,0:T(8,128)}, f32[3,64,1024]{2,1,0:T(8,128)}, bf16[2,3,64,512]{3,2,1,0:T(8,128)(2,1)}, s32[2]{0:T(128)S(1)}, /*i...) while((s32[]{:T(128)}, f32[3,64,1024]{2,1,0:T(8,128)}, ...), condition=%wide.region_48.49_spmd.clone, body=%wide.region_43.48_spmd.clone.sunk | while | flops 1048320000 | bytes 56855424 | solution.py:165
  668.1 19.5 %conditional.12 = (f32[3,64,1024]{2,1,0:T(8,128)S(1)}, f32[3,64,1024]{2,1,0:T(8,128)S(1)}, bf16[1,3,64,512]{3,2,1,0:T(8,128)(2,1)S(1)}) conditional(s32[]{:T(128)} %get-tuple-element.1670, (s32[]{:T(128)}, bf16[3,64,1024]{2,1,0:T(8,128)(2,1)S(1)}, bf16[3,64,512]{2,1,0:T(8,128)(2,1)S(1)}, f32[3,512]{1,0:T(4,128)S(1)}, ...), branch_computations={%region_44.45_spmd, %region_46.47_spmd} | conditional | flops 1047533568 | bytes 47798300 | solution.py:156
  673.7 5.6 fusion.47
  679.4 5.7 fusion.50
  693.6 19.5 %conditional.12 = (f32[3,64,1024]{2,1,0:T(8,128)S(1)}, f32[3,64,1024]{2,1,0:T(8,128)S(1)}, bf16[1,3,64,512]{3,2,1,0:T(8,128)(2,1)S(1)}) conditional(s32[]{:T(128)} %get-tuple-element.1670, (s32[]{:T(128)}, bf16[3,64,1024]{2,1,0:T(8,128)(2,1)S(1)}, bf16[3,64,512]{2,1,0:T(8,128)(2,1)S(1)}, f32[3,512]{1,0:T(4,128)S(1)}, ...), branch_computations={%region_44.45_spmd, %region_46.47_spmd} | conditional | flops 1047533568 | bytes 47798300 | solution.py:156
  699.2 5.6 fusion.47
  704.9 5.7 fusion.50
  716.9 45.0 %all-to-all-start.13 = ((bf16[8,16,142]{2,1,0:T(8,128)(2,1)}), bf16[8,16,142]{2,1,0:T(8,128)(2,1)S(1)}, u32[]{:S(2)}, u32[]{:S(2)}) async-start(bf16[8,16,142]{2,1,0:T(8,128)(2,1)} %bitcast.753), calls=%async_computation.13 | async-start | bytes 131072 | tf_op jit(solution)/shard_map/all_to_all | solution.py:26
  764.6 4.3 all-to-all-done.13
  773.5 95.4 %while.105 = (s32[]{:T(128)}, f32[3,64,1024]{2,1,0:T(8,128)}, f32[3,64,1024]{2,1,0:T(8,128)}, bf16[2,3,64,512]{3,2,1,0:T(8,128)(2,1)}, s32[2]{0:T(128)}, /*index...) while((s32[]{:T(128)}, f32[3,64,1024]{2,1,0:T(8,128)}, ...), condition=%wide.region_63.64_spmd.clone, body=%wide.region_58.63_spmd.clone.sunk | while | flops 1048320000 | bytes 56855424 | solution.py:165
  778.7 39.4 %conditional.13 = (f32[3,64,1024]{2,1,0:T(8,128)S(1)}, f32[3,64,1024]{2,1,0:T(8,128)S(1)}, bf16[1,3,64,512]{3,2,1,0:T(8,128)(2,1)S(1)}) conditional(s32[]{:T(128)} %get-tuple-element.1625, (s32[]{:T(128)}, bf16[3,64,1024]{2,1,0:T(8,128)(2,1)S(1)}, bf16[3,64,512]{2,1,0:T(8,128)(2,1)S(1)}, f32[3,512]{1,0:T(4,128)S(1)}, ...), branch_computations={%region_59.60_spmd, %region_61.62_spmd} | conditional | flops 1047533568 | bytes 47798300 | solution.py:156
  786.7 14.6 %fusion.176 = f32[3,64,1024]{2,1,0:T(8,128)S(1)} fusion(bf16[3,64,512]{2,1,0:T(8,128)(2,1)S(1)} %get-tuple-element.705, f32[3,512,1024]{2,1,0:T(8,128)} %fusion.378, f32[3,512,1024]{2,1,0:T(8,128)} %fusion.377, f32[3,512]{1,0:T(4,128)S(1)} %get-tuple-element.707, pred[1024]{0:T(1024)(128)(4,1)S(1)} %iota_compare_fusion.7), kind=kOutput, calls=%fused_computation.157 | convolution fusion | flops 218630656 | bytes 13573120 | tf_op jit(solution)/shard_map/while/body/eval_jaxpr/while/body/eval_jaxpr/cond/branch_1_fun/hqk,heq->hek/dot_general | solution.py:145
  801.3 12.6 %fusion.179 = bf16[1,3,64,512]{3,2,1,0:T(8,128)(2,1)S(1)} fusion(bf16[3,64,1024]{2,1,0:T(8,128)(2,1)S(1)} %get-tuple-element.706, f32[3,512,1024]{2,1,0:T(8,128)} %fusion.378, f32[3,512,1024]{2,1,0:T(8,128)} %fusion.377, f32[3,512]{1,0:T(4,128)S(1)} %get-tuple-element.707, pred[1024]{0:T(1024)(128)(4,1)S(1)} %iota_compare_fusion.7), kind=kOutput, calls=%fused_computation.158 | convolution fusion | flops 218630656 | bytes 13179904 | tf_op jit(solution)/shard_map/while/body/eval_jaxpr/while/body/eval_jaxpr/cond/branch_1_fun/hqk,hek->heq/dot_general | solution.py:142
  813.9 4.2 fusion.173
  825.6 39.4 %conditional.13 = (f32[3,64,1024]{2,1,0:T(8,128)S(1)}, f32[3,64,1024]{2,1,0:T(8,128)S(1)}, bf16[1,3,64,512]{3,2,1,0:T(8,128)(2,1)S(1)}) conditional(s32[]{:T(128)} %get-tuple-element.1625, (s32[]{:T(128)}, bf16[3,64,1024]{2,1,0:T(8,128)(2,1)S(1)}, bf16[3,64,512]{2,1,0:T(8,128)(2,1)S(1)}, f32[3,512]{1,0:T(4,128)S(1)}, ...), branch_computations={%region_59.60_spmd, %region_61.62_spmd} | conditional | flops 1047533568 | bytes 47798300 | solution.py:156
  833.6 14.6 %fusion.176 = f32[3,64,1024]{2,1,0:T(8,128)S(1)} fusion(bf16[3,64,512]{2,1,0:T(8,128)(2,1)S(1)} %get-tuple-element.705, f32[3,512,1024]{2,1,0:T(8,128)} %fusion.378, f32[3,512,1024]{2,1,0:T(8,128)} %fusion.377, f32[3,512]{1,0:T(4,128)S(1)} %get-tuple-element.707, pred[1024]{0:T(1024)(128)(4,1)S(1)} %iota_compare_fusion.7), kind=kOutput, calls=%fused_computation.157 | convolution fusion | flops 218630656 | bytes 13573120 | tf_op jit(solution)/shard_map/while/body/eval_jaxpr/while/body/eval_jaxpr/cond/branch_1_fun/hqk,heq->hek/dot_general | solution.py:145
  848.2 12.6 %fusion.179 = bf16[1,3,64,512]{3,2,1,0:T(8,128)(2,1)S(1)} fusion(bf16[3,64,1024]{2,1,0:T(8,128)(2,1)S(1)} %get-tuple-element.706, f32[3,512,1024]{2,1,0:T(8,128)} %fusion.378, f32[3,512,1024]{2,1,0:T(8,128)} %fusion.377, f32[3,512]{1,0:T(4,128)S(1)} %get-tuple-element.707, pred[1024]{0:T(1024)(128)(4,1)S(1)} %iota_compare_fusion.7), kind=kOutput, calls=%fused_computation.158 | convolution fusion | flops 218630656 | bytes 13179904 | tf_op jit(solution)/shard_map/while/body/eval_jaxpr/while/body/eval_jaxpr/cond/branch_1_fun/hqk,hek->heq/dot_general | solution.py:142
  860.8 4.2 fusion.173
  880.1 4.1 all-to-all-start.5
  884.9 5.9 all-to-all-done.5
  894.2 5.6 add_convert_fusion.6
  900.6 5.0 all-to-all-start.10
  912.3 18.3 %all-to-all-done.10 = bf16[8,768,96]{1,2,0:T(8,128)(2,1)} async-done(((bf16[8,768,96]{1,2,0:T(8,128)(2,1)}), bf16[8,768,96]{1,2,0:T(8,128)(2,1)}, u32[]{:S(2)}, u32[]{:S(2)}) %all-to-all-start.10) | async-done | bytes 1179680 | tf_op jit(solution)/shard_map/all_to_all | solution.py:26
  930.6 4.4 all-to-all-start.8
  942.5 19.1 %all-to-all-done.8 = bf16[8,96,768]{2,1,0:T(8,128)(2,1)} async-done(((bf16[8,96,768]{2,1,0:T(8,128)(2,1)}), bf16[8,96,768]{2,1,0:T(8,128)(2,1)}, u32[]{:S(2)}, u32[]{:S(2)}) %all-to-all-start.8) | async-done | bytes 1179680 | tf_op jit(solution)/shard_map/all_to_all | solution.py:26
  961.6 4.3 all-to-all-start.6
  971.0 4.3 fusion.256
  981.1 6.0 all-to-all-start.4
  989.2 4.9 copy.272
  994.1 20.5 %all-to-all-done.4 = bf16[8,3,96,192]{2,3,1,0:T(8,128)(2,1)} async-done(((bf16[8,3,96,192]{2,3,1,0:T(8,128)(2,1)}), bf16[8,3,96,192]{2,3,1,0:T(8,128)(2,1)}, u32[]{:S(2)}, u32[]{:S(2)}) %all-to-all-start.4) | async-done | bytes 884768 | tf_op jit(solution)/shard_map/all_to_all | solution.py:26
  1014.6 4.4 all-to-all-start.1
  1019.4 4.1 fusion.252
  1026.2 69.3 %all-reduce.14.cloned.1.call-done = (bf16[1,1024,768]{2,1,0:T(8,128)(2,1)}, bf16[1,1024,768]{2,1,0:T(8,128)(2,1)}) async-done(((bf16[1,1024,768]{2,1,0:T(8,128)(2,1)}, bf16[1,1024,768]{2,1,0:T(8,128)(2,1)}), (bf16[1,1024,768]{2,1,0:T(8,128)(2,1)}, bf16[1,1024,768]{2,1,0:T(8,128)(2,1)})) %all-reduce.14.cloned.1.call-update) | async-done | bytes 3145744 | tf_op jit(solution)/shard_map/psum | solution.py:362
  1099.1 4.9 copy.282
  1104.0 5.6 all-to-all-start.3
  1124.6 5.2 maximum_add_fusion.2
  1129.9 54.3 %all-reduce.4 = (f32[16,14]{0,1:T(8,128)S(1)}, f32[14]{0:T(128)}, f32[4]{0:T(128)S(1)}) all-reduce(f32[16,14]{0,1:T(8,128)S(1)} %select_reduce_fusion, f32[14]{0:T(128)S(1)} %copy-done.107, f32[4]{0:T(128)S(1)} %maximum_add_fusion.2), channel_id=1, replica_groups=mesh['dp'=8,'mp'=4] {'dp'}, use_global_device_ids=true, to_apply=%region_34.35 | all-reduce | flops 242 | bytes 1936 | tf_op jit(solution)/shard_map/psum | solution.py:486
  1199.2 4.3 gather_fusion.2
  1207.8 4.4 gather_fusion.5
  (621 shorter events, 306.5 us)
Async XLA Ops:
  12.3 10.6 copy-start.75
  12.3 158.7 %all-to-all-start = ((bf16[16,128,768]{2,1,0:T(8,128)(2,1)}), bf16[16,128,768]{2,1,0:T(8,128)(2,1)}, u32[]{:S(2)}, u32[]{:S(2)}) async-start(bf16[16,128,768]{2,1,0:T(8,128)(2,1)} %gather_fusion), calls=%async_computation | async-start | bytes 6291456 | tf_op jit(solution)/shard_map/all_to_all | solution.py:426
  19.7 99.7 %copy-start.108 = (bf16[3,16]{1,0:T(4,128)(2,1)S(1)}, bf16[3,16]{1,0:T(4,128)(2,1)}, u32[]{:S(2)}) copy-start(bf16[3,16]{1,0:T(4,128)(2,1)} %param.44) | copy-start | bytes 292
  19.7 118.1 %copy-start.78 = (bf16[192,96]{1,0:T(8,128)(2,1)S(1)}, bf16[192,96]{1,0:T(8,128)(2,1)}, u32[]{:S(2)}) copy-start(bf16[192,96]{1,0:T(8,128)(2,1)} %param.45) | copy-start | bytes 110596
  19.7 340.2 %all-reduce.20.cloned.1.call-start = ((), (), s32[]{:S(2)}) async-start(), calls=%async_computation.19 | async-start | bytes 6291456 | tf_op jit(solution)/shard_map/psum | solution.py:254
  20.4 99.0 %copy-start.99 = (s32[1024]{0:T(1024)}, s32[1024]{0:T(1024)S(1)}, u32[]{:S(2)}) copy-start(s32[1024]{0:T(1024)S(1)} %pad_clamp_fusion.1) | copy-start | bytes 12292
  231.4 138.7 %all-gather.6.cloned.1.call-start = ((), (), s32[]{:S(2)}) async-start(), calls=%async_computation.14 | async-start | bytes 1327104 | tf_op jit(solution)/shard_map/all_gather | solution.py:441
  236.5 97.3 %copy-start.106 = (bf16[12,8]{0,1:T(8,128)(2,1)S(1)}, bf16[12,8]{0,1:T(8,128)(2,1)}, u32[]{:S(2)}) copy-start(bf16[12,8]{0,1:T(8,128)(2,1)} %param.50) | copy-start | bytes 580
  236.5 123.4 %copy-start.6 = (bf16[8,2,128,768]{3,2,0,1:T(8,128)(2,1)S(1)}, bf16[8,2,128,768]{3,2,0,1:T(8,128)(2,1)}, u32[]{:S(2)}) copy-start(bf16[8,2,128,768]{3,2,0,1:T(8,128)(2,1)} %copy-done.5) | copy-start | bytes 9437188
  236.5 275.2 %all-to-all-start.2 = ((bf16[16,128,768]{2,1,0:T(8,128)(2,1)}), bf16[16,128,768]{2,1,0:T(8,128)(2,1)}, u32[]{:S(2)}, u32[]{:S(2)}) async-start(bf16[16,128,768]{2,1,0:T(8,128)(2,1)} %gather_fusion.4), calls=%async_computation.2 | async-start | bytes 6291456 | tf_op jit(solution)/shard_map/all_to_all | solution.py:427
  241.7 150.3 %all-gather.8.cloned.1.call-start = ((), (), s32[]{:S(2)}) async-start(), calls=%async_computation.15 | async-start | bytes 1327104 | tf_op jit(solution)/shard_map/all_gather | solution.py:442
  242.3 273.5 %all-reduce.18.cloned.1.call-start = ((), (), s32[]{:S(2)}) async-start(), calls=%async_computation.18 | async-start | bytes 6291456 | tf_op jit(solution)/shard_map/psum | solution.py:263
  333.7 309.4 %copy-start.79 = (f32[768]{0:T(1024)}, f32[768]{0:T(1024)S(1)}, u32[]{:S(2)}) copy-start(f32[768]{0:T(1024)S(1)} %get-tuple-element.1003) | copy-start | bytes 9220
  333.7 316.7 %copy-start.76 = (f32[768]{0:T(1024)}, f32[768]{0:T(1024)S(1)}, u32[]{:S(2)}) copy-start(f32[768]{0:T(1024)S(1)} %get-tuple-element.1004) | copy-start | bytes 9220
  399.2 17.2 %copy-start.2 = (s32[16]{0:T(128)S(1)}, s32[16]{0:T(128)}, u32[]{:S(2)}) copy-start(s32[16]{0:T(128)} %param.42) | copy-start | bytes 196
  399.2 18.6 %copy-start.104 = (bf16[16,14]{1,0:T(8,128)(2,1)S(1)}, bf16[16,14]{1,0:T(8,128)(2,1)}, u32[]{:S(2)}) copy-start(bf16[16,14]{1,0:T(8,128)(2,1)} %param.60) | copy-start | bytes 1348
  399.2 49.4 %copy-start.105 = (bf16[16,128]{1,0:T(8,128)(2,1)S(1)}, bf16[16,128]{1,0:T(8,128)(2,1)}, u32[]{:S(2)}) copy-start(bf16[16,128]{1,0:T(8,128)(2,1)} %param.58) | copy-start | bytes 12292
  399.2 79.9 %copy-start.85 = (bf16[96,128]{1,0:T(8,128)(2,1)S(1)}, bf16[96,128]{1,0:T(8,128)(2,1)}, u32[]{:S(2)}) copy-start(bf16[96,128]{1,0:T(8,128)(2,1)} %param.55) | copy-start | bytes 73732
  399.2 243.9 %all-reduce.16.cloned.1.call-start = ((), (), s32[]{:S(2)}) async-start(), calls=%async_computation.17 | async-start | bytes 6291456 | tf_op jit(solution)/shard_map/psum | solution.py:341
  530.7 9.2 copy-start.100
  531.4 21.7 %copy-start.102 = (f32[14]{0:T(128)}, f32[14]{0:T(128)S(1)}, u32[]{:S(2)}) copy-start(f32[14]{0:T(128)S(1)} %get-tuple-element.1188) | copy-start | bytes 172
  559.3 8.9 copy-start.28
  575.6 8.7 copy-start.35
  575.6 10.3 copy-start.33
  575.6 10.3 copy-start.56
  576.6 81.2 %all-to-all-start.12 = ((bf16[8,3,16]{2,1,0:T(4,128)(2,1)}), bf16[8,3,16]{2,1,0:T(4,128)(2,1)S(1)}, u32[]{:S(2)}, u32[]{:S(2)}) async-start(bf16[8,3,16]{2,1,0:T(4,128)(2,1)} %copy.293), calls=%async_computation.12 | async-start | bytes 16384 | tf_op jit(solution)/shard_map/all_to_all | solution.py:26
  587.2 55.9 %copy-start.15 = (f32[1,1024,768]{2,1,0:T(8,128)S(1)}, f32[1,1024,768]{2,1,0:T(8,128)}, u32[]{:S(2)}) copy-start(f32[1,1024,768]{2,1,0:T(8,128)} %get-tuple-element.1135) | copy-start | bytes 9437188
  655.5 8.9 copy-start.11
  655.5 8.9 copy-start.24
  655.5 8.9 copy-start.36
  655.5 8.9 copy-start.125
  657.8 59.1 %all-to-all-start.9 = ((bf16[8,12,8]{1,2,0:T(8,128)(2,1)}), bf16[8,12,8]{1,2,0:T(8,128)(2,1)}, u32[]{:S(2)}, u32[]{:S(2)}) async-start(bf16[8,12,8]{1,2,0:T(8,128)(2,1)} %copy.291), calls=%async_computation.9 | async-start | bytes 32768 | tf_op jit(solution)/shard_map/all_to_all | solution.py:26
  716.9 56.5 %copy-start.10 = (bf16[3,64,1024]{2,1,0:T(8,128)(2,1)S(1)}, bf16[3,64,1024]{2,1,0:T(8,128)(2,1)}, u32[]{:S(2)}) copy-start(bf16[3,64,1024]{2,1,0:T(8,128)(2,1)} %copy-done.9) | copy-start | bytes 1179652
  716.9 56.5 %copy-start.21 = (bf16[3,64,1024]{2,1,0:T(8,128)(2,1)S(1)}, bf16[3,64,1024]{2,1,0:T(8,128)(2,1)}, u32[]{:S(2)}) copy-start(bf16[3,64,1024]{2,1,0:T(8,128)(2,1)} %get-tuple-element.1694) | copy-start | bytes 1179652
  716.9 51.9 %all-to-all-start.13 = ((bf16[8,16,142]{2,1,0:T(8,128)(2,1)}), bf16[8,16,142]{2,1,0:T(8,128)(2,1)S(1)}, u32[]{:S(2)}, u32[]{:S(2)}) async-start(bf16[8,16,142]{2,1,0:T(8,128)(2,1)} %bitcast.753), calls=%async_computation.13 | async-start | bytes 131072 | tf_op jit(solution)/shard_map/all_to_all | solution.py:26
  768.9 111.3 %all-to-all-start.11 = ((bf16[8,96,128]{2,1,0:T(8,128)(2,1)}), bf16[8,96,128]{2,1,0:T(8,128)(2,1)S(1)}, u32[]{:S(2)}, u32[]{:S(2)}) async-start(bf16[8,96,128]{2,1,0:T(8,128)(2,1)} %bitcast.221), calls=%async_computation.11 | async-start | bytes 393216 | tf_op jit(solution)/shard_map/all_to_all | solution.py:26
  773.4 95.4 %copy-start.91 = (f32[768]{0:T(1024)S(1)}, f32[768]{0:T(1024)}, u32[]{:S(2)}) copy-start(f32[768]{0:T(1024)} %get-tuple-element.1164) | copy-start | bytes 9220
  773.4 97.9 %copy-start.90 = (f32[768]{0:T(1024)S(1)}, f32[768]{0:T(1024)}, u32[]{:S(2)}) copy-start(f32[768]{0:T(1024)} %get-tuple-element.1107) | copy-start | bytes 9220
  868.9 9.3 copy-start.57
  878.6 21.2 %copy-start.52 = (bf16[3,64,2,512]{3,2,1,0:T(2,128)(2,1)}, bf16[3,64,2,512]{3,2,1,0:T(2,128)(2,1)S(1)}, u32[]{:S(2)}) copy-start(bf16[3,64,2,512]{3,2,1,0:T(2,128)(2,1)S(1)} %copy.280) | copy-start | bytes 1179652
  878.9 20.8 %copy-start.64 = (bf16[3,64,1024]{2,1,0:T(8,128)(2,1)}, bf16[3,64,1024]{2,1,0:T(8,128)(2,1)S(1)}, u32[]{:S(2)}) copy-start(bf16[3,64,1024]{2,1,0:T(8,128)(2,1)S(1)} %convert.58) | copy-start | bytes 1179652
  879.0 20.7 %copy-start.66 = (bf16[3,64,1024]{2,1,0:T(8,128)(2,1)}, bf16[3,64,1024]{2,1,0:T(8,128)(2,1)S(1)}, u32[]{:S(2)}) copy-start(bf16[3,64,1024]{2,1,0:T(8,128)(2,1)S(1)} %convert.59) | copy-start | bytes 1179652
  880.1 19.6 %copy-start.70 = (bf16[8,96,128]{2,1,0:T(8,128)(2,1)}, bf16[8,96,128]{2,1,0:T(8,128)(2,1)S(1)}, u32[]{:S(2)}) copy-start(bf16[8,96,128]{2,1,0:T(8,128)(2,1)S(1)} %all-to-all-done.11) | copy-start | bytes 589828
  880.1 10.7 all-to-all-start.5
  890.8 9.0 copy-start.83
  890.8 9.9 all-to-all-start.7
  894.1 11.6 copy-start.77
  894.1 11.6 copy-start.80
  900.6 30.0 %all-to-all-start.10 = ((bf16[8,768,96]{1,2,0:T(8,128)(2,1)}), bf16[8,768,96]{1,2,0:T(8,128)(2,1)}, u32[]{:S(2)}, u32[]{:S(2)}) async-start(bf16[8,768,96]{1,2,0:T(8,128)(2,1)} %bitcast.217), calls=%async_computation.10 | async-start | bytes 2359296 | tf_op jit(solution)/shard_map/all_to_all | solution.py:26
  912.3 24.7 %copy-start.12 = (f32[1,1024,768]{2,1,0:T(8,128)S(1)}, f32[1,1024,768]{2,1,0:T(8,128)}, u32[]{:S(2)}) copy-start(f32[1,1024,768]{2,1,0:T(8,128)} %get-tuple-element.1165) | copy-start | bytes 9437188
  930.6 31.0 %all-to-all-start.8 = ((bf16[8,96,768]{2,1,0:T(8,128)(2,1)}), bf16[8,96,768]{2,1,0:T(8,128)(2,1)}, u32[]{:S(2)}, u32[]{:S(2)}) async-start(bf16[8,96,768]{2,1,0:T(8,128)(2,1)} %bitcast.748), calls=%async_computation.8 | async-start | bytes 2359296 | tf_op jit(solution)/shard_map/all_to_all | solution.py:26
  961.6 19.4 %all-to-all-start.6 = ((bf16[8,192,96]{2,1,0:T(8,128)(2,1)}), bf16[8,192,96]{2,1,0:T(8,128)(2,1)}, u32[]{:S(2)}, u32[]{:S(2)}) async-start(bf16[8,192,96]{2,1,0:T(8,128)(2,1)} %bitcast.677), calls=%async_computation.6 | async-start | bytes 786432 | tf_op jit(solution)/shard_map/all_to_all | solution.py:26
  981.1 33.5 %all-to-all-start.4 = ((bf16[8,3,96,192]{2,3,1,0:T(8,128)(2,1)}), bf16[8,3,96,192]{2,3,1,0:T(8,128)(2,1)}, u32[]{:S(2)}, u32[]{:S(2)}) async-start(bf16[8,3,96,192]{2,3,1,0:T(8,128)(2,1)} %bitcast.710), calls=%async_computation.4 | async-start | bytes 2359296 | tf_op jit(solution)/shard_map/all_to_all | solution.py:26
  994.1 25.2 %copy-start.62 = (bf16[3,64,1024]{2,1,0:T(8,128)(2,1)S(1)}, bf16[3,64,1024]{2,1,0:T(8,128)(2,1)}, u32[]{:S(2)}) copy-start(bf16[3,64,1024]{2,1,0:T(8,128)(2,1)} %copy-done.61) | copy-start | bytes 1179652
  1014.6 89.4 %all-to-all-start.1 = ((bf16[2,1024,768]{2,0,1:T(2,128)(2,1)}), bf16[2,1024,768]{2,0,1:T(2,128)(2,1)}, u32[]{:S(2)}, u32[]{:S(2)}) async-start(bf16[2,1024,768]{2,0,1:T(2,128)(2,1)} %copy.272), calls=%async_computation.1 | async-start | bytes 6291456 | tf_op jit(solution)/shard_map/all_to_all | solution.py:489
  1019.0 76.5 %all-reduce.14.cloned.1.call-start = ((), (), s32[]{:S(2)}) async-start(), calls=%async_computation.16 | async-start | bytes 6291456 | tf_op jit(solution)/shard_map/psum | solution.py:362
  1104.0 99.5 %all-to-all-start.3 = ((bf16[2,1024,768]{2,0,1:T(2,128)(2,1)}), bf16[2,1024,768]{2,0,1:T(2,128)(2,1)}, u32[]{:S(2)}, u32[]{:S(2)}) async-start(bf16[2,1024,768]{2,0,1:T(2,128)(2,1)} %copy.282), calls=%async_computation.3 | async-start | bytes 6291456 | tf_op jit(solution)/shard_map/all_to_all | solution.py:492
  1109.7 8.7 copy-start.82
  1109.7 10.5 copy-start.74
  1109.7 11.8 copy-start.71
  1109.8 12.4 %copy-start.97 = (f32[1024]{0:T(1024)S(1)}, f32[1024]{0:T(1024)}, u32[]{:S(2)}) copy-start(f32[1024]{0:T(1024)} %get-tuple-element.981) | copy-start | bytes 12292
  1109.8 13.6 %copy-start.96 = (f32[1024]{0:T(1024)S(1)}, f32[1024]{0:T(1024)}, u32[]{:S(2)}) copy-start(f32[1024]{0:T(1024)} %get-tuple-element.1151) | copy-start | bytes 12292
  1109.8 20.1 %copy-start.107 = (f32[14]{0:T(128)S(1)}, f32[14]{0:T(128)}, u32[]{:S(2)}) copy-start(f32[14]{0:T(128)} %get-tuple-element.1109) | copy-start | bytes 172
  1109.8 75.6 %copy-start.84 = (bf16[8,3,16]{2,1,0:T(4,128)(2,1)S(1)}, bf16[8,3,16]{2,1,0:T(4,128)(2,1)}, u32[]{:S(2)}) copy-start(bf16[8,3,16]{2,1,0:T(4,128)(2,1)} %copy-done.83) | copy-start | bytes 2308
  (96 other events, 384.3 us)
Sparse Core Ops, SparseCore 0:
  231.5 69.0 all-reduce.19
  399.4 65.9 all-reduce.17
  575.8 67.3 all-reduce.15
  1026.3 69.1 all-reduce.13
Sparse Core Ops, SparseCore 1:
  234.0 64.0 all-gather.5
  300.1 40.9 all-gather.7
where the time goes:
time: 1230 us; the launch traced here: 1220 us
  blocking collectives  425 us (35%)
  matrix products  230 us (19%)
  waiting for transfers between devices  190 us (15%)
  local copies, waits for them, and re-layouts  128 us (10%)
  starting transfers between devices  108 us (9%)
  other arithmetic  102 us (8%)
  between operations  19.2 us (2%)
  loops' own time  16.6 us (1%)
    all_gather x1, blocking collectives, body(): lax.all_gather(qkv_weight, 'dp', axis=1, tiled=True)  94.2 us
    all_gather x1, blocking collectives, body(): lax.all_gather(wide_vectors, 'dp', axis=1, tiled=True)  91.1 us
    all_to_all x10, starting transfers between devices, sum_at_owner(): lax.all_to_all(blocks, axis, split_axis=0, concat_axis=0, tiled=True)  85.3 us
    psum x1, waiting for transfers between devices, micro_step(): lax.psum(grad_token_part.astype(jnp.bfloat16), 'mp').astype(jnp.float32)  69.3 us
    all_to_all x10, waiting for transfers between devices, sum_at_owner(): lax.all_to_all(blocks, axis, split_axis=0, concat_axis=0, tiled=True)  68.9 us
    psum x1, blocking collectives, body(): lax.psum((sums_total, class_bias_total, logit_table), 'dp')  54.3 us
    psum x1, waiting for transfers between devices, micro_step(): lax.psum(grad_first_part.astype(jnp.bfloat16), 'mp').astype(jnp.float32)  50.9 us
    dot_general x4, matrix products, compute(): jnp.einsum('hqk,heq->hek', grad_raw, query_piece, preferred_element_type=...  40.3 us
  transfers between devices with their start and end apart: 20, of which 8 were waited for; matrix products, arithmetic and copies ran while one was open for 27% of the time, Pallas kernels for 0%

commit v1 on v0

v1 whole, which is shorter than its diff:
```python
import functools

import jax
import jax.numpy as jnp
import numpy as np
from jax import lax
from jax.experimental import pallas as pl
from jax.experimental.pallas import tpu as pltpu
from jax.sharding import PartitionSpec as P

D = 768
HS = 64
CW = 128
PH = 2
CLASSES = 14
EPSILON = 1e-06
NEGATIVE = -1e30
LOG2E = 1.4426950408889634
HIGHEST = lax.Precision.HIGHEST
BF = jnp.bfloat16
F32 = jnp.float32
AXES = ("dp", "mp")
QB = 256


def dot(a, b, ca, cb):
    return lax.dot_general(a, b, (((ca,), (cb,)), ((), ())), preferred_element_type=F32)


def hop(x, dbit, mbit):
    nd, nm = lax.axis_size("dp"), lax.axis_size("mp")
    pairs = [(d * nm + m, (d ^ dbit) * nm + (m ^ mbit)) for d in range(nd) for m in range(nm)]
    return lax.ppermute(x, AXES, pairs)


def bit_groups(nd):
    bits = []
    b = nd // 2
    while b > 1:
        bits.append(b)
        b //= 2
    groups = [bits[i : i + 2] for i in range(0, len(bits), 2)]
    out = []
    for g in groups:
        out.append([0, g[0]] if len(g) == 1 else [0, g[1], g[0], g[0] + g[1]])
    return out


def gather_chips(x):
    nd = lax.axis_size("dp")
    cur = x[None]
    for masks in bit_groups(nd):
        parts = [cur] + [hop(cur, k, 0) for k in masks[1:]]
        cur = jnp.stack(parts, 1).reshape(-1, *x.shape)
    near, far = (hop(cur, 1, 0), hop(cur, 0, 2))
    far2 = hop(cur, 1, 2)
    return (
        jnp.stack([cur, near], 1).reshape(nd, *x.shape),
        jnp.stack([far, far2], 1).reshape(nd, *x.shape),
    )


def scatter_chips(mine, other):
    nd = lax.axis_size("dp")
    tail = mine.shape[1:]
    a = mine.reshape(nd // 2, 2, *tail)
    b = other.reshape(nd // 2, 2, *tail)
    cur = (
        a[:, 0].astype(F32)
        + hop(a[:, 1], 1, 0).astype(F32)
        + hop(b[:, 0], 0, 2).astype(F32)
        + hop(b[:, 1], 1, 2).astype(F32)
    )
    for masks in reversed(bit_groups(nd)):
        low = cur.astype(BF).reshape(-1, len(masks), *tail)
        full = cur.reshape(-1, len(masks), *tail)
        cur = full[:, 0]
        for i, k in enumerate(masks[1:], 1):
            cur = cur + hop(low[:, i], k, 0).astype(F32)
    return cur[0]


def relative(x, me):
    return jnp.take(x, jnp.arange(x.shape[0], dtype=jnp.int32) ^ me, axis=0)


def split3(x):
    a = x.astype(BF)
    r = x - a.astype(F32)
    b = r.astype(BF)
    return a, b, (r - b.astype(F32)).astype(BF)


def swap64(x):
    return jnp.concatenate([x[:, 64:], x[:, :64]], axis=1)


def doubled(kp, head):
    lane = lax.broadcasted_iota(jnp.int32, kp.shape, 1)
    kr = swap64(kp)
    return jnp.where(lane < 64, kp, kr) if head == 0 else jnp.where(lane < 64, kr, kp)


def attn_fwd_kernel(q_ref, k_ref, v_ref, aux_ref, ctx_ref, lse_ref, o_ref):
    n = q_ref.shape[0]
    qt = jnp.transpose(q_ref[...].astype(F32)) * (HS**-0.5 * LOG2E)
    hi = qt.astype(BF)
    lo = (qt - hi.astype(F32)).astype(BF)
    vt = jnp.transpose(v_ref[...].astype(F32)).astype(BF)
    kp = k_ref[...]
    row = lax.broadcasted_iota(jnp.int32, (128, QB), 0)
    auxq = jnp.where(row == 0, 1.0, 0.0).astype(BF)
    for h in range(2):
        lhs = jnp.concatenate([doubled(kp, h), aux_ref[...]], axis=1)
        r = slice(64 * h, 64 * h + 64)
        vaug = jnp.concatenate([vt[r], jnp.ones((16, n), BF)], axis=0)
        for b in range(n // QB):
            s = slice(b * QB, b * QB + QB)
            rhs = jnp.concatenate([hi[r, s], lo[r, s], auxq], axis=0)
            sc = dot(lhs, rhs, 1, 0)
            m = jnp.max(sc, axis=0, keepdims=True)
            p = jnp.exp2(sc - m).astype(BF)
            o = dot(vaug, p, 1, 0)
            total = o[64:65]
            o_ref[r, s] = o[:64] / total
            lse_ref[0, h : h + 1, s] = m + jnp.log2(total)
    ctx_ref[...] = jnp.transpose(o_ref[...]).astype(BF)


def attn_fwd(proj, aux):
    n, w = proj.shape
    pairs = w // 3 // 128
    return pl.pallas_call(
        attn_fwd_kernel,
        grid=(pairs,),
        in_specs=[
            pl.BlockSpec((n, 128), lambda p: (0, p)),
            pl.BlockSpec((n, 128), lambda p: (0, p + pairs)),
            pl.BlockSpec((n, 128), lambda p: (0, p + 2 * pairs)),
            pl.BlockSpec((n, 128), lambda p: (0, 0)),
        ],
        out_specs=[
            pl.BlockSpec((n, 128), lambda p: (0, p)),
            pl.BlockSpec((1, 2, n), lambda p: (p, 0, 0)),
        ],
        out_shape=[
            jax.ShapeDtypeStruct((n, w // 3), BF),
            jax.ShapeDtypeStruct((pairs, 2, n), F32),
        ],
        scratch_shapes=[pltpu.VMEM((128, n), F32)],
        name="attn_fwd",
    )(proj, proj, proj, aux)


def attn_bwd_kernel(q_ref, k_ref, v_ref, aux_ref, ctx_ref, do_ref, lse_ref, dq_ref, dk_ref, dv_ref, dqt_ref):
    n = q_ref.shape[0]
    scale = HS**-0.5
    qp, kp, vp, dop = q_ref[...], k_ref[...], v_ref[...], do_ref[...]
    qt = jnp.transpose(qp.astype(F32)) * (scale * LOG2E)
    hi = qt.astype(BF)
    lo = (qt - hi.astype(F32)).astype(BF)
    kt = jnp.transpose(kp.astype(F32)).astype(BF)
    dot_f = jnp.transpose(dop.astype(F32))
    dot_b = dot_f.astype(BF)
    ctxt = jnp.transpose(ctx_ref[...].astype(F32))
    prod = dot_f * ctxt
    lane = lax.broadcasted_iota(jnp.int32, (n, 128), 1)
    row = lax.broadcasted_iota(jnp.int32, (128, QB), 0)
    lhs_v = jnp.concatenate([vp, aux_ref[...]], axis=1)
    dk = jnp.zeros((n, 128), F32)
    dv = jnp.zeros((n, 128), F32)
    for h in range(2):
        lhs = jnp.concatenate([doubled(kp, h), aux_ref[...]], axis=1)
        r = slice(64 * h, 64 * h + 64)
        mine = (lane < 64) if h == 0 else (lane >= 64)
        qm = jnp.where(mine, qp, jnp.zeros_like(qp))
        dom = jnp.where(mine, dop, jnp.zeros_like(dop))
        dsum = jnp.sum(prod[r], axis=0, keepdims=True)
        l1, l2, l3 = split3(-lse_ref[0, h : h + 1, :])
        d1, d2, d3 = split3(-dsum)
        for b in range(n // QB):
            s = slice(b * QB, b * QB + QB)

            def pieces(first, x1, x2, x3):
                z = jnp.where(row == 1, x1[:, s].astype(F32), jnp.where(row == 0, first, 0.0))
                z = jnp.where(row == 2, x2[:, s].astype(F32), z)
                return jnp.where(row == 3, x3[:, s].astype(F32), z).astype(BF)

            rhs = jnp.concatenate([hi[r, s], lo[r, s], pieces(1.0, l1, l2, l3)], axis=0)
            p = jnp.exp2(dot(lhs, rhs, 1, 0))
            zero = jnp.zeros((64, QB), BF)
            g = dot_b[r, s]
            half = [g, zero] if h == 0 else [zero, g]
            rhs_v = jnp.concatenate(half + [pieces(0.0, d1, d2, d3)], axis=0)
            ds = (p * dot(lhs_v, rhs_v, 1, 0)).astype(BF)
            dv = dv + dot(p.astype(BF), dom[s], 1, 0)
            dk = dk + dot(ds, qm[s], 1, 0)
            dqt_ref[r, s] = dot(kt[r], ds, 1, 0)
    dq_ref[...] = jnp.transpose(dqt_ref[...] * scale).astype(BF)
    dk_ref[...] = (dk * scale).astype(BF)
    dv_ref[...] = dv.astype(BF)


def attn_bwd(proj, aux, ctx, dctx, lse):
    n, w = proj.shape
    pairs = w // 3 // 128
    one = pl.BlockSpec((n, 128), lambda p: (0, p))
    return pl.pallas_call(
        attn_bwd_kernel,
        grid=(pairs,),
        in_specs=[
            one,
            pl.BlockSpec((n, 128), lambda p: (0, p + pairs)),
            pl.BlockSpec((n, 128), lambda p: (0, p + 2 * pairs)),
            pl.BlockSpec((n, 128), lambda p: (0, 0)),
            one,
            one,
            pl.BlockSpec((1, 2, n), lambda p: (p, 0, 0)),
        ],
        out_specs=[one, one, one],
        out_shape=[jax.ShapeDtypeStruct((n, w // 3), BF)] * 3,
        scratch_shapes=[pltpu.VMEM((128, n), F32)],
        name="attn_bwd",
    )(proj, proj, proj, aux, ctx, dctx, lse)


def norm_forward(values, gain, shift):
    center = values - jnp.mean(values, -1, keepdims=True)
    spread = jnp.mean(center * center, -1, keepdims=True)
    row_scale = lax.rsqrt(spread + EPSILON)
    normed = center * row_scale
    return (normed * gain + shift, normed, row_scale)


def norm_backward(upstream, normed, row_scale, gain):
    scaled = upstream * gain
    inner = (
        scaled
        - jnp.mean(scaled, -1, keepdims=True)
        - normed * jnp.mean(scaled * normed, -1, keepdims=True)
    )
    return (inner * row_scale, jnp.sum(upstream * normed, axis=0), jnp.sum(upstream, axis=0))


def pad_rows(flat, rows):
    size = -flat.shape[-1] % (rows * 128)
    flat = jnp.pad(flat, [(0, 0)] * (flat.ndim - 1) + [(0, size)])
    return flat.reshape(*flat.shape[:-1], -1, 128)


def take_parts(flat, shapes):
    out, at = [], 0
    for shape in shapes:
        size = int(np.prod(shape))
        out.append(flat[:, at : at + size].reshape(flat.shape[0], *shape))
        at += size
    return out


def body(
    hidden_in,
    cotangent,
    lengths,
    labels,
    qkv_weight,
    qv_bias,
    out_weight,
    out_bias,
    norm1_gain,
    norm1_bias,
    up_weight,
    up_bias,
    down_weight,
    down_bias,
    norm2_gain,
    norm2_bias,
    student_weight,
    student_bias,
    pool_query,
    pooler_weight,
    pooler_bias,
    class_weight,
    class_bias,
):
    nd = lax.axis_size("dp")
    me = lax.axis_index("dp")
    m = lax.axis_index("mp")
    c, y = m % 2, m // 2
    total, pd, _ = hidden_in.shape
    assert total == 2 * nd and lax.axis_size("mp") == 4
    hp = pd // 2
    half = nd * hp
    rows = D // nd
    hw = qkv_weight.shape[2]
    fw = up_weight.shape[1]
    seq = 2 * me + y
    length = lengths[seq]
    label = labels[seq]

    def deal(x):
        x = x.reshape(nd, 2, 2, hp, D)
        x = lax.dynamic_slice(x, (0, y, c, 0, 0), (nd, 1, 1, hp, D)).reshape(nd, hp, D)
        return lax.all_to_all(x, "dp", 0, 0, tiled=True).reshape(half, D)

    tokens = deal(hidden_in)

    q_near, q_far = gather_chips(jnp.transpose(qkv_weight, (1, 0, 2)).reshape(rows, 3 * hw))
    local_small = jnp.concatenate(
        [
            student_weight.reshape(-1),
            pooler_weight.reshape(-1),
            class_weight.reshape(-1),
            out_bias,
            norm1_gain,
            norm1_bias,
            down_bias,
            norm2_gain,
            norm2_bias,
            student_bias,
            pool_query,
            pooler_bias,
            qv_bias.reshape(-1),
            up_bias.reshape(-1),
        ]
    )
    small = pad_rows(local_small, 8)
    small = lax.all_to_all(jnp.broadcast_to(small[None], (nd, *small.shape)), "dp", 0, 0, tiled=True)
    small = small.reshape(nd, -1)
    nh = qv_bias.shape[0]
    nr = up_bias.shape[0]
    cr = CW // nd
    parts = take_parts(
        small,
        [(rows, CW), (cr, CW), (cr, CLASSES), (6, rows), (3, cr), (nh, 2 * HS // nd), (nr, HS // nd)],
    )
    student_full = parts[0].reshape(D, CW)
    pooler_full = parts[1].reshape(CW, CW).astype(F32)
    class_full = parts[2].reshape(CW, CLASSES).astype(F32)
    wide = jnp.transpose(parts[3], (1, 0, 2)).reshape(6, D).astype(F32)
    narrow = jnp.transpose(parts[4], (1, 0, 2)).reshape(3, CW).astype(F32)
    qv_mine = jnp.transpose(parts[5], (1, 0, 2)).reshape(nh, 2 * HS)
    ub_mine = jnp.transpose(parts[6], (1, 0, 2)).reshape(nr * HS)
    bias_mine = jnp.concatenate([qv_mine.reshape(-1), ub_mine])
    bias_far = hop(bias_mine, 0, 2)
    bias_two = jnp.stack([bias_mine, bias_far])
    bias_sib = hop(bias_two, 0, 1)
    qv_two = bias_two[:, : nh * 2 * HS].reshape(2, nh, 2 * HS).astype(F32)
    up_bias_full = jnp.concatenate([bias_two, bias_sib])[:, nh * 2 * HS :].reshape(-1).astype(F32)
    out_bias_f, gain_one, shift_one, down_bias_f, gain_two, shift_two = [wide[i : i + 1] for i in range(6)]

    f_pack = jnp.concatenate([out_weight.T, up_weight, down_weight.T], axis=1)
    f_near, f_far = gather_chips(f_pack)
    f_two = jnp.stack([relative(f_near, me), relative(f_far, me)])
    f_sib = hop(f_two, 0, 1)
    f_all = jnp.concatenate([f_two, f_sib]).reshape(4, D, hw + 2 * fw)
    out_t = jnp.concatenate([f_all[i, :, :hw] for i in range(4)], axis=1)
    up_full = jnp.concatenate([f_all[i, :, hw : hw + fw] for i in range(4)], axis=1)
    down_t = jnp.concatenate([f_all[i, :, hw + fw :] for i in range(4)], axis=1)
    cot = deal(cotangent)

    q_all = jnp.stack([relative(q_near, me), relative(q_far, me)]).reshape(2, D, 3, hw)
    w_qkv = jnp.transpose(q_all, (1, 2, 0, 3)).reshape(D, 6 * hw)
    zero = jnp.zeros((2, nh * HS), F32)
    proj_bias = jnp.stack([qv_two[:, :, :HS].reshape(2, -1), zero, qv_two[:, :, HS:].reshape(2, -1)]).reshape(1, 6 * hw)

    both = jnp.concatenate([tokens, hop(tokens, 0, 1)], axis=0)
    proj = (dot(both, w_qkv, 1, 0) + proj_bias).astype(BF)
    index = jnp.arange(half, dtype=jnp.int32)
    position = (index // hp) * pd + index % hp
    position = jnp.concatenate([position + c * hp, position + (1 - c) * hp])
    live = position < length
    col = jnp.arange(128, dtype=jnp.int32)[None, :]
    aux = jnp.where(
        col == 0, jnp.where(live, 0.0, NEGATIVE)[:, None], jnp.where(col <= 3, 1.0, 0.0)
    ).astype(BF)
    ctx, lse = attn_fwd(proj, aux)
    ctx_all = jnp.concatenate([ctx[:half], hop(ctx[half:], 0, 1)], axis=1)

    live_own = live[:half]
    live_float = live_own.astype(F32)[:, None]
    token_float = tokens.astype(F32)
    attention = dot(ctx_all, out_t, 1, 1) + out_bias_f
    first, normed_one, scale_one = norm_forward(token_float + attention, gain_one, shift_one)
    first_low = first.astype(BF)
    before = dot(first_low, up_full, 1, 0) + up_bias_full
    phi_c = 0.5 * (1.0 + lax.erf(before * (0.5**0.5)))
    slope = (phi_c + before * (jnp.exp(-0.5 * before * before) * (2 * np.pi) ** -0.5)).astype(BF)
    active = (before * phi_c).astype(BF)
    feed = dot(active, down_t, 1, 1) + down_bias_f
    second, normed_two, scale_two = norm_forward(first + feed, gain_two, shift_two)
    second_low = second.astype(BF)

    def undeal(x):
        a = lax.all_to_all(x.reshape(nd, hp, D), "dp", 0, 0, tiled=True)
        b = hop(a, 0, 2)
        pair = jnp.where(y == 0, jnp.stack([a, b], 1), jnp.stack([b, a], 1))
        sib = hop(pair, 0, 1)
        quad = jnp.where(c == 0, jnp.stack([pair, sib], 2), jnp.stack([sib, pair], 2))
        return quad.reshape(total, pd, D)

    hidden_out = undeal(second_low)

    student_bias_f, query_f, pooler_bias_f = narrow[0:1], narrow[1:2], narrow[2:3]
    student = dot(second_low, student_full, 1, 0) + student_bias_f
    pw = CW // PH
    heads = student.reshape(half, PH, pw)
    scale = pw**-0.5
    pool_logit = jnp.sum(heads * query_f.reshape(1, PH, pw), -1) * scale
    pool_logit = jnp.where(live_own[:, None], pool_logit, NEGATIVE)
    top = jnp.max(pool_logit, 0)
    weight = jnp.where(live_own[:, None], jnp.exp(pool_logit - top), 0.0)
    amount = jnp.sum(weight, 0)
    mass = jnp.sum(weight[:, :, None] * heads, 0).reshape(CW)
    sums = jnp.stack(
        [jnp.sum(live_float * v * v) for v in (token_float, attention, first, feed)]
    )
    mine = jnp.concatenate([top, amount, sums, mass])
    mine = jnp.pad(mine, (0, 256 - mine.shape[0])).reshape(2, 128)
    sib = hop(mine, 0, 1).reshape(-1)
    top2, amount2, sums2, mass2 = sib[0:2], sib[2:4], sib[4:8], sib[8 : 8 + CW]
    best = jnp.maximum(top, top2)
    fa, fb = jnp.exp(top - best), jnp.exp(top2 - best)
    whole = amount * fa + amount2 * fb
    pooled = (mass * jnp.repeat(fa, pw) + mass2 * jnp.repeat(fb, pw)) / jnp.repeat(whole, pw)
    pool_weight = weight * (fa / whole)
    pooled = pooled[None, :]
    z = jnp.tanh(jnp.dot(pooled, pooler_full, precision=HIGHEST) + pooler_bias_f)
    logit = jnp.dot(z, class_full, precision=HIGHEST) + class_bias.astype(F32)[None, :]
    onehot = (jnp.arange(CLASSES) == label).astype(F32)[None, :]
    dlogit = jax.nn.softmax(logit, axis=-1) - onehot
    once = jnp.where(c == 0, 1.0, 0.0)
    grad_class = jnp.dot(z.T, dlogit, precision=HIGHEST) * once
    dz = jnp.dot(dlogit, class_full.T, precision=HIGHEST)
    dzp = dz * (1.0 - z * z)
    grad_pooler = jnp.dot(pooled.T, dzp, precision=HIGHEST) * once
    grad_pooler_bias = dzp[0] * once
    dpooled = jnp.dot(dzp, pooler_full.T, precision=HIGHEST)
    dpooled_h = dpooled.reshape(1, PH, pw)
    dw = jnp.sum(heads * dpooled_h, -1)
    dq_pool = scale * pool_weight * (dw - jnp.sum((pooled * dpooled).reshape(PH, pw), -1)[None, :])
    grad_query = jnp.sum(dq_pool[:, :, None] * heads, 0).reshape(CW)
    dstudent = pool_weight[:, :, None] * dpooled_h + dq_pool[:, :, None] * query_f.reshape(1, PH, pw)
    dstudent = dstudent.reshape(half, CW).astype(BF)
    grad_student_bias = jnp.sum(dstudent.astype(F32), 0)
    grad_student = dot(second_low, dstudent, 0, 0)

    dsecond = dot(dstudent, student_full, 1, 1) + cot.astype(F32)
    dr2, grad_gain_two, grad_shift_two = norm_backward(dsecond, normed_two, scale_two, gain_two)
    grad_down_bias = jnp.sum(dr2, 0)
    dffn = dr2.astype(BF)
    grad_down_t = dot(dffn, active, 0, 0).astype(BF)
    dact = dot(dffn, down_t, 1, 0)
    dpre = (dact * slope.astype(F32)).astype(BF)
    grad_up_bias = jnp.sum(dpre.astype(F32), 0)
    grad_up = dot(first_low, dpre, 0, 0).astype(BF)
    dfirst = dot(dpre, up_full, 1, 1) + dr2
    dr1, grad_gain_one, grad_shift_one = norm_backward(dfirst, normed_one, scale_one, gain_one)
    grad_out_bias = jnp.sum(dr1, 0)
    dattn = dr1.astype(BF)
    grad_out_t = dot(dattn, ctx_all, 0, 0).astype(BF)
    dctx = dot(dattn, out_t, 1, 0).astype(BF)
    w2 = 2 * hw
    dctx_own = jnp.concatenate([dctx[:, :w2], hop(dctx[:, w2:], 0, 1)], axis=0)

    def quarter(i):
        return jnp.concatenate(
            [
                grad_out_t[:, i * hw : (i + 1) * hw],
                grad_up[:, i * fw : (i + 1) * fw],
                grad_down_t[:, i * fw : (i + 1) * fw],
            ],
            axis=1,
        )

    keep = [quarter(0), quarter(1)]
    got = hop(jnp.stack([quarter(2), quarter(3)]), 0, 1)
    f_grads = [
        relative((k.astype(F32) + got[i].astype(F32)).astype(BF).reshape(nd, rows, -1), me)
        for i, k in enumerate(keep)
    ]
    f_sum = scatter_chips(*f_grads)

    dq, dk, dv = attn_bwd(proj, aux, ctx, dctx_own, lse)
    dproj = jnp.concatenate([dq, dk, dv], axis=1)
    grad_qv = jnp.stack([jnp.sum(dq.astype(F32), 0), jnp.sum(dv.astype(F32), 0)])
    part = dot(dproj, w_qkv, 1, 1)
    dtokens = part[:half] + dr1 + hop(part[half:].astype(BF), 0, 1).astype(F32)
    input_grad = undeal(dtokens.astype(BF))
    grad_qkv = dot(both, dproj, 0, 0).astype(BF).reshape(nd, rows, 3, 2, hw)
    grad_qkv = relative(grad_qkv, me)
    q_sum = scatter_chips(
        grad_qkv[:, :, :, 0].reshape(nd, rows, 3 * hw), grad_qkv[:, :, :, 1].reshape(nd, rows, 3 * hw)
    )

    eye = (jnp.arange(4)[:, None] == jnp.stack([m, m ^ 2])[None, :]).astype(F32)
    qv_pair = jnp.transpose(grad_qv.reshape(2, 2, nh, HS), (1, 2, 0, 3)).reshape(2, nh * 2 * HS)
    grad_qv_full = jnp.dot(eye, qv_pair, precision=HIGHEST).reshape(4 * nh, nd, 2 * HS // nd)
    eye4 = (jnp.arange(4)[:, None] == jnp.stack([m, m ^ 2, m ^ 1, m ^ 3])[None, :]).astype(F32)
    grad_ub_full = jnp.dot(eye4, grad_up_bias.reshape(4, fw), precision=HIGHEST).reshape(4 * nr, nd, HS // nd)
    wide_g = jnp.stack([grad_out_bias, grad_gain_one, grad_shift_one, grad_down_bias, grad_gain_two, grad_shift_two])
    narrow_g = jnp.stack([grad_student_bias, grad_query, grad_pooler_bias])
    small_g = jnp.concatenate(
        [
            grad_student.reshape(nd, -1),
            grad_pooler.reshape(nd, -1),
            grad_class.reshape(nd, -1),
            jnp.transpose(wide_g.reshape(6, nd, rows), (1, 0, 2)).reshape(nd, -1),
            jnp.transpose(narrow_g.reshape(3, nd, cr), (1, 0, 2)).reshape(nd, -1),
            jnp.transpose(grad_qv_full, (1, 0, 2)).reshape(nd, -1),
            jnp.transpose(grad_ub_full, (1, 0, 2)).reshape(nd, -1),
        ],
        axis=1,
    )
    small_g = pad_rows(small_g, 8)
    small_g = small_g + hop(small_g.astype(BF), 0, 1).astype(F32)
    small_g = small_g + hop(small_g.astype(BF), 0, 2).astype(F32)
    small_g = lax.all_to_all(small_g.astype(BF), "dp", 0, 0, tiled=True).astype(F32).sum(0)
    g_student, g_pooler, g_class, g_wide, g_narrow, g_qv, g_ub = [
        a[0]
        for a in take_parts(
            small_g.reshape(1, -1),
            [
                (rows, CW),
                (cr, CW),
                (cr, CLASSES),
                (6, rows),
                (3, cr),
                (4, nh, 2 * HS // nd),
                (4, nr, HS // nd),
            ],
        )
    ]
    report = jnp.concatenate([logit[0], dlogit[0], sums + sums2])
    report = jnp.pad(report, (0, 128 - report.shape[0])).reshape(1, 128)
    far = hop(report, 0, 2)
    two = jnp.where(y == 0, jnp.concatenate([report, far]), jnp.concatenate([far, report]))
    two = jnp.pad(two, ((0, 6), (0, 0)))
    table = lax.all_to_all(jnp.broadcast_to(two[None], (nd, 8, 128)), "dp", 0, 0, tiled=True)
    table = table[:, :2].reshape(total, 128)
    logit_all = table[:, :CLASSES]
    class_bias_grad = jnp.sum(table[:, CLASSES : 2 * CLASSES], 0)
    squares = jnp.sum(table[:, 2 * CLASSES : 2 * CLASSES + 4], 0)
    rms = jnp.sqrt(squares / (jnp.sum(lengths).astype(F32) * D))
    return (
        hidden_out,
        logit_all,
        input_grad,
        jnp.transpose(q_sum.reshape(rows, 3, hw), (1, 0, 2)),
        g_qv[m],
        f_sum[:, :hw].T,
        g_wide[0],
        g_wide[1],
        g_wide[2],
        f_sum[:, hw : hw + fw],
        g_ub[m],
        f_sum[:, hw + fw :].T,
        g_wide[3],
        g_wide[4],
        g_wide[5],
        g_student,
        g_narrow[0],
        g_narrow[1],
        g_pooler,
        g_narrow[2],
        g_class,
        class_bias_grad,
        rms,
    )


def solution(mesh):
    rows = P(None, "dp", None)
    vec = P("dp")
    return jax.shard_map(
        body,
        mesh=mesh,
        in_specs=(
            rows,
            rows,
            P(),
            P(),
            P(None, "dp", "mp"),
            P("mp", "dp"),
            P("mp", "dp"),
            vec,
            vec,
            vec,
            P("dp", "mp"),
            P("mp", "dp"),
            P("mp", "dp"),
            vec,
            vec,
            vec,
            P("dp", None),
            vec,
            vec,
            P("dp", None),
            vec,
            P("dp", None),
            P(),
        ),
        out_specs=(
            rows,
            P(),
            rows,
            P(None, "dp", "mp"),
            P("mp", "dp"),
            P("mp", "dp"),
            vec,
            vec,
            vec,
            P("dp", "mp"),
            P("mp", "dp"),
            P("mp", "dp"),
            vec,
            vec,
            vec,
            P("dp", None),
            vec,
            vec,
            P("dp", None),
            vec,
            P("dp", None),
            P(),
            P(),
        ),
        check_vma=False,
    )
```

time: 1230 us -> 677 us (0.55)
  blocking collectives: 425 us -> 0 us
  matrix products: 230 us -> 60.2 us
  local copies, waits for them, and re-layouts: 128 us -> 201 us
  Pallas kernels: 0 us -> 38.6 us
  starting transfers between devices: 108 us -> 75.7 us
  loops' own time: 16.6 us -> 0 us
  between operations: 19.2 us -> 3.29 us
    all_gather x9 -> x0, blocking collectives: 371 us -> none  [the longest x1 94.2 us: body(): lax.all_gather(qkv_weight, 'dp', axis=1, tiled=True)]
    ppermute x0 -> x40, waiting for transfers between devices: none -> 191 us  [hop(): return lax.ppermute(x, AXES, pairs)]
    dot_general x72 -> x21, matrix products: 228 us -> 60.2 us  [the longest x15 56.9 us: dot(): lax.dot_general(a, b, (((ca,), (cb,)), ((), ())), preferred_element_type=...]
    psum x4 -> x0, waiting for transfers between devices: 120 us -> none  [the longest x1 69.3 us: micro_step(): lax.psum(grad_token_part.astype(jnp.bfloat16), 'mp').astype(jnp.float32)]
    all_to_all x14 -> x7, starting transfers between devices: 108 us -> 35.4 us  [the longest x2 11.3 us: undeal(): a = lax.all_to_all(x.reshape(nd, hp, D), 'dp', 0, 0, tiled=True)]
    all_to_all x14 -> x7, waiting for transfers between devices: 68.9 us -> 0.02 us  [the longest x2 0.01 us: undeal(): a = lax.all_to_all(x.reshape(nd, hp, D), 'dp', 0, 0, tiled=True)]
    psum x1 -> x0, blocking collectives: 54.3 us -> none  [body(): lax.psum((sums_total, class_bias_total, logit_table), 'dp')]
    ppermute x0 -> x40, starting transfers between devices: none -> 40.3 us  [hop(): return lax.ppermute(x, AXES, pairs)]
  transfers between devices with their start and end apart: 20 -> 47, of which waited for: 8 -> 14; matrix products, arithmetic and copies ran while one was open for 27% -> 47% of each run, Pallas kernels for 0% -> 6%
where the time goes in v1:
time: 677 us; the launch traced here: 665 us
  local copies, waits for them, and re-layouts  201 us (30%)
  waiting for transfers between devices  191 us (28%)
  other arithmetic  95 us (14%)
  starting transfers between devices  75.7 us (11%)
  matrix products  60.2 us (9%)
  Pallas kernels  38.6 us (6%)
    ppermute x40, waiting for transfers between devices, hop(): return lax.ppermute(x, AXES, pairs)  191 us
    dot_general x15, matrix products, dot(): lax.dot_general(a, b, (((ca,), (cb,)), ((), ())), preferred_element_type=...  56.9 us
    ppermute x40, starting transfers between devices, hop(): return lax.ppermute(x, AXES, pairs)  40.3 us
    concatenate x6, local copies, waits for them, and re-layouts, quarter(): jnp.concatenate([grad_out_t[:, i * hw:(i + 1) * hw], grad_up[:, i * fw:(i...  24.3 us
    gather x7, local copies, waits for them, and re-layouts, relative(): return jnp.take(x, jnp.arange(x.shape[0], dtype=jnp.int32) ^ me, axis=0)  21.7 us
    unnamed x246, local copies, waits for them, and re-layouts  20.8 us
    pallas_call x1, Pallas kernels, attn_fwd(): pl.pallas_call(attn_fwd_kernel, grid=(pairs,), in_specs=[pl.BlockSpec((n,...  20 us
    pallas_call x1, Pallas kernels, attn_bwd(): pl.pallas_call(attn_bwd_kernel, grid=(pairs,), in_specs=[one, pl.BlockSpe...  18.6 us
  transfers between devices with their start and end apart: 47, of which 14 were waited for; matrix products, arithmetic and copies ran while one was open for 47% of the time, Pallas kernels for 6%

profile of v1, /device:TPU:0, one launch (start us, length us, event | category | flops | bytes accessed | tf_op | source)
XLA Modules:
  0.0 664.6 jit_solution(15496633836532176865)
XLA Ops:
  3.0 5.1 collective-permute-start.11
  10.4 3.7 collective-permute-start.3
  16.6 7.5 %concatenate.128 = bf16[15328]{0:T(1024)(128)(2,1)S(1)} concatenate(bf16[12288]{0:T(1024)(128)(2,1)} %bitcast.420, bf16[2048]{0:T(1024)(128)(2,1)} %bitcast.424, bf16[224]{0:T(256)(128)(2,1)S(1)} %reshape.886, bf16[96]{0:T(256)(128)(2,1)} %param.34, bf16[96]{0:T(256)(128)(2,1)} %param.35, bf16[96]{0:T(256)(128)(2,1)} %param.36, bf16[96]{0:T(256)(128)(2,1)} %param.40, ...), dimensions={0} | concatenate | bytes 61312 | tf_op jit(solution)/shard_map/concatenate | solution.py:308
  24.1 20.7 %collective-permute-done.10 = bf16[1,96,1728]{2,1,0:T(8,128)(2,1)} collective-permute-done((bf16[1,96,1728]{2,1,0:T(8,128)(2,1)S(1)}, bf16[1,96,1728]{2,1,0:T(8,128)(2,1)}, u32[]{:S(2)}, u32[]{:S(2)}) %collective-permute-start.10) | collective-permute-done | bytes 331808 | tf_op jit(solution)/shard_map/ppermute | solution.py:33
  44.8 3.0 fusion.43
  51.4 3.9 all-to-all-start.1
  62.1 22.0 %collective-permute-done.14 = bf16[4,96,1728]{2,1,0:T(8,128)(2,1)} collective-permute-done((bf16[4,96,1728]{2,1,0:T(8,128)(2,1)}, bf16[4,96,1728]{2,1,0:T(8,128)(2,1)}, u32[]{:S(2)}, u32[]{:S(2)}) %collective-permute-start.14) | collective-permute-done | bytes 1327136 | tf_op jit(solution)/shard_map/ppermute | solution.py:33
  84.1 24.6 %collective-permute-done.13 = bf16[4,96,1728]{2,1,0:T(8,128)(2,1)} collective-permute-done((bf16[4,96,1728]{2,1,0:T(8,128)(2,1)}, bf16[4,96,1728]{2,1,0:T(8,128)(2,1)}, u32[]{:S(2)}, u32[]{:S(2)}) %collective-permute-start.13) | collective-permute-done | bytes 1327136 | tf_op jit(solution)/shard_map/ppermute | solution.py:33
  112.5 4.0 gather_fusion.4
  116.5 3.5 pad_maximum_fusion.4
  120.0 4.0 gather_fusion.3
  124.0 3.2 broadcast_select_fusion.3
  127.2 3.2 pad_maximum_fusion
  144.1 4.5 all-to-all-start
  157.2 8.7 %collective-permute-done.7 = bf16[1152]{0:T(1024)(128)(2,1)S(1)} collective-permute-done((bf16[1152]{0:T(1024)(128)(2,1)S(1)}, bf16[1152]{0:T(1024)(128)(2,1)S(1)}, u32[]{:S(2)}, u32[]{:S(2)}) %collective-permute-start.7) | collective-permute-done | bytes 2336 | tf_op jit(solution)/shard_map/ppermute | solution.py:33
  168.9 3.8 collective-permute-done.4
  185.9 4.6 all-to-all-start.4
  193.9 6.9 %slice_bitcast_fusion.6 = (bf16[768,768]{1,0:T(8,128)(2,1)}, bf16[768,768]{1,0:T(8,128)(2,1)}, bf16[768,768]{1,0:T(8,128)(2,1)}, bf16[768,768]{1,0:T(8,128)(2,1)}) fusion(bf16[1,768,1728]{2,1,0:T(8,128)(2,1)} %bitcast.348, bf16[1,768,1728]{2,1,0:T(8,128)(2,1)S(1)} %bitcast.345), kind=kLoop, calls=%fused_computation.93 | loop fusion | bytes 9437184 | tf_op jit(solution)/shard_map/squeeze | solution.py:358
  201.7 4.8 add_convert_fusion.q_ref.k_ref.v_ref
  206.5 20.0 %attn_fwd.1 = (bf16[1024,384]{1,0:T(8,128)(2,1)}, f32[3,2,1024]{2,1,0:T(2,128)}) custom-call(bf16[1024,1152]{1,0:T(8,128)(2,1)} %add_convert_fusion.q_ref.k_ref.v_ref, bf16[1024,1152]{1,0:T(8,128)(2,1)} %add_convert_fusion.q_ref.k_ref.v_ref, bf16[1024,1152]{1,0:T(8,128)(2,1)} %add_convert_fusion.q_ref.k_ref.v_ref, bf16[1024,128]{1,0:T(8,128)(2,1)} %select_convert_fusion.aux_ref), custom_call_target="tpu_custom_call" | custom-call | tf_op jit(solution)/shard_map/attn_fwd/pallas_call | solution.py:133
  229.5 5.4 slice_bitcast_fusion.5
  235.0 2.8 fusion.28
  242.1 6.7 %multiply_convert_fusion.1 = (bf16[512,3072]{1,0:T(8,128)(2,1)S(1)}, f32[512,3072]{1,0:T(8,128)}) fusion(f32[3072]{0:T(1024)S(1)} %copy-done.66, bf16[768,768]{1,0:T(8,128)(2,1)S(1)} %get-tuple-element.191, bf16[768,768]{1,0:T(8,128)(2,1)S(1)} %get-tuple-element.192, bf16[768,768]{1,0:T(8,128)(2,1)S(1)} %copy-done.16, bf16[768,768]{1,0:T(8,128)(2,1)S(1)} %copy-done.18, ...), kind=kOutput, calls=%fused_computation.15 | convolution fusion | flops 2445410304 | bytes 15747072 | tf_op jit(solution)/shard_map/dot_general | solution.py:27
  248.9 3.6 fusion.11
  271.9 3.2 maximum_add_fusion
  276.6 2.8 multiply_reduce_fusion
  281.4 4.4 convolution_convert_fusion
  285.8 8.7 %convert_reduce_fusion = (f32[3072]{0:T(1024)S(1)}, bf16[512,3072]{1,0:T(8,128)(2,1)S(1)}) fusion(f32[512,3072]{1,0:T(8,128)} %get-tuple-element.270, f32[3072]{0:T(1024)S(1)} %copy-done.67, bf16[768,768]{1,0:T(8,128)(2,1)S(1)} %copy-done.31, bf16[768,768]{1,0:T(8,128)(2,1)S(1)} %copy-done.29, bf16[768,768]{1,0:T(8,128)(2,1)S(1)} %copy-done.21, ...), kind=kOutput, calls=%fused_computation.13 | convolution fusion | flops 2458776576 | bytes 15753216 | tf_op jit(solution)/shard_map/dot_general | solution.py:27
  294.6 4.8 multiply_reduce_fusion.1
  299.4 4.6 convolution_convert_fusion.1
  308.1 4.8 fusion.99
  324.1 6.1 concatenate.153
  330.1 5.6 concatenate.152
  335.8 5.6 pad_maximum_fusion.1
  343.1 6.0 all-to-all-start.3
  353.3 8.2 %copy.215 = bf16[2,768,1728]{1,2,0:T(8,128)(2,1)} copy(bf16[2,768,1728]{2,1,0:T(8,128)(2,1)} %pad_maximum_fusion.1) | data formatting | bytes 10616832 | tf_op jit(solution)/shard_map/stack | solution.py:476
  362.0 6.1 concatenate.151
  368.1 5.6 concatenate.157
  373.7 6.6 all-to-all-start.2
  384.7 18.6 %attn_bwd.1 = (bf16[1024,384]{1,0:T(8,128)(2,1)}, bf16[1024,384]{1,0:T(8,128)(2,1)}, bf16[1024,384]{1,0:T(8,128)(2,1)}) custom-call(bf16[1024,1152]{1,0:T(8,128)(2,1)} %add_convert_fusion.q_ref.k_ref.v_ref, bf16[1024,1152]{1,0:T(8,128)(2,1)} %add_convert_fusion.q_ref.k_ref.v_ref, bf16[1024,1152]{1,0:T(8,128)(2,1)} %add_convert_fusion.q_ref.k_ref.v_ref, ...), custom_call_target="tpu_custom_call" | custom-call | tf_op jit(solution)/shard_map/attn_bwd/pallas_call | solution.py:208
  410.1 4.6 convolution_convert_fusion.2
  414.8 6.6 reshape.911
  421.4 3.5 copy.199
  424.9 3.9 gather_fusion
  448.3 4.4 fusion.108
  457.3 5.3 collective-permute-done.27
  464.7 7.8 %collective-permute-done.26 = bf16[4,96,576]{2,1,0:T(8,128)(2,1)} collective-permute-done((bf16[4,96,576]{2,1,0:T(8,128)(2,1)}, bf16[4,96,576]{2,1,0:T(8,128)(2,1)}, u32[]{:S(2)}, u32[]{:S(2)}) %collective-permute-start.26) | collective-permute-done | bytes 442400 | tf_op jit(solution)/shard_map/ppermute | solution.py:33
  474.6 2.8 convert_bitcast_fusion.1
  482.6 5.1 all-to-all-start.6
  488.2 9.0 %collective-permute-done.29 = bf16[1,96,576]{1,2,0:T(8,128)(2,1)S(1)} collective-permute-done((bf16[1,96,576]{1,2,0:T(8,128)(2,1)S(1)}, bf16[1,96,576]{1,2,0:T(8,128)(2,1)S(1)}, u32[]{:S(2)}, u32[]{:S(2)}) %collective-permute-start.29) | collective-permute-done | bytes 110624 | tf_op jit(solution)/shard_map/ppermute | solution.py:33
  499.1 2.8 fusion.14
  502.6 4.7 all-to-all-start.5
  507.5 5.3 fusion.98
  512.7 4.6 copy.227
  517.4 4.0 fusion.6
  521.3 4.2 gather_fusion.5
  525.5 4.6 copy.229
  530.1 4.0 fusion.5
  534.1 4.1 gather_fusion.6
  538.2 3.2 broadcast_select_fusion.1
  558.2 62.3 %collective-permute-done.23 = bf16[8,64,768]{2,1,0:T(8,128)(2,1)} collective-permute-done((bf16[8,64,768]{2,1,0:T(8,128)(2,1)}, bf16[8,64,768]{2,1,0:T(8,128)(2,1)}, u32[]{:S(2)}, u32[]{:S(2)}) %collective-permute-start.23) | collective-permute-done | bytes 786464 | tf_op jit(solution)/shard_map/ppermute | solution.py:33
  624.9 2.9 convert_bitcast_fusion
  638.4 9.7 %collective-permute-done.39 = bf16[1,96,1728]{2,1,0:T(8,128)(2,1)S(1)} collective-permute-done((bf16[1,96,1728]{2,1,0:T(8,128)(2,1)S(1)}, bf16[1,96,1728]{2,1,0:T(8,128)(2,1)S(1)}, u32[]{:S(2)}, u32[]{:S(2)}) %collective-permute-start.39) | collective-permute-done | bytes 331808 | tf_op jit(solution)/shard_map/ppermute | solution.py:33
  648.1 14.3 %collective-permute-done.38 = bf16[1,96,1728]{2,1,0:T(8,128)(2,1)S(1)} collective-permute-done((bf16[1,96,1728]{2,1,0:T(8,128)(2,1)S(1)}, bf16[1,96,1728]{2,1,0:T(8,128)(2,1)S(1)}, u32[]{:S(2)}, u32[]{:S(2)}) %collective-permute-start.38) | collective-permute-done | bytes 331808 | tf_op jit(solution)/shard_map/ppermute | solution.py:33
  (561 shorter events, 196.1 us)
Async XLA Ops:
  0.7 132.5 %copy-start = (bf16[16,128,768]{2,1,0:T(8,128)(2,1)S(1)}, bf16[16,128,768]{2,1,0:T(8,128)(2,1)}, u32[]{:S(2)}) copy-start(bf16[16,128,768]{2,1,0:T(8,128)(2,1)} %param.27) | copy-start | bytes 9437188
  3.0 21.2 %collective-permute-start.11 = (bf16[1,96,1728]{2,1,0:T(8,128)(2,1)S(1)}, bf16[1,96,1728]{2,1,0:T(8,128)(2,1)}, u32[]{:S(2)}, u32[]{:S(2)}) collective-permute-start(bf16[1,96,1728]{2,1,0:T(8,128)(2,1)S(1)} %bitcast.378), channel_id=1, source_target_pairs={{0,24},{1,25},{2,26},{3,27},{4,28},{5,29},{6,30},{7,31},{8,16},{9,... | collective-permute-start | bytes 995336 | tf_op jit(solution)/shard_map/ppermute | solution.py:33
  8.1 36.7 %collective-permute-start.10 = (bf16[1,96,1728]{2,1,0:T(8,128)(2,1)S(1)}, bf16[1,96,1728]{2,1,0:T(8,128)(2,1)}, u32[]{:S(2)}, u32[]{:S(2)}) collective-permute-start(bf16[1,96,1728]{2,1,0:T(8,128)(2,1)S(1)} %bitcast.379), channel_id=1, source_target_pairs={{0,16},{1,17},{2,18},{3,19},{4,20},{5,21},{6,22},{7,23},{8,24},{9,... | collective-permute-start | bytes 995336 | tf_op jit(solution)/shard_map/ppermute | solution.py:33
  8.1 36.7 %collective-permute-start.9 = (bf16[1,96,1728]{2,1,0:T(8,128)(2,1)S(1)}, bf16[1,96,1728]{2,1,0:T(8,128)(2,1)}, u32[]{:S(2)}, u32[]{:S(2)}) collective-permute-start(bf16[1,96,1728]{2,1,0:T(8,128)(2,1)S(1)} %bitcast.380), channel_id=1, source_target_pairs={{0,8},{1,9},{2,10},{3,11},{4,12},{5,13},{6,14},{7,15},{8,0},{9,1},... | collective-permute-start | bytes 995336 | tf_op jit(solution)/shard_map/ppermute | solution.py:33
  10.4 127.9 %collective-permute-start.3 = (bf16[1,96,576]{1,2,0:T(8,128)(2,1)}, bf16[1,96,576]{1,2,0:T(8,128)(2,1)}, u32[]{:S(2)}, u32[]{:S(2)}) collective-permute-start(bf16[1,96,576]{1,2,0:T(8,128)(2,1)} %bitcast.391), channel_id=1, source_target_pairs={{0,24},{1,25},{2,26},{3,27},{4,28},{5,29},{6,30},{7,31},{8,16},{9,... | collective-permute-start | bytes 331784 | tf_op jit(solution)/shard_map/ppermute | solution.py:33
  14.2 124.2 %collective-permute-start.2 = (bf16[1,96,576]{1,2,0:T(8,128)(2,1)}, bf16[1,96,576]{1,2,0:T(8,128)(2,1)}, u32[]{:S(2)}, u32[]{:S(2)}) collective-permute-start(bf16[1,96,576]{1,2,0:T(8,128)(2,1)} %bitcast.392), channel_id=1, source_target_pairs={{0,16},{1,17},{2,18},{3,19},{4,20},{5,21},{6,22},{7,23},{8,24},{9,... | collective-permute-start | bytes 331784 | tf_op jit(solution)/shard_map/ppermute | solution.py:33
  47.7 36.3 %collective-permute-start.14 = (bf16[4,96,1728]{2,1,0:T(8,128)(2,1)}, bf16[4,96,1728]{2,1,0:T(8,128)(2,1)}, u32[]{:S(2)}, u32[]{:S(2)}) collective-permute-start(bf16[4,96,1728]{2,1,0:T(8,128)(2,1)} %get-tuple-element.221), channel_id=1, source_target_pairs={{0,6},{1,7},{2,4},{3,5},{4,2},{5,3},{6,0},{7,1},{8,14},{9,15},{10,... | collective-permute-start | bytes 3981320 | tf_op jit(solution)/shard_map/ppermute | solution.py:33
  50.2 58.5 %collective-permute-start.13 = (bf16[4,96,1728]{2,1,0:T(8,128)(2,1)}, bf16[4,96,1728]{2,1,0:T(8,128)(2,1)}, u32[]{:S(2)}, u32[]{:S(2)}) collective-permute-start(bf16[4,96,1728]{2,1,0:T(8,128)(2,1)} %get-tuple-element.221), channel_id=1, source_target_pairs={{0,2},{1,3},{2,0},{3,1},{4,6},{5,7},{6,4},{7,5},{8,10},{9,11},{10,... | collective-permute-start | bytes 3981320 | tf_op jit(solution)/shard_map/ppermute | solution.py:33
  51.4 92.6 %all-to-all-start.1 = ((bf16[8,120,128]{2,1,0:T(8,128)(2,1)}), bf16[8,120,128]{2,1,0:T(8,128)(2,1)S(1)}, u32[]{:S(2)}, u32[]{:S(2)}) async-start(bf16[8,120,128]{2,1,0:T(8,128)(2,1)} %broadcast_in_dim.144), calls=%async_computation.1 | async-start | bytes 491520 | tf_op jit(solution)/shard_map/all_to_all | solution.py:327
  55.4 68.7 %copy-start.69 = (pred[8]{0:T(512)(128)(4,1)}, pred[8]{0:T(512)(128)(4,1)S(1)}, u32[]{:S(2)}) copy-start(pred[8]{0:T(512)(128)(4,1)S(1)} %compare_and_fusion) | copy-start | bytes 28
  55.4 61.1 %collective-permute-start.12 = (bf16[4,96,1728]{2,1,0:T(8,128)(2,1)}, bf16[4,96,1728]{2,1,0:T(8,128)(2,1)}, u32[]{:S(2)}, u32[]{:S(2)}) collective-permute-start(bf16[4,96,1728]{2,1,0:T(8,128)(2,1)} %get-tuple-element.221), channel_id=1, source_target_pairs={{0,4},{1,5},{2,6},{3,7},{4,0},{5,1},{6,2},{7,3},{8,12},{9,13},{10,... | collective-permute-start | bytes 3981320 | tf_op jit(solution)/shard_map/ppermute | solution.py:33
  62.1 114.7 %copy-start.65 = (s32[1024]{0:T(1024)}, s32[1024]{0:T(1024)S(1)}, u32[]{:S(2)}) copy-start(s32[1024]{0:T(1024)S(1)} %pad_clamp_fusion.1) | copy-start | bytes 12292
  84.1 54.2 %collective-permute-start.1 = (bf16[1,96,576]{1,2,0:T(8,128)(2,1)}, bf16[1,96,576]{1,2,0:T(8,128)(2,1)S(1)}, u32[]{:S(2)}, u32[]{:S(2)}) collective-permute-start(bf16[1,96,576]{1,2,0:T(8,128)(2,1)} %bitcast.393), channel_id=1, source_target_pairs={{0,8},{1,9},{2,10},{3,11},{4,12},{5,13},{6,14},{7,15},{8,0},{9,1},... | collective-permute-start | bytes 331784 | tf_op jit(solution)/shard_map/ppermute | solution.py:33
  131.3 96.9 %collective-permute-start.15 = (bf16[2,8,96,1728]{3,2,1,0:T(8,128)(2,1)}, bf16[2,8,96,1728]{3,2,1,0:T(8,128)(2,1)}, u32[]{:S(2)}, u32[]{:S(2)}) collective-permute-start(bf16[2,8,96,1728]{3,2,1,0:T(8,128)(2,1)} %pad_maximum_fusion), channel_id=1, source_target_pairs={{0,1},{1,0},{2,3},{3,2},{4,5},{5,4},{6,7},{7,6},{8,9},{9,8},{10,11... | collective-permute-start | bytes 15925256 | tf_op jit(solution)/shard_map/ppermute | solution.py:33
  140.6 25.8 %copy-start.108 = (f32[3]{0:T(128)S(1)}, f32[3]{0:T(128)}, u32[]{:S(2)}) copy-start(f32[3]{0:T(128)} %pad.107.clone) | copy-start | bytes 40
  140.6 27.4 %collective-permute-start.6 = (bf16[4,96,576]{2,1,0:T(8,128)(2,1)}, bf16[4,96,576]{2,1,0:T(8,128)(2,1)S(1)}, u32[]{:S(2)}, u32[]{:S(2)}) collective-permute-start(bf16[4,96,576]{2,1,0:T(8,128)(2,1)} %copy.181), channel_id=1, source_target_pairs={{0,6},{1,7},{2,4},{3,5},{4,2},{5,3},{6,0},{7,1},{8,14},{9,15},{10,... | collective-permute-start | bytes 1327112 | tf_op jit(solution)/shard_map/ppermute | solution.py:33
  142.3 25.7 %collective-permute-start.5 = (bf16[4,96,576]{2,1,0:T(8,128)(2,1)}, bf16[4,96,576]{2,1,0:T(8,128)(2,1)S(1)}, u32[]{:S(2)}, u32[]{:S(2)}) collective-permute-start(bf16[4,96,576]{2,1,0:T(8,128)(2,1)} %copy.181), channel_id=1, source_target_pairs={{0,2},{1,3},{2,0},{3,1},{4,6},{5,7},{6,4},{7,5},{8,10},{9,11},{10,... | collective-permute-start | bytes 1327112 | tf_op jit(solution)/shard_map/ppermute | solution.py:33
  143.5 29.2 %collective-permute-start.4 = (bf16[4,96,576]{2,1,0:T(8,128)(2,1)}, bf16[4,96,576]{2,1,0:T(8,128)(2,1)}, u32[]{:S(2)}, u32[]{:S(2)}) collective-permute-start(bf16[4,96,576]{2,1,0:T(8,128)(2,1)} %copy.181), channel_id=1, source_target_pairs={{0,4},{1,5},{2,6},{3,7},{4,0},{5,1},{6,2},{7,3},{8,12},{9,13},{10,... | collective-permute-start | bytes 1327112 | tf_op jit(solution)/shard_map/ppermute | solution.py:33
  144.1 41.9 %all-to-all-start = ((bf16[8,64,768]{2,1,0:T(8,128)(2,1)}), bf16[8,64,768]{2,1,0:T(8,128)(2,1)}, u32[]{:S(2)}, u32[]{:S(2)}) async-start(bf16[8,64,768]{2,1,0:T(8,128)(2,1)} %dynamic-slice_bitcast_fusion.1), calls=%async_computation | async-start | bytes 1572864 | tf_op jit(solution)/shard_map/all_to_all | solution.py:303
  148.6 19.4 %copy-start.34 = (bf16[1,8,120,128]{3,1,2,0:T(8,128)(2,1)}, bf16[1,8,120,128]{3,1,2,0:T(8,128)(2,1)S(1)}, u32[]{:S(2)}) copy-start(bf16[1,8,120,128]{3,1,2,0:T(8,128)(2,1)S(1)} %copy.243) | copy-start | bytes 737284
  149.8 16.1 %collective-permute-start.7 = (bf16[1152]{0:T(1024)(128)(2,1)S(1)}, bf16[1152]{0:T(1024)(128)(2,1)S(1)}, u32[]{:S(2)}, u32[]{:S(2)}) collective-permute-start(bf16[1152]{0:T(1024)(128)(2,1)S(1)} %dynamic-update-slice.4), channel_id=1, source_target_pairs={{0,2},{1,3},{2,0},{3,1},{4,6},{5,7},{6,4},{7,5},{8,10},{9,11},{10,... | collective-permute-start | bytes 6920 | tf_op jit(solution)/shard_map/ppermute | solution.py:33
  153.8 95.1 %copy-start.58 = (f32[768]{0:T(1024)}, f32[768]{0:T(1024)S(1)}, u32[]{:S(2)}) copy-start(f32[768]{0:T(1024)S(1)} %mul.407) | copy-start | bytes 9220
  166.2 1.2 collective-permute-start.16
  185.9 90.7 %all-to-all-start.4 = ((bf16[8,64,768]{2,1,0:T(8,128)(2,1)}), bf16[8,64,768]{2,1,0:T(8,128)(2,1)}, u32[]{:S(2)}, u32[]{:S(2)}) async-start(bf16[8,64,768]{2,1,0:T(8,128)(2,1)} %dynamic-slice_bitcast_fusion), calls=%async_computation.4 | async-start | bytes 1572864 | tf_op jit(solution)/shard_map/all_to_all | solution.py:303
  190.5 10.3 %collective-permute-start = (bf16[512,768]{1,0:T(8,128)(2,1)}, bf16[512,768]{1,0:T(8,128)(2,1)S(1)}, u32[]{:S(2)}, u32[]{:S(2)}) collective-permute-start(bf16[512,768]{1,0:T(8,128)(2,1)} %bitcast.2), channel_id=1, source_target_pairs={{0,1},{1,0},{2,3},{3,2},{4,5},{5,4},{6,7},{7,6},{8,9},{9,8},{10,11... | collective-permute-start | bytes 2359304 | tf_op jit(solution)/shard_map/ppermute | solution.py:33
  193.9 41.0 %copy-start.40 = (bf16[768,192]{1,0:T(8,128)(2,1)}, bf16[768,192]{1,0:T(8,128)(2,1)S(1)}, u32[]{:S(2)}) copy-start(bf16[768,192]{1,0:T(8,128)(2,1)S(1)} %get-tuple-element.281) | copy-start | bytes 884740
  193.9 41.0 %copy-start.42 = (bf16[768,192]{1,0:T(8,128)(2,1)}, bf16[768,192]{1,0:T(8,128)(2,1)S(1)}, u32[]{:S(2)}) copy-start(bf16[768,192]{1,0:T(8,128)(2,1)S(1)} %get-tuple-element.282) | copy-start | bytes 884740
  227.7 7.2 %collective-permute-start.8 = (bf16[512,384]{1,0:T(8,128)(2,1)S(1)}, bf16[512,384]{1,0:T(8,128)(2,1)S(1)}, u32[]{:S(2)}, u32[]{:S(2)}) collective-permute-start(bf16[512,384]{1,0:T(8,128)(2,1)S(1)} %get-tuple-element.231), channel_id=1, source_target_pairs={{0,1},{1,0},{2,3},{3,2},{4,5},{5,4},{6,7},{7,6},{8,9},{9,8},{10,11... | collective-permute-start | bytes 1179656 | tf_op jit(solution)/shard_map/ppermute | solution.py:33
  234.9 14.0 %copy-start.28 = (bf16[768,768]{1,0:T(8,128)(2,1)}, bf16[768,768]{1,0:T(8,128)(2,1)S(1)}, u32[]{:S(2)}) copy-start(bf16[768,768]{1,0:T(8,128)(2,1)S(1)} %get-tuple-element.189) | copy-start | bytes 3538948
  234.9 14.0 %copy-start.30 = (bf16[768,768]{1,0:T(8,128)(2,1)}, bf16[768,768]{1,0:T(8,128)(2,1)S(1)}, u32[]{:S(2)}) copy-start(bf16[768,768]{1,0:T(8,128)(2,1)S(1)} %get-tuple-element.190) | copy-start | bytes 3538948
  259.2 4.3 collective-permute-start.19
  306.8 35.0 %collective-permute-start.20 = (f32[1,128]{1,0:T(1,128)}, f32[1,128]{1,0:T(1,128)}, u32[]{:S(2)}, u32[]{:S(2)}) collective-permute-start(f32[1,128]{1,0:T(1,128)} %fusion.77), channel_id=1, source_target_pairs={{0,2},{1,3},{2,0},{3,1},{4,6},{5,7},{6,4},{7,5},{8,10},{9,11},{10,... | collective-permute-start | bytes 1544 | tf_op jit(solution)/shard_map/ppermute | solution.py:33
  335.7 14.1 %copy-start.50 = (f32[128,14]{1,0:T(8,128)S(1)}, f32[128,14]{1,0:T(8,128)}, u32[]{:S(2)}) copy-start(f32[128,14]{1,0:T(8,128)} %multiply_multiply_fusion.5) | copy-start | bytes 21508
  335.7 14.9 %copy-start.89 = (f32[768]{0:T(1024)S(1)}, f32[768]{0:T(1024)}, u32[]{:S(2)}) copy-start(f32[768]{0:T(1024)} %get-tuple-element.150) | copy-start | bytes 9220
  335.8 15.0 %copy-start.92 = (f32[768]{0:T(1024)S(1)}, f32[768]{0:T(1024)}, u32[]{:S(2)}) copy-start(f32[768]{0:T(1024)} %get-tuple-element.152) | copy-start | bytes 9220
  335.8 15.0 %copy-start.61 = (f32[768]{0:T(1024)S(1)}, f32[768]{0:T(1024)}, u32[]{:S(2)}) copy-start(f32[768]{0:T(1024)} %get-tuple-element.171) | copy-start | bytes 9220
  335.8 15.1 %copy-start.62 = (f32[768]{0:T(1024)S(1)}, f32[768]{0:T(1024)}, u32[]{:S(2)}) copy-start(f32[768]{0:T(1024)} %get-tuple-element.173) | copy-start | bytes 9220
  335.8 15.2 %copy-start.91 = (f32[768]{0:T(1024)S(1)}, f32[768]{0:T(1024)}, u32[]{:S(2)}) copy-start(f32[768]{0:T(1024)} %get-tuple-element.157) | copy-start | bytes 9220
  335.8 15.2 %copy-start.86 = (f32[768]{0:T(1024)S(1)}, f32[768]{0:T(1024)}, u32[]{:S(2)}) copy-start(f32[768]{0:T(1024)} %get-tuple-element.156) | copy-start | bytes 9220
  343.1 30.5 %all-to-all-start.3 = ((f32[8,8,128]{2,1,0:T(8,128)}), f32[8,8,128]{2,1,0:T(8,128)}, u32[]{:S(2)}, u32[]{:S(2)}) async-start(f32[8,8,128]{2,1,0:T(8,128)} %broadcast_in_dim.159), calls=%async_computation.3 | async-start | bytes 65536 | tf_op jit(solution)/shard_map/all_to_all | solution.py:538
  361.5 21.3 %collective-permute-start.21 = (bf16[512,384]{1,0:T(8,128)(2,1)}, bf16[512,384]{1,0:T(8,128)(2,1)}, u32[]{:S(2)}, u32[]{:S(2)}) collective-permute-start(bf16[512,384]{1,0:T(8,128)(2,1)} %get-tuple-element.229), channel_id=1, source_target_pairs={{0,1},{1,0},{2,3},{3,2},{4,5},{5,4},{6,7},{7,6},{8,9},{9,8},{10,11... | collective-permute-start | bytes 1179656 | tf_op jit(solution)/shard_map/ppermute | solution.py:33
  361.5 145.9 %collective-permute-start.33 = (bf16[2,768,1728]{1,2,0:T(8,128)(2,1)}, bf16[2,768,1728]{1,2,0:T(8,128)(2,1)}, u32[]{:S(2)}, u32[]{:S(2)}) collective-permute-start(bf16[2,768,1728]{1,2,0:T(8,128)(2,1)} %copy.215), channel_id=1, source_target_pairs={{0,1},{1,0},{2,3},{3,2},{4,5},{5,4},{6,7},{7,6},{8,9},{9,8},{10,11... | collective-permute-start | bytes 15925256 | tf_op jit(solution)/shard_map/ppermute | solution.py:33
  373.7 108.9 %all-to-all-start.2 = ((bf16[8,64,768]{2,1,0:T(8,128)(2,1)}), bf16[8,64,768]{2,1,0:T(8,128)(2,1)}, u32[]{:S(2)}, u32[]{:S(2)}) async-start(bf16[8,64,768]{2,1,0:T(8,128)(2,1)} %bitcast.57), calls=%async_computation.2 | async-start | bytes 1572864 | tf_op jit(solution)/shard_map/all_to_all | solution.py:394
  407.0 46.8 %collective-permute-start.31 = (bf16[8,128,128]{2,1,0:T(8,128)(2,1)S(1)}, bf16[8,128,128]{2,1,0:T(8,128)(2,1)S(1)}, u32[]{:S(2)}, u32[]{:S(2)}) collective-permute-start(bf16[8,128,128]{2,1,0:T(8,128)(2,1)S(1)} %bitcast.397), channel_id=1, source_target_pairs={{0,1},{1,0},{2,3},{3,2},{4,5},{5,4},{6,7},{7,6},{8,9},{9,8},{10,11... | collective-permute-start | bytes 786440 | tf_op jit(solution)/shard_map/ppermute | solution.py:33
  437.1 17.6 %collective-permute-start.25 = (bf16[4,96,576]{2,1,0:T(8,128)(2,1)}, bf16[4,96,576]{2,1,0:T(8,128)(2,1)}, u32[]{:S(2)}, u32[]{:S(2)}) collective-permute-start(bf16[4,96,576]{2,1,0:T(8,128)(2,1)} %copy.201), channel_id=1, source_target_pairs={{0,4},{1,5},{2,6},{3,7},{4,0},{5,1},{6,2},{7,3},{8,12},{9,13},{10,... | collective-permute-start | bytes 1327112 | tf_op jit(solution)/shard_map/ppermute | solution.py:33
  446.8 15.8 %collective-permute-start.27 = (bf16[4,96,576]{2,1,0:T(8,128)(2,1)}, bf16[4,96,576]{2,1,0:T(8,128)(2,1)}, u32[]{:S(2)}, u32[]{:S(2)}) collective-permute-start(bf16[4,96,576]{2,1,0:T(8,128)(2,1)} %copy.206), channel_id=1, source_target_pairs={{0,6},{1,7},{2,4},{3,5},{4,2},{5,3},{6,0},{7,1},{8,14},{9,15},{10,... | collective-permute-start | bytes 1327112 | tf_op jit(solution)/shard_map/ppermute | solution.py:33
  447.6 24.9 %collective-permute-start.26 = (bf16[4,96,576]{2,1,0:T(8,128)(2,1)}, bf16[4,96,576]{2,1,0:T(8,128)(2,1)}, u32[]{:S(2)}, u32[]{:S(2)}) collective-permute-start(bf16[4,96,576]{2,1,0:T(8,128)(2,1)} %copy.204), channel_id=1, source_target_pairs={{0,2},{1,3},{2,0},{3,1},{4,6},{5,7},{6,4},{7,5},{8,10},{9,11},{10,... | collective-permute-start | bytes 1327112 | tf_op jit(solution)/shard_map/ppermute | solution.py:33
  453.7 45.4 %collective-permute-start.22 = (bf16[512,768]{1,0:T(8,128)(2,1)}, bf16[512,768]{1,0:T(8,128)(2,1)}, u32[]{:S(2)}, u32[]{:S(2)}) collective-permute-start(bf16[512,768]{1,0:T(8,128)(2,1)} %slice.644), channel_id=1, source_target_pairs={{0,1},{1,0},{2,3},{3,2},{4,5},{5,4},{6,7},{7,6},{8,9},{9,8},{10,11... | collective-permute-start | bytes 2359304 | tf_op jit(solution)/shard_map/ppermute | solution.py:33
  454.6 27.1 %collective-permute-start.32 = (bf16[8,128,128]{2,1,0:T(8,128)(2,1)}, bf16[8,128,128]{2,1,0:T(8,128)(2,1)S(1)}, u32[]{:S(2)}, u32[]{:S(2)}) collective-permute-start(bf16[8,128,128]{2,1,0:T(8,128)(2,1)} %fusion.33), channel_id=1, source_target_pairs={{0,2},{1,3},{2,0},{3,1},{4,6},{5,7},{6,4},{7,5},{8,10},{9,11},{10,... | collective-permute-start | bytes 786440 | tf_op jit(solution)/shard_map/ppermute | solution.py:33
  477.4 10.3 %collective-permute-start.28 = (bf16[1,96,576]{1,2,0:T(8,128)(2,1)S(1)}, bf16[1,96,576]{1,2,0:T(8,128)(2,1)S(1)}, u32[]{:S(2)}, u32[]{:S(2)}) collective-permute-start(bf16[1,96,576]{1,2,0:T(8,128)(2,1)S(1)} %get-tuple-element.234), channel_id=1, source_target_pairs={{0,8},{1,9},{2,10},{3,11},{4,12},{5,13},{6,14},{7,15},{8,0},{9,1},... | collective-permute-start | bytes 331784 | tf_op jit(solution)/shard_map/ppermute | solution.py:33
  479.3 8.9 %collective-permute-start.30 = (bf16[1,96,576]{1,2,0:T(8,128)(2,1)S(1)}, bf16[1,96,576]{1,2,0:T(8,128)(2,1)S(1)}, u32[]{:S(2)}, u32[]{:S(2)}) collective-permute-start(bf16[1,96,576]{1,2,0:T(8,128)(2,1)S(1)} %get-tuple-element.235), channel_id=1, source_target_pairs={{0,24},{1,25},{2,26},{3,27},{4,28},{5,29},{6,30},{7,31},{8,16},{9,... | collective-permute-start | bytes 331784 | tf_op jit(solution)/shard_map/ppermute | solution.py:33
  481.7 15.5 %collective-permute-start.29 = (bf16[1,96,576]{1,2,0:T(8,128)(2,1)S(1)}, bf16[1,96,576]{1,2,0:T(8,128)(2,1)S(1)}, u32[]{:S(2)}, u32[]{:S(2)}) collective-permute-start(bf16[1,96,576]{1,2,0:T(8,128)(2,1)S(1)} %get-tuple-element.236), channel_id=1, source_target_pairs={{0,16},{1,17},{2,18},{3,19},{4,20},{5,21},{6,22},{7,23},{8,24},{9,... | collective-permute-start | bytes 331784 | tf_op jit(solution)/shard_map/ppermute | solution.py:33
  482.6 20.0 %all-to-all-start.6 = ((bf16[8,128,128]{2,1,0:T(8,128)(2,1)}), bf16[8,128,128]{2,1,0:T(8,128)(2,1)S(1)}, u32[]{:S(2)}, u32[]{:S(2)}) async-start(bf16[8,128,128]{2,1,0:T(8,128)(2,1)} %add_convert_fusion.2), calls=%async_computation.6 | async-start | bytes 524288 | tf_op jit(solution)/shard_map/all_to_all | solution.py:517
  501.9 51.9 %collective-permute-start.17 = (bf16[8,64,768]{2,1,0:T(8,128)(2,1)}, bf16[8,64,768]{2,1,0:T(8,128)(2,1)}, u32[]{:S(2)}, u32[]{:S(2)}) collective-permute-start(bf16[8,64,768]{2,1,0:T(8,128)(2,1)} %all-to-all-done.2), channel_id=1, source_target_pairs={{0,2},{1,3},{2,0},{3,1},{4,6},{5,7},{6,4},{7,5},{8,10},{9,11},{10,... | collective-permute-start | bytes 2359304 | tf_op jit(solution)/shard_map/ppermute | solution.py:33
  502.6 45.5 %all-to-all-start.5 = ((bf16[8,64,768]{2,1,0:T(8,128)(2,1)}), bf16[8,64,768]{2,1,0:T(8,128)(2,1)}, u32[]{:S(2)}, u32[]{:S(2)}) async-start(bf16[8,64,768]{2,1,0:T(8,128)(2,1)} %bitcast.91), calls=%async_computation.5 | async-start | bytes 1572864 | tf_op jit(solution)/shard_map/all_to_all | solution.py:394
  544.2 80.6 %collective-permute-start.34 = (bf16[4,96,1728]{2,1,0:T(8,128)(2,1)}, bf16[4,96,1728]{2,1,0:T(8,128)(2,1)}, u32[]{:S(2)}, u32[]{:S(2)}) collective-permute-start(bf16[4,96,1728]{2,1,0:T(8,128)(2,1)} %slice_bitcast_fusion.2), channel_id=1, source_target_pairs={{0,4},{1,5},{2,6},{3,7},{4,0},{5,1},{6,2},{7,3},{8,12},{9,13},{10,... | collective-permute-start | bytes 3981320 | tf_op jit(solution)/shard_map/ppermute | solution.py:33
  546.3 78.6 %collective-permute-start.35 = (bf16[4,96,1728]{2,1,0:T(8,128)(2,1)}, bf16[4,96,1728]{2,1,0:T(8,128)(2,1)}, u32[]{:S(2)}, u32[]{:S(2)}) collective-permute-start(bf16[4,96,1728]{2,1,0:T(8,128)(2,1)} %get-tuple-element.209), channel_id=1, source_target_pairs={{0,2},{1,3},{2,0},{3,1},{4,6},{5,7},{6,4},{7,5},{8,10},{9,11},{10,... | collective-permute-start | bytes 3981320 | tf_op jit(solution)/shard_map/ppermute | solution.py:33
  547.7 77.2 %collective-permute-start.36 = (bf16[4,96,1728]{2,1,0:T(8,128)(2,1)}, bf16[4,96,1728]{2,1,0:T(8,128)(2,1)}, u32[]{:S(2)}, u32[]{:S(2)}) collective-permute-start(bf16[4,96,1728]{2,1,0:T(8,128)(2,1)} %get-tuple-element.210), channel_id=1, source_target_pairs={{0,6},{1,7},{2,4},{3,5},{4,2},{5,3},{6,0},{7,1},{8,14},{9,15},{10,... | collective-permute-start | bytes 3981320 | tf_op jit(solution)/shard_map/ppermute | solution.py:33
  548.0 72.5 %collective-permute-start.23 = (bf16[8,64,768]{2,1,0:T(8,128)(2,1)}, bf16[8,64,768]{2,1,0:T(8,128)(2,1)}, u32[]{:S(2)}, u32[]{:S(2)}) collective-permute-start(bf16[8,64,768]{2,1,0:T(8,128)(2,1)} %all-to-all-done.5), channel_id=1, source_target_pairs={{0,2},{1,3},{2,0},{3,1},{4,6},{5,7},{6,4},{7,5},{8,10},{9,11},{10,... | collective-permute-start | bytes 2359304 | tf_op jit(solution)/shard_map/ppermute | solution.py:33
  556.0 75.8 %collective-permute-start.18 = (bf16[8,2,64,768]{3,2,0,1:T(8,128)(2,1)S(1)}, bf16[8,2,64,768]{3,2,0,1:T(8,128)(2,1)S(1)}, u32[]{:S(2)}, u32[]{:S(2)}) collective-permute-start(bf16[8,2,64,768]{3,2,0,1:T(8,128)(2,1)S(1)} %maximum_select_fusion.2), channel_id=1, source_target_pairs={{0,1},{1,0},{2,3},{3,2},{4,5},{5,4},{6,7},{7,6},{8,9},{9,8},{10,11... | collective-permute-start | bytes 4718600 | tf_op jit(solution)/shard_map/ppermute | solution.py:33
  622.7 11.6 %collective-permute-start.24 = (bf16[8,2,64,768]{3,2,0,1:T(8,128)(2,1)S(1)}, bf16[8,2,64,768]{3,2,0,1:T(8,128)(2,1)S(1)}, u32[]{:S(2)}, u32[]{:S(2)}) collective-permute-start(bf16[8,2,64,768]{3,2,0,1:T(8,128)(2,1)S(1)} %maximum_select_fusion.4), channel_id=1, source_target_pairs={{0,1},{1,0},{2,3},{3,2},{4,5},{5,4},{6,7},{7,6},{8,9},{9,8},{10,11... | collective-permute-start | bytes 4718600 | tf_op jit(solution)/shard_map/ppermute | solution.py:33
  627.9 10.5 %collective-permute-start.37 = (bf16[1,96,1728]{2,1,0:T(8,128)(2,1)S(1)}, bf16[1,96,1728]{2,1,0:T(8,128)(2,1)S(1)}, u32[]{:S(2)}, u32[]{:S(2)}) collective-permute-start(bf16[1,96,1728]{2,1,0:T(8,128)(2,1)S(1)} %get-tuple-element.217), channel_id=1, source_target_pairs={{0,8},{1,9},{2,10},{3,11},{4,12},{5,13},{6,14},{7,15},{8,0},{9,1},... | collective-permute-start | bytes 995336 | tf_op jit(solution)/shard_map/ppermute | solution.py:33
  629.4 18.7 %collective-permute-start.39 = (bf16[1,96,1728]{2,1,0:T(8,128)(2,1)S(1)}, bf16[1,96,1728]{2,1,0:T(8,128)(2,1)S(1)}, u32[]{:S(2)}, u32[]{:S(2)}) collective-permute-start(bf16[1,96,1728]{2,1,0:T(8,128)(2,1)S(1)} %get-tuple-element.218), channel_id=1, source_target_pairs={{0,24},{1,25},{2,26},{3,27},{4,28},{5,29},{6,30},{7,31},{8,16},{9,... | collective-permute-start | bytes 995336 | tf_op jit(solution)/shard_map/ppermute | solution.py:33
  631.8 30.6 %collective-permute-start.38 = (bf16[1,96,1728]{2,1,0:T(8,128)(2,1)S(1)}, bf16[1,96,1728]{2,1,0:T(8,128)(2,1)S(1)}, u32[]{:S(2)}, u32[]{:S(2)}) collective-permute-start(bf16[1,96,1728]{2,1,0:T(8,128)(2,1)S(1)} %get-tuple-element.219), channel_id=1, source_target_pairs={{0,16},{1,17},{2,18},{3,19},{4,20},{5,21},{6,22},{7,23},{8,24},{9,... | collective-permute-start | bytes 995336 | tf_op jit(solution)/shard_map/ppermute | solution.py:33
  (100 other events, 475.4 us)

commit v2 on v1

v2 whole, which is shorter than its diff:
```python
import functools

import jax
import jax.numpy as jnp
import numpy as np
from jax import lax
from jax.experimental import pallas as pl
from jax.experimental.pallas import tpu as pltpu
from jax.sharding import PartitionSpec as P

D = 768
HS = 64
CW = 128
PH = 2
CLASSES = 14
EPSILON = 1e-06
NEGATIVE = -1e30
LOG2E = 1.4426950408889634
HIGHEST = lax.Precision.HIGHEST
BF = jnp.bfloat16
F32 = jnp.float32
AXES = ("dp", "mp")
QB = 256
RB = 128
SLOW = 1
ROOM = 16


def dot(a, b, ca, cb):
    return lax.dot_general(a, b, (((ca,), (cb,)), ((), ())), preferred_element_type=F32)


def hop(x, dbit, mbit):
    nd, nm = lax.axis_size("dp"), lax.axis_size("mp")
    pairs = [(d * nm + m, (d ^ dbit) * nm + (m ^ mbit)) for d in range(nd) for m in range(nm)]
    return lax.ppermute(x, AXES, pairs)


def after(x, *others):
    return lax.optimization_barrier((x, *others))[0]


def bit_groups(nd):
    bits = []
    b = nd // 2
    while b > 1:
        bits.append(b)
        b //= 2
    groups = [bits[i : i + 2] for i in range(0, len(bits), 2)]
    out = []
    for g in groups:
        out.append([0, g[0]] if len(g) == 1 else [0, g[1], g[0], g[0] + g[1]])
    return out


def gather_chips(x):
    nd = lax.axis_size("dp")
    cur = x[None]
    for masks in bit_groups(nd):
        parts = [cur] + [hop(cur, k, 0) for k in masks[1:]]
        cur = jnp.stack(parts, 1).reshape(-1, *x.shape)
    near, far = (hop(cur, 1, 0), hop(cur, 0, 2))
    far2 = hop(cur, 1, 2)
    return (
        jnp.stack([cur, near], 1).reshape(nd, *x.shape),
        jnp.stack([far, far2], 1).reshape(nd, *x.shape),
    )


def scatter_chips(mine, other):
    nd = lax.axis_size("dp")
    tail = mine.shape[1:]
    a = mine.reshape(nd // 2, 2, *tail)
    b = other.reshape(nd // 2, 2, *tail)
    cur = (
        a[:, 0].astype(F32)
        + hop(a[:, 1], 1, 0).astype(F32)
        + hop(b[:, 0], 0, 2).astype(F32)
        + hop(b[:, 1], 1, 2).astype(F32)
    )
    for masks in reversed(bit_groups(nd)):
        low = cur.astype(BF).reshape(-1, len(masks), *tail)
        full = cur.reshape(-1, len(masks), *tail)
        cur = full[:, 0]
        for i, k in enumerate(masks[1:], 1):
            cur = cur + hop(low[:, i], k, 0).astype(F32)
    return cur[0]


def relative(x, me):
    return jnp.take(x, jnp.arange(x.shape[0], dtype=jnp.int32) ^ me, axis=0)


def split3(x):
    a = x.astype(BF)
    r = x - a.astype(F32)
    b = r.astype(BF)
    return a, b, (r - b.astype(F32)).astype(BF)


def swap64(x):
    return jnp.concatenate([x[:, 64:], x[:, :64]], axis=1)


def doubled(kp, head):
    lane = lax.broadcasted_iota(jnp.int32, kp.shape, 1)
    kr = swap64(kp)
    return jnp.where(lane < 64, kp, kr) if head == 0 else jnp.where(lane < 64, kr, kp)


ANY = pl.BlockSpec(memory_space=pl.ANY)
SMEM = pl.BlockSpec(memory_space=pltpu.SMEM)


def room(mib):
    return pltpu.CompilerParams(vmem_limit_bytes=mib << 20)


def call(kernel, outs, args, specs=None, scratch=(), name=None, flops=0, mib=ROOM):
    specs = [pl.BlockSpec(memory_space=pltpu.VMEM) if s is None else s for s in (specs or [None] * len(args))]
    size = sum(a.size * a.dtype.itemsize for a in args) + sum(
        int(np.prod(o.shape)) * np.dtype(o.dtype).itemsize for o in outs
    )
    return pl.pallas_call(
        kernel,
        in_specs=specs,
        out_specs=[pl.BlockSpec(memory_space=pltpu.VMEM)] * len(outs),
        out_shape=outs,
        scratch_shapes=list(scratch),
        cost_estimate=cost(size, flops),
        compiler_params=room(mib),
        name=name,
    )(*args)


def cost(size, flops=0):
    return pl.CostEstimate(flops=int(flops) // SLOW, bytes_accessed=int(size) // SLOW, transcendentals=0)


def sds(shape, dtype=F32):
    return jax.ShapeDtypeStruct(shape, dtype)


def by_rows(kernel, outs, sums, args, consts, info=None, name=None):
    n = args[0].shape[0]

    def cut(a):
        return pl.BlockSpec((RB, a.shape[1]), lambda i: (i, 0))

    def whole(a):
        return pl.BlockSpec(a.shape, lambda i: (0,) * len(a.shape))

    head = [] if info is None else [info]
    size = sum(a.size * a.dtype.itemsize for a in [*args, *consts])
    return pl.pallas_call(
        kernel,
        grid=(n // RB,),
        in_specs=[SMEM] * len(head) + [cut(a) for a in args] + [whole(a) for a in consts],
        out_specs=[cut(o) for o in outs] + [whole(o) for o in sums],
        out_shape=[*outs, *sums],
        cost_estimate=cost(size),
        compiler_params=room(ROOM),
        name=name,
    )(*head, *args, *consts)


def start_sums(*refs):
    @pl.when(pl.program_id(0) == 0)
    def _():
        for r in refs:
            r[...] = jnp.zeros(r.shape, F32)


def start(copies):
    for cp in copies:
        cp.start()
    return copies


def load_pair(info, arrays, w_ref, sems):
    if len(arrays) == 1:
        return start([pltpu.make_async_copy(arrays[0].at[0], w_ref, sems.at[0])])
    nz = arrays[0].shape[1]
    rows = D // (2 * nz)
    copies = []
    for x, a in enumerate(arrays):
        for z in range(nz):
            at = pl.multiple_of((info[0] ^ (2 * z + x)) * rows, 16)
            copies.append(
                pltpu.make_async_copy(a.at[0, z, pl.ds(0, rows), :], w_ref.at[pl.ds(at, rows), :], sems.at[len(copies)])
            )
    return start(copies)


def load_rows(info, arrays, b_ref, sems):
    nz = arrays[0].shape[1]
    rows = D // (2 * nz)
    copies = []
    for x, a in enumerate(arrays):
        for z in range(nz):
            copies.append(
                pltpu.make_async_copy(
                    a.at[0, z, pl.ds(rows, 8), :], b_ref.at[info[0] ^ (2 * z + x)], sems.at[len(copies)]
                )
            )
    return start(copies)


def load_weight(info, arrays, w_ref, sems):
    if len(arrays) == 2:
        return start([pltpu.make_async_copy(a.at[0], w_ref.at[i], sems.at[i]) for i, a in enumerate(arrays)])
    nz = arrays[0].shape[1]
    rows = D // (2 * nz)
    copies = []
    for i, a in enumerate(arrays):
        for z in range(nz):
            at = pl.multiple_of((info[0] ^ (2 * z + i % 2)) * rows, 16)
            copies.append(
                pltpu.make_async_copy(
                    a.at[0, z, pl.ds(0, rows), :], w_ref.at[i // 2, pl.ds(at, rows), :], sems.at[len(copies)]
                )
            )
    return start(copies)


def wait(copies):
    for cp in copies:
        cp.wait()


def weight_scratch(arrays):
    count = len(arrays) if len(arrays) == 2 else 4 * arrays[0].shape[1]
    return [pltpu.VMEM((2, D, arrays[0].shape[-1]), BF), pltpu.SemaphoreType.DMA((count,))]


def gather_lines(local):
    k, rows, n = local.shape
    cur = local[:, None]
    for masks in bit_groups(lax.axis_size("dp")):
        parts = [cur] + [hop(cur, b, 0) for b in masks[1:]]
        cur = jnp.stack(parts, 2).reshape(k, -1, rows, n)
    return cur, parts[1:]


def gather_planes(cur, fast):
    near, far, far2 = hop(cur, 1, 0), hop(cur, 0, 2), hop(cur, 1, 2)
    if fast:
        return cur, near, far, far2
    me = lax.axis_index("dp")
    k, half, rows, n = cur.shape

    def ordered(a, b):
        both = jnp.stack([a, b], 2).reshape(k, 2 * half, rows, n)
        return jnp.moveaxis(relative(jnp.moveaxis(both, 1, 0), me), 0, 1).reshape(k, 2 * half * rows, n)

    return ordered(cur, near), ordered(far, far2)


def spread(info, g_ref, k, outs):
    nz = outs[0].shape[1]
    rows = D // (2 * nz)
    for z in range(nz):
        for x in range(2):
            at = pl.multiple_of((info[0] ^ (2 * z + x)) * rows, 8)
            outs[x][k, z, :rows] = g_ref[pl.ds(at, rows), :].astype(BF)


def grad_outs(k, ys, nd, rows, fast, more=0):
    return [sds((k, nd // 2, rows + more, D), BF)] * (2 * ys) if fast else [sds((k, D, D), BF)] * ys


def store_grad(info, k, y, g, g_ref, outs):
    if len(outs[0].shape) == 4:
        g_ref[...] = g
        spread(info, g_ref, k, outs[2 * y : 2 * y + 2])
    else:
        outs[y][k] = g.astype(BF)


def sum_first_kernel(count, *refs):
    parts, (keep_ref, *send_refs) = refs[:count], refs[count:]
    for k in range(parts[0].shape[0]):
        for z in range(parts[0].shape[1]):
            total = parts[0][k, z].astype(F32)
            for r in parts[1:]:
                total = total + r[k, z].astype(F32)
            if z == 0:
                keep_ref[k] = total
            else:
                send_refs[z - 1][k] = total.astype(BF)


def sum_planes(parts):
    if len(parts) == 2:
        return list(parts)
    keep, x, y, xy = parts
    return [keep, hop(x, 1, 0), hop(y, 0, 2), hop(xy, 1, 2)]


def sum_lines(parts):
    nd = lax.axis_size("dp")
    if len(parts) == 2:
        me = lax.axis_index("dp")
        k = parts[0].shape[0]
        near, far = (
            relative(jnp.moveaxis(p.reshape(k, nd, D // nd, D), 0, 1), me) for p in parts
        )
        return scatter_chips(near, far)
    return finish_lines(sum_blocks(parts))


def sum_blocks(parts):
    if len(parts) == 2:
        return parts
    k, nz, rows, n = parts[0].shape
    return call(
        functools.partial(sum_first_kernel, len(parts)),
        [sds((k, rows, n))] + [sds((k, rows, n), BF)] * (nz - 1),
        list(parts),
        name="grad_sum",
    )


def finish_lines(sums):
    own, *send = sums
    for z, piece in enumerate(send, 1):
        own = own + hop(piece, 2 * z, 0).astype(F32)
    return own


def bias_rows(b, first, count, low, high):
    return jnp.concatenate([b[first + i : first + i + 1, low:high] for i in range(count)], axis=1)


def block(ref, i):
    return ref[:, 128 * i : 128 * i + 128]


def attn_fwd_kernel(nh, info, own_ref, sib_ref, bias_ref, aux_ref, *rest):
    *arrays, proj_ref, w_ref, ctx_ref, lse_ref, w_sems, o_ref, b_ref, b_sems = rest
    copies = load_pair(info, arrays, w_ref, w_sems)
    hw = nh * HS
    if len(arrays) == 2:
        wait(load_rows(info, arrays, b_ref, b_sems))
        nd = b_ref.shape[0]
        w = 2 * HS // nd

        def bias_part(first):
            return [b_ref[a, 0:1, h * w : h * w + w] for h in range(nh) for a in range(first, first + nd // 2)]

        q_part, v_part = (
            jnp.concatenate(bias_part(a), axis=1).astype(F32) for a in (0, nd // 2)
        )
    else:
        bias = bias_ref[...].astype(F32)
        q_part = bias_rows(bias, 0, nh, 0, HS)
        v_part = bias_rows(bias, 0, nh, HS, 2 * HS)
    row_bias = jnp.concatenate([q_part, jnp.zeros((1, hw), F32), v_part, jnp.zeros((1, HS), F32)], axis=1)
    wait(copies)
    half = own_ref.shape[0]
    n = 2 * half
    for i, ref in enumerate((own_ref, sib_ref)):
        for j in range(2):
            r = slice(j * half // 2, (j + 1) * half // 2)
            out = dot(ref[r], w_ref[:, : 10 * HS], 1, 0) + row_bias
            proj_ref[i * half + r.start : i * half + r.stop] = out.astype(BF)
    qt = [jnp.transpose(block(proj_ref, i).astype(F32)) * (HS**-0.5 * LOG2E) for i in (0, 1)]
    hi = [q.astype(BF) for q in qt]
    lo = [(q - h.astype(F32)).astype(BF) for q, h in zip(qt, hi)]
    vt = [jnp.transpose(block(proj_ref, i).astype(F32)).astype(BF) for i in (3, 4)]
    row = lax.broadcasted_iota(jnp.int32, (128, QB), 0)
    auxq = jnp.where(row == 0, 1.0, 0.0).astype(BF)
    o_ref[0:HS] = jnp.zeros((HS, n), F32)
    lse_ref[...] = jnp.zeros(lse_ref.shape, F32)
    for h in range(nh):
        kb, kh = ((1, 1), (2, 0), (2, 1))[h]
        lhs = jnp.concatenate([doubled(block(proj_ref, kb), kh), aux_ref[...]], axis=1)
        i, r = h // 2, slice(64 * (h % 2), 64 * (h % 2) + 64)
        vaug = jnp.concatenate([vt[i][r], jnp.ones((16, n), BF)], axis=0)
        to = slice(64 * h + 64, 64 * h + 128)
        for b in range(n // QB):
            s = slice(b * QB, b * QB + QB)
            rhs = jnp.concatenate([hi[i][r, s], lo[i][r, s], auxq], axis=0)
            sc = dot(lhs, rhs, 1, 0)
            m = jnp.max(sc, axis=0, keepdims=True)
            p = jnp.exp2(sc - m).astype(BF)
            o = dot(vaug, p, 1, 0)
            total = o[64:65]
            o_ref[to, s] = o[:64] / total
            lse_ref[h : h + 1, s] = m + jnp.log2(total)
    for j in range(2):
        ctx_ref[:, 128 * j : 128 * j + 128] = jnp.transpose(o_ref[128 * j : 128 * j + 128]).astype(BF)


def attn_fwd(nh, info, own, sib, bias, aux, arrays):
    n = 2 * own.shape[0]
    count = len(arrays) * arrays[0].shape[1] if len(arrays) == 2 else 1
    return call(
        functools.partial(attn_fwd_kernel, nh),
        [sds((n, 10 * HS), BF), sds((D, D), BF), sds((n, 4 * HS), BF), sds((8, n))],
        [info, own, sib, bias, aux, *arrays],
        [SMEM] + [None] * 4 + [ANY] * len(arrays),
        [
            pltpu.SemaphoreType.DMA((count,)),
            pltpu.VMEM((4 * HS, n), F32),
            pltpu.VMEM((count, 8, D), BF),
            pltpu.SemaphoreType.DMA((count,)),
        ],
        "attn_fwd",
        flops=11_000_000_000,
    )


def out_kernel(first, c0_ref, c1_ref, w0_ref, w1_ref, out_ref):
    rows, cols = slice(first, first + out_ref.shape[0]), slice(8 * HS, 12 * HS)
    part = dot(c0_ref[rows], w0_ref[:, cols], 1, 1) + dot(c1_ref[rows], w1_ref[:, cols], 1, 1)
    out_ref[...] = part.astype(out_ref.dtype)


def norm(values, gain, shift):
    center = values - jnp.mean(values, -1, keepdims=True)
    spread_ = jnp.mean(center * center, -1, keepdims=True)
    scale = lax.rsqrt(spread_ + EPSILON)
    normed = center * scale
    return normed * gain + shift, normed, scale


def live_rows(aux_ref):
    return jnp.where(aux_ref[:, 0:1].astype(F32) > -1.0, 1.0, 0.0)


def square(live, v):
    return jnp.sum(jnp.sum(v * v, -1, keepdims=True) * live, axis=0, keepdims=True)


def ln1_kernel(part_ref, got_ref, tok_ref, aux_ref, wide_ref, first_ref, low_ref, n_ref, s_ref, sq_ref):
    start_sums(sq_ref)
    tok = tok_ref[...].astype(F32)
    att = part_ref[...] + got_ref[...].astype(F32) + wide_ref[0:1]
    first, normed, scale = norm(tok + att, wide_ref[1:2], wide_ref[2:3])
    first_ref[...] = first
    low_ref[...] = first.astype(BF)
    n_ref[...] = normed
    s_ref[...] = scale
    live = live_rows(aux_ref)
    lane = lax.broadcasted_iota(jnp.int32, (1, 128), 1)
    out = jnp.zeros((1, 128), F32)
    for i, v in enumerate((tok, att, first)):
        out = jnp.where(lane == i, square(live, v), out)
    sq_ref[...] += out


def hidden_bias(b_ref, nr):
    nd = b_ref.shape[0]
    w = HS // nd
    first = jnp.concatenate([b_ref[a, 0:1, :128] for a in range(nd)], axis=0)
    i = lax.broadcasted_iota(jnp.int32, (128, nr * HS), 0)
    f = lax.broadcasted_iota(jnp.int32, (128, nr * HS), 1)
    place = jnp.where(i == (f // HS) * w + f % w, 1.0, 0.0).astype(BF)
    spread_ = dot(first, place, 1, 0)
    a = lax.broadcasted_iota(jnp.int32, (nd, nr * HS), 0)
    f = lax.broadcasted_iota(jnp.int32, (nd, nr * HS), 1)
    return jnp.sum(jnp.where((f % HS) // w == a, spread_, 0.0), axis=0, keepdims=True)


def ffn_up_kernel(nh, nr, info, x_ref, b0_ref, b1_ref, *rest):
    *up, act_ref, slope_ref, up_ref, sems, r0_ref, r1_ref, r_sems = rest
    copies = load_weight(info, up, up_ref, sems)
    fw = nr * HS
    x = x_ref[...]
    if len(up) == 4:
        for i, r_ref in enumerate((r0_ref, r1_ref)):
            wait(load_rows(info, up[2 * i : 2 * i + 2], r_ref, r_sems))
        biases = [hidden_bias(r_ref, nr) for r_ref in (r0_ref, r1_ref)]
    else:
        biases = [bias_rows(b_ref[...].astype(F32), nh, nr, 0, HS) for b_ref in (b0_ref, b1_ref)]
    wait(copies)
    for y in range(2):
        for j in range(fw // 256):
            s = slice(j * 256, (j + 1) * 256)
            t = slice(y * fw + j * 256, y * fw + (j + 1) * 256)
            pre = dot(x, up_ref[y, :, s], 1, 0) + biases[y][:, s]
            phi = 0.5 + 0.5 * lax.erf(pre * (0.5**0.5))
            act_ref[:, t] = (pre * phi).astype(BF)
            slope_ref[:, t] = (phi + pre * (jnp.exp(-0.5 * pre * pre) * (2 * np.pi) ** -0.5)).astype(BF)


def product_kernel(info, a_ref, *rest):
    *w, out_ref, w_ref, sems = rest
    wait(load_weight(info, w, w_ref, sems))
    fw = w_ref.shape[2]
    out_ref[...] = (dot(a_ref[:, :fw], w_ref[0], 1, 1) + dot(a_ref[:, fw:], w_ref[1], 1, 1)).astype(out_ref.dtype)


def head_ones():
    a = lax.broadcasted_iota(jnp.int32, (CW, CW), 0) // (CW // PH)
    b = lax.broadcasted_iota(jnp.int32, (CW, CW), 1) // (CW // PH)
    return jnp.where(a == b, 1.0, 0.0)


def fdot(a, b, ca=1, cb=0):
    return lax.dot_general(a, b, (((ca,), (cb,)), ((), ())), precision=HIGHEST, preferred_element_type=F32)


def ln2_kernel(
    part_ref, got_ref, first_ref, aux_ref, wide_ref, narrow_ref, sw_ref, low_ref, n_ref, s_ref, st_ref, lg_ref, stat_ref
):
    feed = part_ref[...] + got_ref[...].astype(F32) + wide_ref[3:4]
    second, normed, scale = norm(first_ref[...] + feed, wide_ref[4:5], wide_ref[5:6])
    low = second.astype(BF)
    low_ref[...] = low
    n_ref[...] = normed
    s_ref[...] = scale
    student = dot(low, sw_ref[...], 1, 0) + narrow_ref[0:1]
    st_ref[...] = student
    live = live_rows(aux_ref)
    logit = fdot(student * narrow_ref[1:2], head_ones()) * (CW // PH) ** -0.5
    logit = jnp.where(live > 0.0, logit, NEGATIVE)
    lg_ref[...] = logit

    @pl.when(pl.program_id(0) == 0)
    def _():
        stat_ref[...] = jnp.zeros((8, 128), F32)
        stat_ref[0:1] = jnp.full((1, 128), NEGATIVE, F32)

    old = stat_ref[0:1]
    top = jnp.maximum(old, jnp.max(logit, axis=0, keepdims=True))
    shrink = jnp.exp(old - top)
    weight = jnp.where(live > 0.0, jnp.exp(logit - top), 0.0)
    stat_ref[0:1] = top
    stat_ref[1:2] = stat_ref[1:2] * shrink + jnp.sum(weight, axis=0, keepdims=True)
    stat_ref[2:3] = stat_ref[2:3] * shrink + jnp.sum(weight * student, axis=0, keepdims=True)
    stat_ref[3:4] += jnp.broadcast_to(square(live, feed), (1, 128))


def norm_back(up, normed, scale, gain):
    scaled = up * gain
    inner = scaled - jnp.mean(scaled, -1, keepdims=True) - normed * jnp.mean(scaled * normed, -1, keepdims=True)
    return inner * scale


def colsum(x):
    return jnp.sum(x, axis=0, keepdims=True)


def head_kernel(
    info,
    st_ref,
    lg_ref,
    low_ref,
    cot_ref,
    n_ref,
    s_ref,
    stat_ref,
    sib_ref,
    sq_ref,
    pooler_ref,
    class_ref,
    cb_ref,
    narrow_ref,
    sw_ref,
    wide_ref,
    dr2_ref,
    dffn_ref,
    gst_ref,
    gpool_ref,
    gclass_ref,
    rep_ref,
    vec_ref,
    nvec_ref,
    keep_ref,
):
    scale = (CW // PH) ** -0.5
    once = jnp.where(info[1] == 0, 1.0, 0.0)

    @pl.when(pl.program_id(0) == 0)
    def _():
        top, top2 = stat_ref[0:1], sib_ref[0:1]
        best = jnp.maximum(top, top2)
        fa, fb = jnp.exp(top - best), jnp.exp(top2 - best)
        whole = stat_ref[1:2] * fa + sib_ref[1:2] * fb
        pooled = (stat_ref[2:3] * fa + sib_ref[2:3] * fb) / whole
        pooled = jnp.broadcast_to(pooled, (8, CW))
        z = jnp.tanh(fdot(pooled, pooler_ref[...]) + narrow_ref[2:3])
        lane = lax.broadcasted_iota(jnp.int32, (8, 128), 1)
        row = lax.broadcasted_iota(jnp.int32, (8, 128), 0)
        logit = fdot(z, class_ref[...]) + cb_ref[...]
        masked = jnp.where(lane < CLASSES, logit, NEGATIVE)
        e = jnp.exp(masked - jnp.max(masked, axis=1, keepdims=True))
        dlogit = e / jnp.sum(e, axis=1, keepdims=True) - jnp.where(lane == info[3], 1.0, 0.0)
        only = jnp.where(row == 0, once, 0.0)
        gclass_ref[...] = fdot(z * only, dlogit, 0, 0)
        dz = fdot(dlogit, class_ref[...], 1, 1)
        dzp = dz * (1.0 - z * z)
        gpool_ref[...] = fdot(pooled * only, dzp, 0, 0)
        dpooled = fdot(dzp, pooler_ref[...], 1, 1)
        sq = jnp.where(lane[0:1] == 3, stat_ref[3:4] + sib_ref[3:4] * 0.0, sq_ref[...])
        sq = jnp.where(info[1] == 0, pltpu.roll(sq, 2 * CLASSES, 1), pltpu.roll(sq, 2 * CLASSES + 4, 1))
        rep = jnp.where(lane < CLASSES, logit, pltpu.roll(jnp.where(lane < CLASSES, dlogit, 0.0), CLASSES, 1)) * once
        rep_ref[...] = jnp.where(lane < 2 * CLASSES, rep, sq)
        nvec_ref[...] = jnp.zeros((8, CW), F32)
        nvec_ref[2:3] = dzp[0:1] * once
        vec_ref[...] = jnp.zeros((8, D), F32)
        gst_ref[...] = jnp.zeros((D, CW), F32)
        keep_ref[0:1] = best
        keep_ref[1:2] = whole
        keep_ref[2:3] = dpooled[0:1]
        keep_ref[3:4] = fdot(pooled * dpooled, head_ones())[0:1]

    student = st_ref[...]
    dp = keep_ref[2:3]
    logit = lg_ref[...]
    weight = jnp.where(logit > 0.5 * NEGATIVE, jnp.exp(logit - keep_ref[0:1]), 0.0) / keep_ref[1:2]
    dq = scale * weight * (fdot(student * dp, head_ones()) - keep_ref[3:4])
    dstudent = (weight * dp + dq * narrow_ref[1:2]).astype(BF)
    nvec_ref[0:1] += colsum(dstudent.astype(F32))
    nvec_ref[1:2] += colsum(dq * student)
    gst_ref[...] += dot(low_ref[...], dstudent, 0, 0)
    dsecond = dot(dstudent, sw_ref[...], 1, 1) + cot_ref[...].astype(F32)
    normed = n_ref[...]
    dr2 = norm_back(dsecond, normed, s_ref[...], wide_ref[4:5])
    dr2_ref[...] = dr2
    dffn_ref[...] = dr2.astype(BF)
    vec_ref[0:1] += colsum(dr2)
    vec_ref[1:2] += colsum(dsecond * normed)
    vec_ref[2:3] += colsum(dsecond)


def ffn_back_kernel(info, g_ref, slope_ref, *rest):
    *down, dpre_ref, ub_ref, w_ref, sems = rest
    copies = load_weight(info, down, w_ref, sems)
    fw = w_ref.shape[2]
    g = g_ref[...]
    ub_ref[...] = jnp.zeros(ub_ref.shape, F32)
    wait(copies)
    for y in range(2):
        for j in range(fw // 256):
            s = slice(j * 256, (j + 1) * 256)
            t = slice(y * fw + j * 256, y * fw + (j + 1) * 256)
            dpre = (dot(g, w_ref[y, :, s], 1, 0) * slope_ref[:, t].astype(F32)).astype(BF)
            dpre_ref[:, t] = dpre
            ub_ref[0:1, t] = colsum(dpre.astype(F32))


def ffn_grad_kernel(info, first, first2, dpre, dpre2, dffn, dffn2, act, act2, *rest):
    *outs, g_ref = rest
    fw = dpre.shape[1] // 2
    for k, (a0, a1, b0, b1) in enumerate(((first, first2, dpre, dpre2), (dffn, dffn2, act, act2))):
        for y in range(2):
            s = slice(y * fw, (y + 1) * fw)
            g = dot(a0[...], b0[:, s], 0, 0) + dot(a1[...], b1[:, s], 0, 0)
            store_grad(info, k, y, g, g_ref, outs)


def ln1_back_kernel(part_ref, got_ref, dr2_ref, n_ref, s_ref, wide_ref, dr1_ref, low_ref, vec_ref):
    start_sums(vec_ref)
    up = part_ref[...] + got_ref[...].astype(F32) + dr2_ref[...]
    normed = n_ref[...]
    dr1 = norm_back(up, normed, s_ref[...], wide_ref[1:2])
    dr1_ref[...] = dr1
    low_ref[...] = dr1.astype(BF)
    vec_ref[0:1] += colsum(dr1)
    vec_ref[1:2] += colsum(up * normed)
    vec_ref[2:3] += colsum(up)


def attn_bwd_kernel(nh, proj_ref, w_ref, aux_ref, ctx_ref, da_ref, db_ref, lse_ref, out_ref, sum_ref, do_ref, dqt_ref):
    n = proj_ref.shape[0]
    half = n // 2
    scale = HS**-0.5
    cols = slice(8 * HS, 12 * HS)
    for i, ref in enumerate((da_ref, db_ref)):
        do_ref[i * half : (i + 1) * half] = dot(ref[...], w_ref[:, cols], 1, 0).astype(BF)
    qb = [block(proj_ref, i) for i in (0, 1)]
    qt = [jnp.transpose(q.astype(F32)) * (scale * LOG2E) for q in qb]
    hi = [q.astype(BF) for q in qt]
    lo = [(q - h.astype(F32)).astype(BF) for q, h in zip(qt, hi)]
    kt = [jnp.transpose(block(proj_ref, i).astype(F32)).astype(BF) for i in (1, 2)]
    dob = [block(do_ref, i) for i in (0, 1)]
    dot_f = [jnp.transpose(d.astype(F32)) for d in dob]
    dot_b = [d.astype(BF) for d in dot_f]
    prod = [d * jnp.transpose(block(ctx_ref, i).astype(F32)) for i, d in enumerate(dot_f)]
    lane = lax.broadcasted_iota(jnp.int32, (n, 128), 1)
    row = lax.broadcasted_iota(jnp.int32, (128, QB), 0)
    zero = jnp.zeros((64, QB), BF)
    empty = jnp.zeros((n, 128), BF)
    dqt_ref[...] = jnp.zeros(dqt_ref.shape, F32)
    dk, dv = [], []
    for h in range(nh):
        kb, kh = ((1, 1), (2, 0), (2, 1))[h]
        i, ih = h // 2, h % 2
        vi, vh = ((3, 0), (3, 1), (4, 0))[h]
        oi, oh = ((0, 1), (1, 0), (1, 1))[h]
        lhs = jnp.concatenate([doubled(block(proj_ref, kb), kh), aux_ref[...]], axis=1)
        lhs_v = jnp.concatenate([block(proj_ref, vi), aux_ref[...]], axis=1)
        r = slice(64 * ih, 64 * ih + 64)
        ro = slice(64 * oh, 64 * oh + 64)
        rk = slice(64 * kh, 64 * kh + 64)
        qm = jnp.where((lane < 64) == (ih == 0), qb[i], empty)
        dom = jnp.where((lane < 64) == (oh == 0), dob[oi], empty)
        dsum = jnp.sum(prod[oi][ro], axis=0, keepdims=True)
        l1, l2, l3 = split3(-lse_ref[h : h + 1, :])
        d1, d2, d3 = split3(-dsum)
        dkh = jnp.zeros((n, 128), F32)
        dvh = jnp.zeros((n, 128), F32)
        for b in range(n // QB):
            s = slice(b * QB, b * QB + QB)

            def pieces(first, x1, x2, x3):
                z = jnp.where(row == 1, x1[:, s].astype(F32), jnp.where(row == 0, first, 0.0))
                z = jnp.where(row == 2, x2[:, s].astype(F32), z)
                return jnp.where(row == 3, x3[:, s].astype(F32), z).astype(BF)

            rhs = jnp.concatenate([hi[i][r, s], lo[i][r, s], pieces(1.0, l1, l2, l3)], axis=0)
            p = jnp.exp2(dot(lhs, rhs, 1, 0))
            g = dot_b[oi][ro, s]
            part = [g, zero] if vh == 0 else [zero, g]
            rhs_v = jnp.concatenate(part + [pieces(0.0, d1, d2, d3)], axis=0)
            ds = (p * dot(lhs_v, rhs_v, 1, 0)).astype(BF)
            dvh = dvh + dot(p.astype(BF), dom[s], 1, 0)
            dkh = dkh + dot(ds, qm[s], 1, 0)
            dqt_ref[64 * h : 64 * h + 64, s] = dot(kt[kb - 1][rk], ds, 1, 0)
        dk.append(dkh * scale)
        dv.append(dvh)

    def put(i, x):
        out_ref[:, 128 * i : 128 * i + 128] = x.astype(BF)
        sum_ref[:, 128 * i : 128 * i + 128] = jnp.broadcast_to(colsum(x.astype(BF).astype(F32)), (8, 128))

    left = lane < 64
    put(0, jnp.transpose(dqt_ref[0:128] * scale))
    put(1, jnp.where(left, jnp.transpose(dqt_ref[128:256] * scale), swap64(dk[0])))
    put(2, jnp.where(left, swap64(dk[1]), swap64(dk[2])))
    put(3, jnp.where(left, swap64(dv[0]), swap64(dv[1])))
    put(4, jnp.where(left, swap64(dv[2]), 0.0))


def attn_bwd(nh, proj, w, aux, ctx, da, db, lse):
    n = proj.shape[0]
    return call(
        functools.partial(attn_bwd_kernel, nh),
        [sds((n, 10 * HS), BF), sds((8, 10 * HS))],
        [proj, w, aux, ctx, da, db, lse],
        None,
        [pltpu.VMEM((n, 4 * HS), BF), pltpu.VMEM((4 * HS, n), F32)],
        "attn_bwd",
        flops=11_000_000_000,
    )


def token_grad_kernel(g0_ref, g1_ref, w0_ref, w1_ref, dr1_ref, send_ref, own_ref):
    n = g0_ref.shape[0]
    half = n // 2
    cols = slice(0, 10 * HS)
    for out_ref, s in ((send_ref, slice(half, n)), (own_ref, slice(0, half))):
        part = dot(g0_ref[s], w0_ref[:, cols], 1, 1) + dot(g1_ref[s], w1_ref[:, cols], 1, 1)
        if out_ref is own_ref:
            part = part + dr1_ref[...]
        out_ref[...] = part.astype(out_ref.dtype)


def qkv_grad_kernel(nh, info, x0, x1, g_in, da, db, ctx_ref, sum_ref, *rest):
    *outs, g_ref, t_ref = rest
    half = x0.shape[0]
    g = dot(x0[...], g_in[:half], 0, 0) + dot(x1[...], g_in[half:], 0, 0)
    o = dot(da[...], ctx_ref[:half], 0, 0) + dot(db[...], ctx_ref[half:], 0, 0)
    g = jnp.concatenate([g[:, : 8 * HS], g[:, 8 * HS :] + o[:, : 2 * HS], o[:, 2 * HS :]], axis=1)
    store_grad(info, 0, 0, g, g_ref, outs)
    if len(outs) == 2:
        nz = outs[0].shape[1]
        rows = D // (2 * nz)
        piece = HS // nz
        zero = jnp.zeros((1, 128 - nh * piece), F32)
        for a in range(2 * nz):
            base = (a % nz) * piece + (a // nz) * 2 * nh * HS
            cuts = [sum_ref[0:1, base + h * HS : base + h * HS + piece] for h in range(nh)]
            t_ref[a : a + 1] = jnp.concatenate([*cuts, zero], axis=1)
        for z in range(nz):
            for x in range(2):
                outs[x][0, z, rows:] = jnp.zeros((outs[x].shape[2] - rows, D), BF)
                row = t_ref[pl.ds(info[0] ^ (2 * z + x), 1), :]
                outs[x][0, z, rows : rows + 8, :128] = jnp.broadcast_to(row, (8, 128)).astype(BF)


def place_kernel(info, a_ref, b_ref, c_ref, d_ref, out_ref):
    c, y = info[1], info[2]
    out_ref[0, y, c] = a_ref[0]
    out_ref[0, 1 - y, c] = b_ref[0]
    out_ref[0, y, 1 - c] = c_ref[0]
    out_ref[0, 1 - y, 1 - c] = d_ref[0]


def lanes(x):
    x = x.reshape(1, -1) if x.ndim == 1 else x
    return jnp.pad(x, ((0, 0), (0, 128 - x.shape[1])))


def unpack_kernel(sizes, in_ref, sw_ref, pooler_ref, class_ref, wide_ref, narrow_ref, bias_ref):
    rows, cr, nh, nr = sizes
    nd = in_ref.shape[0]
    blocks = [in_ref[d].astype(F32) for d in range(nd)]
    at = rows + 2 * cr

    def joined(first, count, width):
        return jnp.concatenate([b[first : first + count, :width] for b in blocks], axis=1)

    sw_ref[...] = jnp.concatenate([b[:rows] for b in blocks], axis=0).astype(BF)
    pooler_ref[...] = jnp.concatenate([b[rows : rows + cr] for b in blocks], axis=0)
    class_ref[...] = jnp.concatenate([b[rows + cr : at] for b in blocks], axis=0)
    wide_ref[...] = jnp.zeros(wide_ref.shape, F32)
    wide_ref[0:6] = joined(at, 6, rows)
    narrow_ref[...] = jnp.zeros(narrow_ref.shape, F32)
    narrow_ref[0:3] = joined(at + 6, 3, cr)
    bias_ref[...] = jnp.zeros(bias_ref.shape, F32)
    bias_ref[0:nh, :] = joined(at + 9, nh, 2 * HS // nd)
    bias_ref[nh : nh + nr, :HS] = joined(at + 9 + nh, nr, HS // nd)


def pack_grads_kernel(sizes, info, gst, gpool, gclass, v1, v2, nv, ub0, ub1, rep, out_ref):
    rows, cr, nh, nr = sizes
    nd = out_ref.shape[0]
    fw = nr * HS
    me = info[2] * 2 + info[1]
    ub = ub0[0:1] + ub1[0:1]
    pair = [
        jnp.concatenate([ub[:, y * fw + r * HS : y * fw + (r + 1) * HS] for r in range(nr)], axis=0) for y in range(2)
    ]
    quads = jnp.concatenate(
        [jnp.where(me == q, pair[0], jnp.where((me ^ 2) == q, pair[1], 0.0)) for q in range(4)], axis=0
    )
    wide = jnp.concatenate([v1[0:1], v1[1:2], v1[2:3], v2[0:1], v2[1:2], v2[2:3]], axis=0)

    def wider(x):
        return jnp.concatenate([x, jnp.zeros((x.shape[0], 128 - x.shape[1]), F32)], axis=1)

    total = 2 * nd
    row = lax.broadcasted_iota(jnp.int32, (total, 128), 0)
    high = rep[0:1].astype(BF).astype(F32)
    mine = row == 2 * info[0] + info[2]
    table = [jnp.where(mine, high, 0.0), jnp.where(mine, rep[0:1] - high, 0.0)]
    hs = HS // nd
    for d in range(nd):
        parts = [
            gst[d * rows : (d + 1) * rows],
            gpool[d * cr : (d + 1) * cr],
            gclass[d * cr : (d + 1) * cr],
            wider(wide[:, d * rows : (d + 1) * rows]),
            wider(nv[0:3, d * cr : (d + 1) * cr]),
            wider(quads[:, d * hs : (d + 1) * hs]),
            *table,
        ]
        parts = jnp.concatenate(parts, axis=0)
        out_ref[d, : parts.shape[0]] = parts
        if parts.shape[0] < out_ref.shape[1]:
            out_ref[d, parts.shape[0] :] = jnp.zeros((out_ref.shape[1] - parts.shape[0], 128), F32)


def body(
    hidden_in,
    cotangent,
    lengths,
    labels,
    qkv_weight,
    qv_bias,
    out_weight,
    out_bias,
    norm1_gain,
    norm1_bias,
    up_weight,
    up_bias,
    down_weight,
    down_bias,
    norm2_gain,
    norm2_bias,
    student_weight,
    student_bias,
    pool_query,
    pooler_weight,
    pooler_bias,
    class_weight,
    class_bias,
):
    nd = lax.axis_size("dp")
    me = lax.axis_index("dp")
    m = lax.axis_index("mp")
    c, y = m % 2, m // 2
    total, pd, _ = hidden_in.shape
    assert total == 2 * nd and lax.axis_size("mp") == 4
    hp = pd // 2
    half = nd * hp
    rows, cr = D // nd, CW // nd
    nh, nr = qv_bias.shape[0], up_bias.shape[0]
    hw, fw = nh * HS, nr * HS
    fast = rows % 16 == 0 and len(bit_groups(nd)) == 1
    sizes = (rows, cr, nh, nr)
    seq = 2 * me + y
    length = lengths[seq]
    info = jnp.stack([me, c, y, labels[seq]]).astype(jnp.int32)

    def deal(x):
        x = x.reshape(nd, 2, 2, hp, D)
        x = lax.dynamic_slice(x, (0, y, c, 0, 0), (nd, 1, 1, hp, D)).reshape(nd, hp, D)
        return lax.all_to_all(x, "dp", 0, 0, tiled=True).reshape(half, D)

    def undeal(x):
        return lax.all_to_all(x.reshape(nd, hp, D), "dp", 0, 0, tiled=True)

    def place(a, b):
        one = pl.BlockSpec((1, hp, D), lambda d: (d, 0, 0))
        out = pl.pallas_call(
            place_kernel,
            grid=(nd,),
            in_specs=[SMEM] + [one] * 4,
            out_specs=pl.BlockSpec((1, 2, 2, hp, D), lambda d: (d, 0, 0, 0, 0)),
            out_shape=sds((nd, 2, 2, hp, D), BF),
            cost_estimate=cost(6_000_000),
            compiler_params=room(8),
            name="place",
        )(info, a, b, hop(a, 0, 1), hop(b, 0, 1))
        return out.reshape(total, pd, D)

    qo = jnp.concatenate([jnp.transpose(qkv_weight, (1, 0, 2)).reshape(rows, 3 * hw), out_weight.T], axis=1)
    if fast:
        row = jnp.pad(qv_bias.reshape(1, -1), ((0, 7), (0, D - qv_bias.size)))
        qo = jnp.concatenate([qo, row], axis=0)
    qo_line, _ = gather_lines(qo[None])
    tokens = deal(after(hidden_in, qo_line))
    w_qo = gather_planes(qo_line, fast)
    w_qo = (w_qo[:2], w_qo[2:]) if fast else (w_qo[:1], w_qo[1:])
    up_pack = up_weight
    if fast:
        row = jnp.pad(up_bias.reshape(1, -1), ((0, 7), (0, D - up_bias.size)))
        up_pack = jnp.concatenate([up_weight, row], axis=0)
    up_line, up_got = gather_lines(after(up_pack, qo_line)[None])
    w_up = gather_planes(up_line, fast)
    down_line, down_got = gather_lines(after(down_weight.T, up_line)[None])
    small = jnp.concatenate(
        [student_weight, pooler_weight]
        + [
            lanes(v)
            for v in (
                class_weight,
                out_bias,
                norm1_gain,
                norm1_bias,
                down_bias,
                norm2_gain,
                norm2_bias,
                student_bias,
                pool_query,
                pooler_bias,
                qv_bias,
                up_bias,
            )
        ],
        axis=0,
    )
    small = jnp.pad(small, ((0, -small.shape[0] % 16), (0, 0)))
    class_b = lanes(class_bias.astype(F32))
    cot = deal(cotangent)

    index = jnp.arange(half, dtype=jnp.int32)
    position = (index // hp) * pd + index % hp
    position = jnp.concatenate([position + c * hp, position + (1 - c) * hp])
    col = jnp.arange(128, dtype=jnp.int32)[None, :]
    aux = jnp.where(
        col == 0, jnp.where(position < length, 0.0, NEGATIVE)[:, None], jnp.where(col <= 3, 1.0, 0.0)
    ).astype(BF)
    aux_own = aux[:half]

    sib = hop(after(tokens, w_qo, up_got), 0, 1)
    n = 2 * half
    biases = [aux, aux]
    if not fast:
        piece = jnp.broadcast_to(qv_bias[None], (nd, *qv_bias.shape))
        piece = lax.all_to_all(piece, "dp", 0, 0, tiled=True)
        piece = jnp.transpose(piece, (1, 0, 2)).reshape(nh, 2 * HS)
        piece = jnp.pad(piece, ((0, 16 - nh), (0, 0)))
        biases = [piece, hop(piece, 0, 2)]
    proj0, w0, ctx0, lse0 = attn_fwd(nh, info, tokens, sib, biases[0], aux, w_qo[0])
    small = lax.all_to_all(jnp.broadcast_to(after(small, ctx0)[None], (nd, *small.shape)), "dp", 0, 0, tiled=True)
    student_w, pooler_f, class_f, wide, narrow, bias_near = call(
        functools.partial(unpack_kernel, sizes),
        [sds((D, CW), BF), sds((CW, CW)), sds((CW, CW)), sds((8, D)), sds((8, CW)), sds((16, 128))],
        [small],
        name="unpack",
    )
    bias_near = bias_near.astype(BF)
    bias_far = bias_near if fast else hop(bias_near, 0, 2)
    proj1, w1, ctx1, lse1 = attn_fwd(nh, info, tokens, sib, biases[1], after(aux, down_got, ctx0), w_qo[1])
    w_down = gather_planes(after(down_line, ctx0), fast)

    if fast:
        ctx1 = after(ctx1, w_up, w_down[1:3], student_w)

    def out(first, kind):
        return call(
            functools.partial(out_kernel, first), [sds((half, D), kind)], [ctx0, ctx1, w0, w1], name="out"
        )[0]

    att_got = hop(out(half, BF), 0, 1)
    att_part = out(0, F32)
    first, first_low, n1, s1, sq1 = by_rows(
        ln1_kernel,
        [sds((half, D)), sds((half, D), BF), sds((half, D)), sds((half, 1))],
        [sds((1, 128))],
        [att_part, att_got, tokens, aux_own],
        [wide],
        name="ln1",
    )
    first_sib = hop(first_low, 0, 1)

    def ffn_up(x):
        return call(
            functools.partial(ffn_up_kernel, nh, nr),
            [sds((half, 2 * fw), BF), sds((half, 2 * fw), BF)],
            [info, x, bias_near, bias_far, *w_up],
            [SMEM] + [None] * 3 + [ANY] * len(w_up),
            weight_scratch(w_up)
            + [pltpu.VMEM((max(nd, 8), 8, D), BF)] * 2
            + [pltpu.SemaphoreType.DMA((nd,))],
            "ffn_up",
        )

    def product(a, w, kind):
        return call(
            product_kernel,
            [sds((half, D), kind)],
            [info, a, *w],
            [SMEM, None] + [ANY] * len(w),
            weight_scratch(w),
            "product",
        )[0]

    act, slope = ffn_up(first_low)
    act_sib, slope_sib = ffn_up(after(first_sib, act))
    ffn_got = hop(product(act_sib, w_down, BF), 0, 1)
    ffn_part = product(act, w_down, F32)
    second_low, n2, s2, student, pool_logit, stat = by_rows(
        ln2_kernel,
        [sds((half, D), BF), sds((half, D)), sds((half, 1)), sds((half, CW)), sds((half, CW))],
        [sds((8, 128))],
        [ffn_part, ffn_got, after(first, cot), aux_own],
        [wide, narrow, student_w],
        name="ln2",
    )
    hidden_a = undeal(second_low)
    hidden_b = hop(hidden_a, 0, 2)

    dr2, dffn, g_st, g_pool, g_class, report, vec2, nvec, _ = by_rows(
        head_kernel,
        [sds((half, D)), sds((half, D), BF)],
        [
            sds((D, CW)),
            sds((CW, CW)),
            sds((CW, CW)),
            sds((8, 128)),
            sds((8, D)),
            sds((8, CW)),
            sds((8, 128)),
        ],
        [student, pool_logit, second_low, cot, n2, s2],
        [stat, hop(stat, 0, 1), sq1, pooler_f, class_f, class_b, narrow, student_w, wide],
        info,
        "head",
    )
    dffn_sib = hop(dffn, 0, 1)

    def ffn_back(g, s):
        return call(
            ffn_back_kernel,
            [sds((half, 2 * fw), BF), sds((8, 2 * fw))],
            [info, g, s, *w_down],
            [SMEM, None, None] + [ANY] * len(w_down),
            weight_scratch(w_down),
            "ffn_back",
        )

    dpre, ub0 = ffn_back(dffn, slope)
    dpre_sib, ub1 = ffn_back(after(dffn_sib, dpre, hidden_a), slope_sib)
    dfirst_got = hop(product(dpre_sib, w_up, BF), 0, 1)
    dfirst_part = product(dpre, w_up, F32)
    f_grads = call(
        ffn_grad_kernel,
        grad_outs(2, 2, nd, rows, fast),
        [info, first_low, first_sib, dpre, dpre_sib, dffn, dffn_sib, act, act_sib],
        [SMEM] + [None] * 8,
        [pltpu.VMEM((D, D), F32)],
        "ffn_grad",
    )
    dr1, dattn, vec1 = by_rows(
        ln1_back_kernel,
        [sds((half, D)), sds((half, D), BF)],
        [sds((8, D))],
        [dfirst_part, dfirst_got, after(dr2, hidden_b), n1, s1],
        [wide],
        name="ln1_back",
    )
    dattn_sib = hop(dattn, 0, 1)
    dattn_sib = after(dattn_sib, f_grads, hidden_b)
    f_parts = sum_planes(f_grads)
    count = rows + 2 * cr + 9 + 4 * nr + 2 * total
    (small_g,) = call(
        functools.partial(pack_grads_kernel, sizes),
        [sds((nd, count + -count % 16, 128))],
        [info, g_st, g_pool, g_class, vec1, vec2, nvec, ub0, ub1, report],
        [SMEM] + [None] * 9,
        name="pack",
    )
    small_g = small_g + hop(small_g.astype(BF), 0, 1).astype(F32)
    small_y = small_g + hop(small_g.astype(BF), 0, 2).astype(F32)


    def qkv_grad(g, ctx, sums):
        return call(
            functools.partial(qkv_grad_kernel, nh),
            grad_outs(1, 1, nd, rows, fast, 8),
            [info, tokens, sib, g, dattn, dattn_sib, ctx, sums],
            [SMEM] + [None] * 7,
            [pltpu.VMEM((D, D), F32), pltpu.VMEM((max(8, nd), 128), F32)],
            "qkv_grad",
        )

    g1, g1_sum = attn_bwd(nh, proj1, w1, aux, ctx1, dattn, after(dattn_sib, small_y), lse1)
    far_grad = qkv_grad(g1, ctx1, g1_sum)
    if fast:
        far_got = hop(far_grad[1], 1, 0)
    g0, g0_sum = attn_bwd(
        nh, proj0, w0, aux, ctx0, dattn, after(dattn_sib, g1, far_grad), lse0
    )
    if fast:
        g0, f_parts[1], f_parts[2], far_got = lax.optimization_barrier((g0, f_parts[1], f_parts[2], far_got))
        far_part = (far_grad[0].astype(F32) + far_got.astype(F32)).astype(BF)
    tok_send, tok_own = call(
        token_grad_kernel, [sds((half, D), BF), sds((half, D))], [g0, g1, w0, w1, dr1], name="token_grad"
    )
    near_grad = qkv_grad(g0, ctx0, g0_sum)
    tok_sum = after((tok_own + hop(tok_send, 0, 1).astype(F32)).astype(BF), near_grad)
    input_a = undeal(tok_sum)
    f_sums = sum_blocks(f_parts)
    small_g = lax.all_to_all(after(small_y.astype(BF), input_a), "dp", 0, 0, tiled=True).astype(F32).sum(0)
    hidden_out = place(after(hidden_a, f_sums), hidden_b)
    input_grad = place(input_a, hop(after(input_a, hidden_out), 0, 2))
    f_sum = finish_lines(f_sums) if fast else sum_lines(f_parts)
    up_sum, down_sum = f_sum
    if fast:
        qo_own = (near_grad[0], hop(near_grad[1], 1, 0), hop(far_part, 0, 2))
        qo_own = (after(qo_own[0], f_sum), *qo_own[1:])
        qo_sum = finish_lines(sum_blocks(qo_own))[0]
    else:
        qo_sum = sum_lines([*near_grad, *far_grad])[0]

    width = 2 * HS // nd
    if fast:
        g_qv = qo_sum[rows, : nh * width].reshape(nh, width)
        qo_sum = qo_sum[:rows]
    else:
        g_qv = [
            jnp.concatenate([g[0, :hw].reshape(nh, HS), g[0, 2 * hw : 3 * hw].reshape(nh, HS)], axis=1)
            for g in (g0_sum, g1_sum)
        ]
        g_qv = g_qv[0] + hop(g_qv[1], 0, 2)
        bit = 1
        while bit < nd:
            g_qv = g_qv + hop(g_qv, bit, 0)
            bit *= 2
        g_qv = lax.dynamic_slice(g_qv, (0, width * me), (nh, width))

    at = rows + 2 * cr + 9 + 4 * nr
    table = small_g[at : at + total] + small_g[at + total : at + 2 * total]
    logit_all = table[:, :CLASSES]
    class_bias_grad = jnp.sum(table[:, CLASSES : 2 * CLASSES], 0)
    squares = jnp.sum(table[:, 2 * CLASSES : 2 * CLASSES + 8], 0).reshape(2, 4).sum(0)
    rms = jnp.sqrt(squares / (jnp.sum(lengths).astype(F32) * D))

    at = rows + 2 * cr
    g_wide = small_g[at : at + 6, :rows]
    g_narrow = small_g[at + 6 : at + 9, :cr]
    g_ub = lax.dynamic_slice(small_g, (at + 9 + nr * m, 0), (nr, HS // nd))
    return (
        hidden_out,
        logit_all,
        input_grad,
        jnp.transpose(qo_sum[:, : 3 * hw].reshape(rows, 3, hw), (1, 0, 2)),
        g_qv,
        qo_sum[:, 3 * hw :].T,
        g_wide[0],
        g_wide[1],
        g_wide[2],
        up_sum,
        g_ub,
        down_sum.T,
        g_wide[3],
        g_wide[4],
        g_wide[5],
        small_g[:rows],
        g_narrow[0],
        g_narrow[1],
        small_g[rows : rows + cr],
        g_narrow[2],
        small_g[rows + cr : at, :CLASSES],
        class_bias_grad,
        rms,
    )


def solution(mesh):
    rows = P(None, "dp", None)
    vec = P("dp")
    return jax.shard_map(
        body,
        mesh=mesh,
        in_specs=(
            rows,
            rows,
            P(),
            P(),
            P(None, "dp", "mp"),
            P("mp", "dp"),
            P("mp", "dp"),
            vec,
            vec,
            vec,
            P("dp", "mp"),
            P("mp", "dp"),
            P("mp", "dp"),
            vec,
            vec,
            vec,
            P("dp", None),
            vec,
            vec,
            P("dp", None),
            vec,
            P("dp", None),
            P(),
        ),
        out_specs=(
            rows,
            P(),
            rows,
            P(None, "dp", "mp"),
            P("mp", "dp"),
            P("mp", "dp"),
            vec,
            vec,
            vec,
            P("dp", "mp"),
            P("mp", "dp"),
            P("mp", "dp"),
            vec,
            vec,
            vec,
            P("dp", None),
            vec,
            vec,
            P("dp", None),
            vec,
            P("dp", None),
            P(),
            P(),
        ),
        check_vma=False,
    )
```

time: 677 us -> 443 us (0.65)
  local copies, waits for them, and re-layouts: 201 us -> 71.4 us
  Pallas kernels: 38.6 us -> 130 us
  other arithmetic: 95 us -> 16.2 us
  waiting for transfers between devices: 191 us -> 122 us
  matrix products: 60.2 us -> 0 us
  starting transfers between devices: 75.7 us -> 94.4 us
    pallas_call x2 -> x28, Pallas kernels: 38.6 us -> 130 us  [the longest x22 106 us: call(): pl.pallas_call(kernel, in_specs=specs, out_specs=[pl.BlockSpec(memory_spa...]
    ppermute x40 -> x47, waiting for transfers between devices: 191 us -> 122 us  [hop(): return lax.ppermute(x, AXES, pairs)]
    dot_general x21 -> x0, matrix products: 60.2 us -> none  [the longest x15 56.9 us: dot(): lax.dot_general(a, b, (((ca,), (cb,)), ((), ())), preferred_element_type=...]
    unnamed x246 -> x279, local copies, waits for them, and re-layouts: 20.8 us -> 59.7 us
    concatenate x12 -> x1, local copies, waits for them, and re-layouts: 36.2 us -> 0.21 us  [body(): jnp.concatenate([student_weight, pooler_weight] + [lanes(v) for v in (cla...]
    slice x28 -> x7, local copies, waits for them, and re-layouts: 30.9 us -> 1.44 us  [the longest x1 0.62 us: body(): small_g[:rows]]
    squeeze x14 -> x0, local copies, waits for them, and re-layouts: 25.4 us -> none  [the longest x2 12.3 us: body(): down_t = jnp.concatenate([f_all[i, :, hw + fw:] for i in range(4)], axis=1)]
    gather x7 -> x0, local copies, waits for them, and re-layouts: 21.7 us -> none  [relative(): return jnp.take(x, jnp.arange(x.shape[0], dtype=jnp.int32) ^ me, axis=0)]
  transfers between devices with their start and end apart: 47 -> 53, of which waited for: 14 -> 20; matrix products, arithmetic and copies ran while one was open for 47% -> 6% of each run, Pallas kernels for 6% -> 26%
where the time goes in v2:
time: 443 us; the launch traced here: 437 us
  Pallas kernels  130 us (29%)
  waiting for transfers between devices  122 us (28%)
  starting transfers between devices  94.4 us (21%)
  local copies, waits for them, and re-layouts  71.4 us (16%)
  other arithmetic  16.2 us (4%)
    ppermute x47, waiting for transfers between devices, hop(): return lax.ppermute(x, AXES, pairs)  122 us
    pallas_call x22, Pallas kernels, call(): pl.pallas_call(kernel, in_specs=specs, out_specs=[pl.BlockSpec(memory_spa...  106 us
    unnamed x279, local copies, waits for them, and re-layouts  59.7 us
    ppermute x47, starting transfers between devices, hop(): return lax.ppermute(x, AXES, pairs)  55.7 us
    all_to_all x2, starting transfers between devices, deal(): return lax.all_to_all(x, 'dp', 0, 0, tiled=True).reshape(half, D)  21 us
    pallas_call x4, Pallas kernels, by_rows(): pl.pallas_call(kernel, grid=(n // RB,), in_specs=[SMEM] * len(head) + [cu...  14.6 us
    pallas_call x2, Pallas kernels, place(): pl.pallas_call(place_kernel, grid=(nd,), in_specs=[SMEM] + [one] * 4, out...  9.4 us
    all_to_all x2, starting transfers between devices, undeal(): return lax.all_to_all(x.reshape(nd, hp, D), 'dp', 0, 0, tiled=True)  9.23 us
  transfers between devices with their start and end apart: 53, of which 20 were waited for; matrix products, arithmetic and copies ran while one was open for 6% of the time, Pallas kernels for 26%

profile of v2, /device:TPU:0, one launch (start us, length us, event | category | flops | bytes accessed | tf_op | source)
XLA Modules:
  0.0 436.8 jit_solution(17173083752660176332)
XLA Ops:
  4.5 5.0 %collective-permute-start.2 = (bf16[1,1,104,768]{3,2,1,0:T(8,128)(2,1)}, bf16[1,1,104,768]{3,2,1,0:T(8,128)(2,1)S(1)}, u32[]{:S(2)}, u32[]{:S(2)}) collective-permute-start(bf16[1,1,104,768]{3,2,1,0:T(8,128)(2,1)} %get-tuple-element.252), channel_id=1, source_target_pairs={{0,24},{1,25},{2,26},{3,27},{4,28},{5,29},{6,30},{7,31},{8,16},{9,... | collective-permute-start | bytes 479240 | tf_op jit(solution)/shard_map/ppermute | solution.py:36
  10.1 4.6 %collective-permute-done.2 = bf16[1,1,104,768]{3,2,1,0:T(8,128)(2,1)S(1)} collective-permute-done((bf16[1,1,104,768]{3,2,1,0:T(8,128)(2,1)}, bf16[1,1,104,768]{3,2,1,0:T(8,128)(2,1)S(1)}, u32[]{:S(2)}, u32[]{:S(2)}) %collective-permute-start.2) | collective-permute-done | bytes 159776 | tf_op jit(solution)/shard_map/ppermute | solution.py:36
  14.7 3.7 collective-permute-done
  18.5 4.9 %collective-permute-done.1 = bf16[1,1,104,768]{3,2,1,0:T(8,128)(2,1)} collective-permute-done((bf16[1,1,104,768]{3,2,1,0:T(8,128)(2,1)}, bf16[1,1,104,768]{3,2,1,0:T(8,128)(2,1)}, u32[]{:S(2)}, u32[]{:S(2)}) %collective-permute-start.1) | collective-permute-done | bytes 159776 | tf_op jit(solution)/shard_map/ppermute | solution.py:36
  23.4 1.9 maximum_bitcast_fusion.rest_0_
  26.4 4.8 %all-to-all-start = ((bf16[8,64,768]{2,1,0:T(8,128)(2,1)}), bf16[8,64,768]{2,1,0:T(8,128)(2,1)S(1)}, u32[]{:S(2)}, u32[]{:S(2)}) async-start(bf16[8,64,768]{2,1,0:T(8,128)(2,1)} %dynamic-slice_bitcast_fusion.1), calls=%async_computation | async-start | bytes 1572864 | tf_op jit(solution)/shard_map/all_to_all | solution.py:903
  31.2 2.0 collective-permute-start.3
  33.2 1.5 collective-permute-start.4
  35.0 2.0 collective-permute-start.6
  37.0 2.4 collective-permute-start.7
  39.4 9.0 %collective-permute-done.6 = bf16[1,1,104,768]{3,2,1,0:T(8,128)(2,1)S(1)} collective-permute-done((bf16[1,1,104,768]{3,2,1,0:T(8,128)(2,1)S(1)}, bf16[1,1,104,768]{3,2,1,0:T(8,128)(2,1)S(1)}, u32[]{:S(2)}, u32[]{:S(2)}) %collective-permute-start.6) | collective-permute-done | bytes 159776 | tf_op jit(solution)/shard_map/ppermute | solution.py:36
  48.4 4.1 collective-permute-start.8
  53.1 9.5 %collective-permute-done.7 = bf16[1,1,104,768]{3,2,1,0:T(8,128)(2,1)S(1)} collective-permute-done((bf16[1,1,104,768]{3,2,1,0:T(8,128)(2,1)S(1)}, bf16[1,1,104,768]{3,2,1,0:T(8,128)(2,1)S(1)}, u32[]{:S(2)}, u32[]{:S(2)}) %collective-permute-start.7) | collective-permute-done | bytes 159776 | tf_op jit(solution)/shard_map/ppermute | solution.py:36
  63.4 6.0 %collective-permute-done.5.rest_1_ = bf16[1,4,104,768]{3,2,1,0:T(8,128)(2,1)S(1)} collective-permute-done((bf16[1,4,104,768]{3,2,1,0:T(8,128)(2,1)S(1)}, bf16[1,4,104,768]{3,2,1,0:T(8,128)(2,1)S(1)}, u32[]{:S(2)}, u32[]{:S(2)}) %collective-permute-start.5) | collective-permute-done | bytes 639008 | tf_op jit(solution)/shard_map/ppermute | solution.py:36
  71.1 1.5 collective-permute-start.10
  72.6 2.4 collective-permute-start.11
  78.0 2.3 collective-permute-done.10
  80.8 6.0 %collective-permute-done.11 = bf16[1,1,96,768]{3,2,1,0:T(8,128)(2,1)S(1)} collective-permute-done((bf16[1,1,96,768]{3,2,1,0:T(8,128)(2,1)}, bf16[1,1,96,768]{3,2,1,0:T(8,128)(2,1)S(1)}, u32[]{:S(2)}, u32[]{:S(2)}) %collective-permute-start.11) | collective-permute-done | bytes 147488 | tf_op jit(solution)/shard_map/ppermute | solution.py:36
  92.1 12.5 %attn_fwd.2 = (bf16[1024,640]{1,0:T(8,128)(2,1)S(1)}, bf16[768,768]{1,0:T(8,128)(2,1)S(1)}, bf16[1024,256]{1,0:T(8,128)(2,1)S(1)}, f32[8,1024]{1,0:T(8,128)S(1)}) custom-call(s32[4]{0:T(128)S(1)} %pad_add_fusion.info, bf16[512,768]{1,0:T(8,128)(2,1)S(1)} %bitcast.87, bf16[512,768]{1,0:T(8,128)(2,1)S(1)} %copy-done.32, ...), custom_call_target="tpu_custom_call" | custom-call | flops 11000000512 | bytes 6422544 | tf_op jit(solution)/shard_map/attn_fwd/pallas_call | solution.py:124
  110.3 4.0 all-to-all-start.1
  118.5 12.4 %attn_fwd.3 = (bf16[1024,640]{1,0:T(8,128)(2,1)S(1)}, bf16[768,768]{1,0:T(8,128)(2,1)S(1)}, bf16[1024,256]{1,0:T(8,128)(2,1)S(1)}, f32[8,1024]{1,0:T(8,128)S(1)}) custom-call(s32[4]{0:T(128)S(1)} %pad_add_fusion.info, bf16[512,768]{1,0:T(8,128)(2,1)S(1)} %bitcast.88, bf16[512,768]{1,0:T(8,128)(2,1)S(1)} %copy-done.33, bf16[1024,128]{1,0:T(8,128)(2,1)S(1)} %copy-done.70, ...), custom_call_target="tpu_custom_call" | custom-call | flops 11000000512 | bytes 6422544 | tf_op jit(solution)/shard_map/attn_fwd/pallas_call | solution.py:124
  143.5 2.4 ln1.1
  149.4 2.1 dynamic-slice_bitcast_fusion
  151.5 16.1 %all-to-all-start.2 = ((bf16[8,64,768]{2,1,0:T(8,128)(2,1)}), bf16[8,64,768]{2,1,0:T(8,128)(2,1)}, u32[]{:S(2)}, u32[]{:S(2)}) async-start(bf16[8,64,768]{2,1,0:T(8,128)(2,1)} %dynamic-slice_bitcast_fusion), calls=%async_computation.2 | async-start | bytes 1572864 | tf_op jit(solution)/shard_map/all_to_all | solution.py:903
  167.6 3.0 collective-permute-start.19
  170.7 6.9 %ffn_up.2 = (bf16[512,1536]{1,0:T(8,128)(2,1)S(1)}, bf16[512,1536]{1,0:T(8,128)(2,1)S(1)}) custom-call(s32[4]{0:T(128)S(1)} %pad_add_fusion.info, bf16[512,768]{1,0:T(8,128)(2,1)} %get-tuple-element.127.x_ref.first, bf16[16,128]{1,0:T(8,128)(2,1)S(1)} %convert_element_type.87.b0_ref.b1_ref, bf16[16,128]{1,0:T(8,128)(2,1)S(1)} %convert_element_type.87.b0_ref.b1_ref, ...), custom_call_target="tpu_custom_call" | custom-call | bytes 6496272 | tf_op jit(solution)/shard_map/ffn_up/pallas_call | solution.py:124
  178.9 7.5 %ffn_up.3 = (bf16[512,1536]{1,0:T(8,128)(2,1)S(1)}, bf16[512,1536]{1,0:T(8,128)(2,1)S(1)}) custom-call(s32[4]{0:T(128)S(1)} %pad_add_fusion.info, bf16[512,768]{1,0:T(8,128)(2,1)} %collective-permute-done.20.x_ref.first2, bf16[16,128]{1,0:T(8,128)(2,1)S(1)} %convert_element_type.87.b0_ref.b1_ref, bf16[16,128]{1,0:T(8,128)(2,1)S(1)} %convert_element_type.87.b0_ref.b1_ref, ...), custom_call_target="tpu_custom_call" | custom-call | bytes 6496272 | tf_op jit(solution)/shard_map/ffn_up/pallas_call | solution.py:124
  186.4 5.8 %collective-permute-done.19.rest_3_ = bf16[1,4,96,768]{3,2,1,0:T(8,128)(2,1)S(1)} collective-permute-done((bf16[1,4,96,768]{3,2,1,0:T(8,128)(2,1)S(1)}, bf16[1,4,96,768]{3,2,1,0:T(8,128)(2,1)S(1)}, u32[]{:S(2)}, u32[]{:S(2)}) %collective-permute-start.19) | collective-permute-done | bytes 589856 | tf_op jit(solution)/shard_map/ppermute | solution.py:36
  192.2 5.1 %product.5 = bf16[512,768]{1,0:T(8,128)(2,1)} custom-call(s32[4]{0:T(128)S(1)} %pad_add_fusion.info, bf16[512,1536]{1,0:T(8,128)(2,1)S(1)} %get-tuple-element.131.a_ref.act2, bf16[1,4,96,768]{3,2,1,0:T(8,128)(2,1)S(1)} %maximum_bitcast_fusion.2.rest_0_, bf16[1,4,96,768]{3,2,1,0:T(8,128)(2,1)} %collective-permute-done.16.rest_1_, ...), custom_call_target="tpu_custom_call" | custom-call | bytes 4718608 | tf_op jit(solution)/shard_map/product/pallas_call | solution.py:124
  200.0 4.2 product.4.part_ref
  204.2 4.3 ln2.1
  213.3 4.5 %all-to-all-start.3 = ((bf16[8,64,768]{2,1,0:T(8,128)(2,1)}), bf16[8,64,768]{2,1,0:T(8,128)(2,1)}, u32[]{:S(2)}, u32[]{:S(2)}) async-start(bf16[8,64,768]{2,1,0:T(8,128)(2,1)} %bitcast.92), calls=%async_computation.3 | async-start | bytes 1572864 | tf_op jit(solution)/shard_map/all_to_all | solution.py:906
  226.0 6.2 %head.1 = (f32[512,768]{1,0:T(8,128)S(1)}, bf16[512,768]{1,0:T(8,128)(2,1)S(1)}, f32[768,128]{1,0:T(8,128)S(1)}, f32[128,128]{1,0:T(8,128)S(1)}, f32[128,128]{1,...) custom-call(s32[4]{0:T(128)S(1)} %pad_add_fusion.info, ...), custom_call_target="tpu_custom_call" | custom-call | bytes 4037632 | tf_op jit(solution)/shard_map/head/pallas_call | solution.py:155
  234.4 4.3 ffn_back.2
  245.0 4.3 ffn_back.3
  249.3 4.4 %product.7 = bf16[512,768]{1,0:T(8,128)(2,1)S(1)} custom-call(s32[4]{0:T(128)S(1)} %pad_add_fusion.info, bf16[512,1536]{1,0:T(8,128)(2,1)S(1)} %get-tuple-element.149.dpre2.a_ref, bf16[1,4,104,768]{3,2,1,0:T(8,128)(2,1)S(1)} %maximum_bitcast_fusion.1.rest_0_, bf16[1,4,104,768]{3,2,1,0:T(8,128)(2,1)} %collective-permute-done.13.rest_1_, ...), custom_call_target="tpu_custom_call" | custom-call | bytes 4915216 | tf_op jit(solution)/shard_map/product/pallas_call | solution.py:124
  253.8 4.4 %product.6.part_ref = f32[512,768]{1,0:T(8,128)S(1)} custom-call(s32[4]{0:T(128)S(1)} %pad_add_fusion.info, bf16[512,1536]{1,0:T(8,128)(2,1)S(1)} %copy-done.15, bf16[1,4,104,768]{3,2,1,0:T(8,128)(2,1)S(1)} %maximum_bitcast_fusion.1.rest_0_, bf16[1,4,104,768]{3,2,1,0:T(8,128)(2,1)} %collective-permute-done.13.rest_1_, ...), custom_call_target="tpu_custom_call" | custom-call | bytes 5701648 | tf_op jit(solution)/shard_map/product/pallas_call | solution.py:124
  258.2 2.6 collective-permute-done.25.b_ref
  260.9 1.7 ln1_back.1
  266.1 7.9 %ffn_grad.1 = (bf16[2,4,96,768]{3,2,1,0:T(8,128)(2,1)S(1)}, bf16[2,4,96,768]{3,2,1,0:T(8,128)(2,1)S(1)}, bf16[2,4,96,768]{3,2,1,0:T(8,128)(2,1)S(1)}, bf16[2,4,96,768]{3,2,1,0:T(8,128)(2,1)}) custom-call(s32[4]{0:T(128)S(1)} %pad_add_fusion.info, bf16[512,768]{1,0:T(8,128)(2,1)} %get-tuple-element.127.x_ref.first, ...), custom_call_target="tpu_custom_call" | custom-call | bytes 14155792 | tf_op jit(solution)/shard_map/ffn_grad/pallas_call | solution.py:124
  275.1 2.1 collective-permute-start.29
  279.7 8.8 %attn_bwd.2 = (bf16[1024,640]{1,0:T(8,128)(2,1)S(1)}, f32[8,640]{1,0:T(8,128)S(1)}) custom-call(bf16[1024,640]{1,0:T(8,128)(2,1)S(1)} %copy-done.111, bf16[768,768]{1,0:T(8,128)(2,1)S(1)} %copy-done.4, bf16[1024,128]{1,0:T(8,128)(2,1)S(1)} %copy-done.72, bf16[1024,256]{1,0:T(8,128)(2,1)S(1)} %copy-done.21, ...), custom_call_target="tpu_custom_call" | custom-call | flops 11000000512 | bytes 6213632 | tf_op jit(solution)/shard_map/attn_bwd/pallas_call | solution.py:124
  288.5 2.5 qkv_grad.2
  291.0 1.9 collective-permute-start.31
  292.9 8.6 %attn_bwd.3 = (bf16[1024,640]{1,0:T(8,128)(2,1)S(1)}, f32[8,640]{1,0:T(8,128)S(1)}) custom-call(bf16[1024,640]{1,0:T(8,128)(2,1)S(1)} %copy-done.109, bf16[768,768]{1,0:T(8,128)(2,1)S(1)} %get-tuple-element.124.w0_ref.w_ref, bf16[1024,128]{1,0:T(8,128)(2,1)S(1)} %copy-done.72, bf16[1024,256]{1,0:T(8,128)(2,1)S(1)} %copy-done.18, ...), custom_call_target="tpu_custom_call" | custom-call | flops 11000000512 | bytes 6213632 | tf_op jit(solution)/shard_map/attn_bwd/pallas_call | solution.py:124
  301.5 2.4 collective-permute-done.29.refs_1_
  304.6 12.2 %collective-permute-done.31 = bf16[1,4,104,768]{3,2,1,0:T(8,128)(2,1)S(1)} collective-permute-done((bf16[1,4,104,768]{3,2,1,0:T(8,128)(2,1)S(1)}, bf16[1,4,104,768]{3,2,1,0:T(8,128)(2,1)S(1)}, u32[]{:S(2)}, u32[]{:S(2)}) %collective-permute-start.31) | collective-permute-done | bytes 639008 | tf_op jit(solution)/shard_map/ppermute | solution.py:36
  316.8 2.9 token_grad.1
  319.8 2.7 collective-permute-start.32
  322.6 3.4 qkv_grad.3
  327.1 4.7 %all-to-all-start.4 = ((bf16[8,64,768]{2,1,0:T(8,128)(2,1)}), bf16[8,64,768]{2,1,0:T(8,128)(2,1)S(1)}, u32[]{:S(2)}, u32[]{:S(2)}) async-start(bf16[8,64,768]{2,1,0:T(8,128)(2,1)} %bitcast.95), calls=%async_computation.4 | async-start | bytes 1572864 | tf_op jit(solution)/shard_map/all_to_all | solution.py:906
  331.8 24.4 %collective-permute-done.32.refs_3_ = bf16[2,4,96,768]{3,2,1,0:T(8,128)(2,1)} collective-permute-done((bf16[2,4,96,768]{3,2,1,0:T(8,128)(2,1)}, bf16[2,4,96,768]{3,2,1,0:T(8,128)(2,1)}, u32[]{:S(2)}, u32[]{:S(2)}) %collective-permute-start.32) | collective-permute-done | bytes 1179680 | tf_op jit(solution)/shard_map/ppermute | solution.py:36
  357.5 1.9 grad_sum.2
  359.5 1.8 collective-permute-start.39
  361.3 2.4 collective-permute-start.40
  368.1 4.9 %collective-permute-done.39 = bf16[2,96,768]{2,1,0:T(8,128)(2,1)} collective-permute-done((bf16[2,96,768]{2,1,0:T(8,128)(2,1)S(1)}, bf16[2,96,768]{2,1,0:T(8,128)(2,1)}, u32[]{:S(2)}, u32[]{:S(2)}) %collective-permute-start.39) | collective-permute-done | bytes 294944 | tf_op jit(solution)/shard_map/ppermute | solution.py:36
  373.1 11.6 %collective-permute-done.40 = bf16[2,96,768]{2,1,0:T(8,128)(2,1)} collective-permute-done((bf16[2,96,768]{2,1,0:T(8,128)(2,1)S(1)}, bf16[2,96,768]{2,1,0:T(8,128)(2,1)}, u32[]{:S(2)}, u32[]{:S(2)}) %collective-permute-start.40) | collective-permute-done | bytes 294944 | tf_op jit(solution)/shard_map/ppermute | solution.py:36
  387.5 2.1 grad_sum.3
  389.6 3.6 collective-permute-start.44
  396.5 5.6 %place.2 = bf16[8,2,2,64,768]{4,3,2,1,0:T(8,128)(2,1)} custom-call(s32[4]{0:T(128)S(1)} %pad_add_fusion.info, bf16[8,64,768]{2,1,0:T(8,128)(2,1)} %all-to-all-done.3.a_ref, bf16[8,64,768]{2,1,0:T(8,128)(2,1)S(1)} %copy-done.56, bf16[8,64,768]{2,1,0:T(8,128)(2,1)S(1)} %collective-permute-done.33.c_ref, bf16[8,64,768]{2,1,0:T(8,128)(2,1)S(1)} %collective-permute-done.34.d_ref), custom_call_target="tpu_custom_call" | custom-call | bytes 6000000 | tf_op jit(solution)/shard_map/place/pallas_call | solution.py:910
  402.1 1.5 collective-permute-start.36
  403.6 4.5 %all-to-all-start.5 = ((bf16[8,224,128]{2,1,0:T(8,128)(2,1)}), bf16[8,224,128]{2,1,0:T(8,128)(2,1)}, u32[]{:S(2)}, u32[]{:S(2)}) async-start(bf16[8,224,128]{2,1,0:T(8,128)(2,1)} %convert_add_fusion), calls=%async_computation.5 | async-start | bytes 917504 | tf_op jit(solution)/shard_map/all_to_all | solution.py:1141
  411.9 7.7 %collective-permute-done.36.b_ref = bf16[8,64,768]{2,1,0:T(8,128)(2,1)S(1)} collective-permute-done((bf16[8,64,768]{2,1,0:T(8,128)(2,1)S(1)}, bf16[8,64,768]{2,1,0:T(8,128)(2,1)S(1)}, u32[]{:S(2)}, u32[]{:S(2)}) %collective-permute-start.36) | collective-permute-done | bytes 786464 | tf_op jit(solution)/shard_map/ppermute | solution.py:36
  432.7 3.8 place.3
  (414 shorter events, 105.2 us)
Async XLA Ops:
  4.5 10.2 %collective-permute-start.2 = (bf16[1,1,104,768]{3,2,1,0:T(8,128)(2,1)}, bf16[1,1,104,768]{3,2,1,0:T(8,128)(2,1)S(1)}, u32[]{:S(2)}, u32[]{:S(2)}) collective-permute-start(bf16[1,1,104,768]{3,2,1,0:T(8,128)(2,1)} %get-tuple-element.252), channel_id=1, source_target_pairs={{0,24},{1,25},{2,26},{3,27},{4,28},{5,29},{6,30},{7,31},{8,16},{9,... | collective-permute-start | bytes 479240 | tf_op jit(solution)/shard_map/ppermute | solution.py:36
  9.5 8.9 %collective-permute-start = (bf16[1,1,104,768]{3,2,1,0:T(8,128)(2,1)}, bf16[1,1,104,768]{3,2,1,0:T(8,128)(2,1)}, u32[]{:S(2)}, u32[]{:S(2)}) collective-permute-start(bf16[1,1,104,768]{3,2,1,0:T(8,128)(2,1)} %get-tuple-element.252), channel_id=1, source_target_pairs={{0,8},{1,9},{2,10},{3,11},{4,12},{5,13},{6,14},{7,15},{8,0},{9,1},... | collective-permute-start | bytes 479240 | tf_op jit(solution)/shard_map/ppermute | solution.py:36
  9.5 13.8 %collective-permute-start.1 = (bf16[1,1,104,768]{3,2,1,0:T(8,128)(2,1)}, bf16[1,1,104,768]{3,2,1,0:T(8,128)(2,1)}, u32[]{:S(2)}, u32[]{:S(2)}) collective-permute-start(bf16[1,1,104,768]{3,2,1,0:T(8,128)(2,1)} %get-tuple-element.252), channel_id=1, source_target_pairs={{0,16},{1,17},{2,18},{3,19},{4,20},{5,21},{6,22},{7,23},{8,24},{9,... | collective-permute-start | bytes 479240 | tf_op jit(solution)/shard_map/ppermute | solution.py:36
  26.2 50.1 %copy-start.126 = (bf16[96]{0:T(256)(128)(2,1)S(1)}, bf16[96]{0:T(256)(128)(2,1)}, u32[]{:S(2)}) copy-start(bf16[96]{0:T(256)(128)(2,1)} %param.30) | copy-start | bytes 580
  26.3 50.1 %copy-start.127 = (bf16[96]{0:T(256)(128)(2,1)S(1)}, bf16[96]{0:T(256)(128)(2,1)}, u32[]{:S(2)}) copy-start(bf16[96]{0:T(256)(128)(2,1)} %param.31) | copy-start | bytes 580
  26.3 50.2 %copy-start.128 = (bf16[96]{0:T(256)(128)(2,1)S(1)}, bf16[96]{0:T(256)(128)(2,1)}, u32[]{:S(2)}) copy-start(bf16[96]{0:T(256)(128)(2,1)} %param.32) | copy-start | bytes 580
  26.3 50.2 %copy-start.129 = (bf16[96]{0:T(256)(128)(2,1)S(1)}, bf16[96]{0:T(256)(128)(2,1)}, u32[]{:S(2)}) copy-start(bf16[96]{0:T(256)(128)(2,1)} %param.36) | copy-start | bytes 580
  26.3 50.2 %copy-start.130 = (bf16[96]{0:T(256)(128)(2,1)S(1)}, bf16[96]{0:T(256)(128)(2,1)}, u32[]{:S(2)}) copy-start(bf16[96]{0:T(256)(128)(2,1)} %param.37) | copy-start | bytes 580
  26.3 50.2 %copy-start.131 = (bf16[96]{0:T(256)(128)(2,1)S(1)}, bf16[96]{0:T(256)(128)(2,1)}, u32[]{:S(2)}) copy-start(bf16[96]{0:T(256)(128)(2,1)} %param.38) | copy-start | bytes 580
  26.3 50.2 %copy-start.132 = (bf16[16]{0:T(256)(128)(2,1)S(1)}, bf16[16]{0:T(256)(128)(2,1)}, u32[]{:S(2)}) copy-start(bf16[16]{0:T(256)(128)(2,1)} %param.40) | copy-start | bytes 100
  26.3 50.2 %copy-start.133 = (bf16[16]{0:T(256)(128)(2,1)S(1)}, bf16[16]{0:T(256)(128)(2,1)}, u32[]{:S(2)}) copy-start(bf16[16]{0:T(256)(128)(2,1)} %param.41) | copy-start | bytes 100
  26.3 50.2 %copy-start.134 = (bf16[16]{0:T(256)(128)(2,1)S(1)}, bf16[16]{0:T(256)(128)(2,1)}, u32[]{:S(2)}) copy-start(bf16[16]{0:T(256)(128)(2,1)} %param.43) | copy-start | bytes 100
  26.4 50.2 %copy-start.120 = (bf16[96,128]{1,0:T(8,128)(2,1)S(1)}, bf16[96,128]{1,0:T(8,128)(2,1)}, u32[]{:S(2)}) copy-start(bf16[96,128]{1,0:T(8,128)(2,1)} %param.39) | copy-start | bytes 73732
  26.4 50.2 %copy-start.121 = (bf16[16,128]{1,0:T(8,128)(2,1)S(1)}, bf16[16,128]{1,0:T(8,128)(2,1)}, u32[]{:S(2)}) copy-start(bf16[16,128]{1,0:T(8,128)(2,1)} %param.42) | copy-start | bytes 12292
  26.4 43.9 %all-to-all-start = ((bf16[8,64,768]{2,1,0:T(8,128)(2,1)}), bf16[8,64,768]{2,1,0:T(8,128)(2,1)S(1)}, u32[]{:S(2)}, u32[]{:S(2)}) async-start(bf16[8,64,768]{2,1,0:T(8,128)(2,1)} %dynamic-slice_bitcast_fusion.1), calls=%async_computation | async-start | bytes 1572864 | tf_op jit(solution)/shard_map/all_to_all | solution.py:903
  31.2 31.4 %collective-permute-start.3 = (bf16[1,4,104,768]{3,2,1,0:T(8,128)(2,1)S(1)}, bf16[1,4,104,768]{3,2,1,0:T(8,128)(2,1)}, u32[]{:S(2)}, u32[]{:S(2)}) collective-permute-start(bf16[1,4,104,768]{3,2,1,0:T(8,128)(2,1)S(1)} %copy-done.63), channel_id=1, source_target_pairs={{0,4},{1,5},{2,6},{3,7},{4,0},{5,1},{6,2},{7,3},{8,12},{9,13},{10,... | collective-permute-start | bytes 1916936 | tf_op jit(solution)/shard_map/ppermute | solution.py:36
  33.2 29.3 %collective-permute-start.4 = (bf16[1,4,104,768]{3,2,1,0:T(8,128)(2,1)S(1)}, bf16[1,4,104,768]{3,2,1,0:T(8,128)(2,1)S(1)}, u32[]{:S(2)}, u32[]{:S(2)}) collective-permute-start(bf16[1,4,104,768]{3,2,1,0:T(8,128)(2,1)S(1)} %copy-done.63), channel_id=1, source_target_pairs={{0,2},{1,3},{2,0},{3,1},{4,6},{5,7},{6,4},{7,5},{8,10},{9,11},{10,... | collective-permute-start | bytes 1916936 | tf_op jit(solution)/shard_map/ppermute | solution.py:36
  34.7 34.7 %collective-permute-start.5 = (bf16[1,4,104,768]{3,2,1,0:T(8,128)(2,1)S(1)}, bf16[1,4,104,768]{3,2,1,0:T(8,128)(2,1)S(1)}, u32[]{:S(2)}, u32[]{:S(2)}) collective-permute-start(bf16[1,4,104,768]{3,2,1,0:T(8,128)(2,1)S(1)} %copy-done.63), channel_id=1, source_target_pairs={{0,6},{1,7},{2,4},{3,5},{4,2},{5,3},{6,0},{7,1},{8,14},{9,15},{10,... | collective-permute-start | bytes 1916936 | tf_op jit(solution)/shard_map/ppermute | solution.py:36
  35.0 13.4 %collective-permute-start.6 = (bf16[1,1,104,768]{3,2,1,0:T(8,128)(2,1)S(1)}, bf16[1,1,104,768]{3,2,1,0:T(8,128)(2,1)S(1)}, u32[]{:S(2)}, u32[]{:S(2)}) collective-permute-start(bf16[1,1,104,768]{3,2,1,0:T(8,128)(2,1)S(1)} %bitcast.98), channel_id=1, source_target_pairs={{0,8},{1,9},{2,10},{3,11},{4,12},{5,13},{6,14},{7,15},{8,0},{9,1},... | collective-permute-start | bytes 479240 | tf_op jit(solution)/shard_map/ppermute | solution.py:36
  37.0 25.5 %collective-permute-start.7 = (bf16[1,1,104,768]{3,2,1,0:T(8,128)(2,1)S(1)}, bf16[1,1,104,768]{3,2,1,0:T(8,128)(2,1)S(1)}, u32[]{:S(2)}, u32[]{:S(2)}) collective-permute-start(bf16[1,1,104,768]{3,2,1,0:T(8,128)(2,1)S(1)} %bitcast.99), channel_id=1, source_target_pairs={{0,16},{1,17},{2,18},{3,19},{4,20},{5,21},{6,22},{7,23},{8,24},{9,... | collective-permute-start | bytes 479240 | tf_op jit(solution)/shard_map/ppermute | solution.py:36
  48.4 14.2 %collective-permute-start.8 = (bf16[1,1,104,768]{3,2,1,0:T(8,128)(2,1)S(1)}, bf16[1,1,104,768]{3,2,1,0:T(8,128)(2,1)S(1)}, u32[]{:S(2)}, u32[]{:S(2)}) collective-permute-start(bf16[1,1,104,768]{3,2,1,0:T(8,128)(2,1)S(1)} %bitcast.100), channel_id=1, source_target_pairs={{0,24},{1,25},{2,26},{3,27},{4,28},{5,29},{6,30},{7,31},{8,16},{9,... | collective-permute-start | bytes 479240 | tf_op jit(solution)/shard_map/ppermute | solution.py:36
  70.3 18.7 %collective-permute-start.9 = (bf16[512,768]{1,0:T(8,128)(2,1)S(1)}, bf16[512,768]{1,0:T(8,128)(2,1)S(1)}, u32[]{:S(2)}, u32[]{:S(2)}) collective-permute-start(bf16[512,768]{1,0:T(8,128)(2,1)S(1)} %bitcast.86), channel_id=1, source_target_pairs={{0,1},{1,0},{2,3},{3,2},{4,5},{5,4},{6,7},{7,6},{8,9},{9,8},{10,11... | collective-permute-start | bytes 2359304 | tf_op jit(solution)/shard_map/ppermute | solution.py:36
  71.1 9.2 %collective-permute-start.10 = (bf16[1,1,96,768]{3,2,1,0:T(8,128)(2,1)}, bf16[1,1,96,768]{3,2,1,0:T(8,128)(2,1)S(1)}, u32[]{:S(2)}, u32[]{:S(2)}) collective-permute-start(bf16[1,1,96,768]{3,2,1,0:T(8,128)(2,1)} %bitcast.109), channel_id=1, source_target_pairs={{0,8},{1,9},{2,10},{3,11},{4,12},{5,13},{6,14},{7,15},{8,0},{9,1},... | collective-permute-start | bytes 442376 | tf_op jit(solution)/shard_map/ppermute | solution.py:36
  72.6 14.2 %collective-permute-start.11 = (bf16[1,1,96,768]{3,2,1,0:T(8,128)(2,1)}, bf16[1,1,96,768]{3,2,1,0:T(8,128)(2,1)S(1)}, u32[]{:S(2)}, u32[]{:S(2)}) collective-permute-start(bf16[1,1,96,768]{3,2,1,0:T(8,128)(2,1)} %bitcast.110), channel_id=1, source_target_pairs={{0,16},{1,17},{2,18},{3,19},{4,20},{5,21},{6,22},{7,23},{8,24},{9,... | collective-permute-start | bytes 442376 | tf_op jit(solution)/shard_map/ppermute | solution.py:36
  75.0 12.3 %collective-permute-start.12 = (bf16[1,1,96,768]{3,2,1,0:T(8,128)(2,1)}, bf16[1,1,96,768]{3,2,1,0:T(8,128)(2,1)S(1)}, u32[]{:S(2)}, u32[]{:S(2)}) collective-permute-start(bf16[1,1,96,768]{3,2,1,0:T(8,128)(2,1)} %bitcast.111), channel_id=1, source_target_pairs={{0,24},{1,25},{2,26},{3,27},{4,28},{5,29},{6,30},{7,31},{8,16},{9,... | collective-permute-start | bytes 442376 | tf_op jit(solution)/shard_map/ppermute | solution.py:36
  77.6 59.6 %collective-permute-start.13 = (bf16[1,4,104,768]{3,2,1,0:T(8,128)(2,1)S(1)}, bf16[1,4,104,768]{3,2,1,0:T(8,128)(2,1)}, u32[]{:S(2)}, u32[]{:S(2)}) collective-permute-start(bf16[1,4,104,768]{3,2,1,0:T(8,128)(2,1)S(1)} %maximum_bitcast_fusion.1.rest_0_), channel_id=1, source_target_pairs={{0,4},{1,5},{2,6},{3,7},{4,0},{5,1},{6,2},{7,3},{8,12},{9,13},{10,... | collective-permute-start | bytes 1916936 | tf_op jit(solution)/shard_map/ppermute | solution.py:36
  80.3 56.9 %collective-permute-start.14 = (bf16[1,4,104,768]{3,2,1,0:T(8,128)(2,1)S(1)}, bf16[1,4,104,768]{3,2,1,0:T(8,128)(2,1)}, u32[]{:S(2)}, u32[]{:S(2)}) collective-permute-start(bf16[1,4,104,768]{3,2,1,0:T(8,128)(2,1)S(1)} %maximum_bitcast_fusion.1.rest_0_), channel_id=1, source_target_pairs={{0,2},{1,3},{2,0},{3,1},{4,6},{5,7},{6,4},{7,5},{8,10},{9,11},{10,... | collective-permute-start | bytes 1916936 | tf_op jit(solution)/shard_map/ppermute | solution.py:36
  86.8 50.4 %collective-permute-start.15 = (bf16[1,4,104,768]{3,2,1,0:T(8,128)(2,1)S(1)}, bf16[1,4,104,768]{3,2,1,0:T(8,128)(2,1)}, u32[]{:S(2)}, u32[]{:S(2)}) collective-permute-start(bf16[1,4,104,768]{3,2,1,0:T(8,128)(2,1)S(1)} %maximum_bitcast_fusion.1.rest_0_), channel_id=1, source_target_pairs={{0,6},{1,7},{2,4},{3,5},{4,2},{5,3},{6,0},{7,1},{8,14},{9,15},{10,... | collective-permute-start | bytes 1916936 | tf_op jit(solution)/shard_map/ppermute | solution.py:36
  106.5 30.6 %collective-permute-start.16 = (bf16[1,4,96,768]{3,2,1,0:T(8,128)(2,1)S(1)}, bf16[1,4,96,768]{3,2,1,0:T(8,128)(2,1)}, u32[]{:S(2)}, u32[]{:S(2)}) collective-permute-start(bf16[1,4,96,768]{3,2,1,0:T(8,128)(2,1)S(1)} %maximum_bitcast_fusion.2.rest_0_), channel_id=1, source_target_pairs={{0,4},{1,5},{2,6},{3,7},{4,0},{5,1},{6,2},{7,3},{8,12},{9,13},{10,... | collective-permute-start | bytes 1769480 | tf_op jit(solution)/shard_map/ppermute | solution.py:36
  108.0 29.2 %collective-permute-start.17 = (bf16[1,4,96,768]{3,2,1,0:T(8,128)(2,1)S(1)}, bf16[1,4,96,768]{3,2,1,0:T(8,128)(2,1)}, u32[]{:S(2)}, u32[]{:S(2)}) collective-permute-start(bf16[1,4,96,768]{3,2,1,0:T(8,128)(2,1)S(1)} %maximum_bitcast_fusion.2.rest_0_), channel_id=1, source_target_pairs={{0,2},{1,3},{2,0},{3,1},{4,6},{5,7},{6,4},{7,5},{8,10},{9,11},{10,... | collective-permute-start | bytes 1769480 | tf_op jit(solution)/shard_map/ppermute | solution.py:36
  110.3 24.2 %all-to-all-start.1 = ((bf16[8,160,128]{2,1,0:T(8,128)(2,1)}), bf16[8,160,128]{2,1,0:T(8,128)(2,1)S(1)}, u32[]{:S(2)}, u32[]{:S(2)}) async-start(bf16[8,160,128]{2,1,0:T(8,128)(2,1)} %broadcast_in_dim.55), calls=%async_computation.1 | async-start | bytes 655360 | tf_op jit(solution)/shard_map/all_to_all | solution.py:981
  141.2 2.4 collective-permute-start.18
  148.9 30.0 %collective-permute-start.20 = (bf16[512,768]{1,0:T(8,128)(2,1)}, bf16[512,768]{1,0:T(8,128)(2,1)}, u32[]{:S(2)}, u32[]{:S(2)}) collective-permute-start(bf16[512,768]{1,0:T(8,128)(2,1)} %get-tuple-element.127.x_ref.first), channel_id=1, source_target_pairs={{0,1},{1,0},{2,3},{3,2},{4,5},{5,4},{6,7},{7,6},{8,9},{9,8},{10,11... | collective-permute-start | bytes 2359304 | tf_op jit(solution)/shard_map/ppermute | solution.py:36
  151.5 46.0 %all-to-all-start.2 = ((bf16[8,64,768]{2,1,0:T(8,128)(2,1)}), bf16[8,64,768]{2,1,0:T(8,128)(2,1)}, u32[]{:S(2)}, u32[]{:S(2)}) async-start(bf16[8,64,768]{2,1,0:T(8,128)(2,1)} %dynamic-slice_bitcast_fusion), calls=%async_computation.2 | async-start | bytes 1572864 | tf_op jit(solution)/shard_map/all_to_all | solution.py:903
  167.6 24.6 %collective-permute-start.19 = (bf16[1,4,96,768]{3,2,1,0:T(8,128)(2,1)S(1)}, bf16[1,4,96,768]{3,2,1,0:T(8,128)(2,1)S(1)}, u32[]{:S(2)}, u32[]{:S(2)}) collective-permute-start(bf16[1,4,96,768]{3,2,1,0:T(8,128)(2,1)S(1)} %maximum_bitcast_fusion.2.rest_0_), channel_id=1, source_target_pairs={{0,6},{1,7},{2,4},{3,5},{4,2},{5,3},{6,0},{7,1},{8,14},{9,15},{10,... | collective-permute-start | bytes 1769480 | tf_op jit(solution)/shard_map/ppermute | solution.py:36
  197.4 6.8 %collective-permute-start.21 = (bf16[512,768]{1,0:T(8,128)(2,1)}, bf16[512,768]{1,0:T(8,128)(2,1)}, u32[]{:S(2)}, u32[]{:S(2)}) collective-permute-start(bf16[512,768]{1,0:T(8,128)(2,1)} %product.5), channel_id=1, source_target_pairs={{0,1},{1,0},{2,3},{3,2},{4,5},{5,4},{6,7},{7,6},{8,9},{9,8},{10,11... | collective-permute-start | bytes 2359304 | tf_op jit(solution)/shard_map/ppermute | solution.py:36
  213.3 27.6 %all-to-all-start.3 = ((bf16[8,64,768]{2,1,0:T(8,128)(2,1)}), bf16[8,64,768]{2,1,0:T(8,128)(2,1)}, u32[]{:S(2)}, u32[]{:S(2)}) async-start(bf16[8,64,768]{2,1,0:T(8,128)(2,1)} %bitcast.92), calls=%async_computation.3 | async-start | bytes 1572864 | tf_op jit(solution)/shard_map/all_to_all | solution.py:906
  217.8 1.4 collective-permute-start.22
  234.1 5.8 %collective-permute-start.23 = (bf16[512,768]{1,0:T(8,128)(2,1)S(1)}, bf16[512,768]{1,0:T(8,128)(2,1)S(1)}, u32[]{:S(2)}, u32[]{:S(2)}) collective-permute-start(bf16[512,768]{1,0:T(8,128)(2,1)S(1)} %get-tuple-element.144.g_ref.dffn), channel_id=1, source_target_pairs={{0,1},{1,0},{2,3},{3,2},{4,5},{5,4},{6,7},{7,6},{8,9},{9,8},{10,11... | collective-permute-start | bytes 2359304 | tf_op jit(solution)/shard_map/ppermute | solution.py:36
  240.9 19.9 %collective-permute-start.25 = (bf16[8,64,768]{2,1,0:T(8,128)(2,1)}, bf16[8,64,768]{2,1,0:T(8,128)(2,1)S(1)}, u32[]{:S(2)}, u32[]{:S(2)}) collective-permute-start(bf16[8,64,768]{2,1,0:T(8,128)(2,1)} %all-to-all-done.3.a_ref), channel_id=1, source_target_pairs={{0,2},{1,3},{2,0},{3,1},{4,6},{5,7},{6,4},{7,5},{8,10},{9,11},{10,... | collective-permute-start | bytes 2359304 | tf_op jit(solution)/shard_map/ppermute | solution.py:36
  253.7 7.1 %collective-permute-start.24 = (bf16[512,768]{1,0:T(8,128)(2,1)S(1)}, bf16[512,768]{1,0:T(8,128)(2,1)S(1)}, u32[]{:S(2)}, u32[]{:S(2)}) collective-permute-start(bf16[512,768]{1,0:T(8,128)(2,1)S(1)} %product.7), channel_id=1, source_target_pairs={{0,1},{1,0},{2,3},{3,2},{4,5},{5,4},{6,7},{7,6},{8,9},{9,8},{10,11... | collective-permute-start | bytes 2359304 | tf_op jit(solution)/shard_map/ppermute | solution.py:36
  263.5 1.9 collective-permute-start.27
  263.6 15.1 %collective-permute-start.26 = (bf16[512,768]{1,0:T(8,128)(2,1)S(1)}, bf16[512,768]{1,0:T(8,128)(2,1)S(1)}, u32[]{:S(2)}, u32[]{:S(2)}) collective-permute-start(bf16[512,768]{1,0:T(8,128)(2,1)S(1)} %get-tuple-element.156.da_ref.da), channel_id=1, source_target_pairs={{0,1},{1,0},{2,3},{3,2},{4,5},{5,4},{6,7},{7,6},{8,9},{9,8},{10,11... | collective-permute-start | bytes 2359304 | tf_op jit(solution)/shard_map/ppermute | solution.py:36
  265.5 13.2 %collective-permute-start.28 = (bf16[8,224,128]{2,1,0:T(8,128)(2,1)S(1)}, bf16[8,224,128]{2,1,0:T(8,128)(2,1)S(1)}, u32[]{:S(2)}, u32[]{:S(2)}) collective-permute-start(bf16[8,224,128]{2,1,0:T(8,128)(2,1)S(1)} %fusion), channel_id=1, source_target_pairs={{0,2},{1,3},{2,0},{3,1},{4,6},{5,7},{6,4},{7,5},{8,10},{9,11},{10,... | collective-permute-start | bytes 1376264 | tf_op jit(solution)/shard_map/ppermute | solution.py:36
  275.1 28.9 %collective-permute-start.29 = (bf16[2,4,96,768]{3,2,1,0:T(8,128)(2,1)S(1)}, bf16[2,4,96,768]{3,2,1,0:T(8,128)(2,1)S(1)}, u32[]{:S(2)}, u32[]{:S(2)}) collective-permute-start(bf16[2,4,96,768]{3,2,1,0:T(8,128)(2,1)S(1)} %get-tuple-element.157), channel_id=1, source_target_pairs={{0,4},{1,5},{2,6},{3,7},{4,0},{5,1},{6,2},{7,3},{8,12},{9,13},{10,... | collective-permute-start | bytes 3538952 | tf_op jit(solution)/shard_map/ppermute | solution.py:36
  277.2 27.4 %collective-permute-start.30 = (bf16[2,4,96,768]{3,2,1,0:T(8,128)(2,1)S(1)}, bf16[2,4,96,768]{3,2,1,0:T(8,128)(2,1)S(1)}, u32[]{:S(2)}, u32[]{:S(2)}) collective-permute-start(bf16[2,4,96,768]{3,2,1,0:T(8,128)(2,1)S(1)} %get-tuple-element.158), channel_id=1, source_target_pairs={{0,2},{1,3},{2,0},{3,1},{4,6},{5,7},{6,4},{7,5},{8,10},{9,11},{10,... | collective-permute-start | bytes 3538952 | tf_op jit(solution)/shard_map/ppermute | solution.py:36
  291.0 25.8 %collective-permute-start.31 = (bf16[1,4,104,768]{3,2,1,0:T(8,128)(2,1)S(1)}, bf16[1,4,104,768]{3,2,1,0:T(8,128)(2,1)S(1)}, u32[]{:S(2)}, u32[]{:S(2)}) collective-permute-start(bf16[1,4,104,768]{3,2,1,0:T(8,128)(2,1)S(1)} %get-tuple-element.176), channel_id=1, source_target_pairs={{0,4},{1,5},{2,6},{3,7},{4,0},{5,1},{6,2},{7,3},{8,12},{9,13},{10,... | collective-permute-start | bytes 1916936 | tf_op jit(solution)/shard_map/ppermute | solution.py:36
  319.8 6.2 %collective-permute-start.35 = (bf16[512,768]{1,0:T(8,128)(2,1)S(1)}, bf16[512,768]{1,0:T(8,128)(2,1)S(1)}, u32[]{:S(2)}, u32[]{:S(2)}) collective-permute-start(bf16[512,768]{1,0:T(8,128)(2,1)S(1)} %get-tuple-element.190), channel_id=1, source_target_pairs={{0,1},{1,0},{2,3},{3,2},{4,5},{5,4},{6,7},{7,6},{8,9},{9,8},{10,11... | collective-permute-start | bytes 2359304 | tf_op jit(solution)/shard_map/ppermute | solution.py:36
  319.8 36.4 %collective-permute-start.32 = (bf16[2,4,96,768]{3,2,1,0:T(8,128)(2,1)}, bf16[2,4,96,768]{3,2,1,0:T(8,128)(2,1)}, u32[]{:S(2)}, u32[]{:S(2)}) collective-permute-start(bf16[2,4,96,768]{3,2,1,0:T(8,128)(2,1)} %get-tuple-element.159), channel_id=1, source_target_pairs={{0,6},{1,7},{2,4},{3,5},{4,2},{5,3},{6,0},{7,1},{8,14},{9,15},{10,... | collective-permute-start | bytes 3538952 | tf_op jit(solution)/shard_map/ppermute | solution.py:36
  327.1 75.0 %all-to-all-start.4 = ((bf16[8,64,768]{2,1,0:T(8,128)(2,1)}), bf16[8,64,768]{2,1,0:T(8,128)(2,1)S(1)}, u32[]{:S(2)}, u32[]{:S(2)}) async-start(bf16[8,64,768]{2,1,0:T(8,128)(2,1)} %bitcast.95), calls=%async_computation.4 | async-start | bytes 1572864 | tf_op jit(solution)/shard_map/all_to_all | solution.py:906
  359.5 13.6 %collective-permute-start.39 = (bf16[2,96,768]{2,1,0:T(8,128)(2,1)S(1)}, bf16[2,96,768]{2,1,0:T(8,128)(2,1)}, u32[]{:S(2)}, u32[]{:S(2)}) collective-permute-start(bf16[2,96,768]{2,1,0:T(8,128)(2,1)S(1)} %get-tuple-element.183), channel_id=1, source_target_pairs={{0,8},{1,9},{2,10},{3,11},{4,12},{5,13},{6,14},{7,15},{8,0},{9,1},... | collective-permute-start | bytes 884744 | tf_op jit(solution)/shard_map/ppermute | solution.py:36
  361.3 23.4 %collective-permute-start.40 = (bf16[2,96,768]{2,1,0:T(8,128)(2,1)S(1)}, bf16[2,96,768]{2,1,0:T(8,128)(2,1)}, u32[]{:S(2)}, u32[]{:S(2)}) collective-permute-start(bf16[2,96,768]{2,1,0:T(8,128)(2,1)S(1)} %get-tuple-element.184), channel_id=1, source_target_pairs={{0,16},{1,17},{2,18},{3,19},{4,20},{5,21},{6,22},{7,23},{8,24},{9,... | collective-permute-start | bytes 884744 | tf_op jit(solution)/shard_map/ppermute | solution.py:36
  364.6 22.9 %collective-permute-start.43 = (bf16[1,4,104,768]{3,2,1,0:T(8,128)(2,1)}, bf16[1,4,104,768]{3,2,1,0:T(8,128)(2,1)}, u32[]{:S(2)}, u32[]{:S(2)}) collective-permute-start(bf16[1,4,104,768]{3,2,1,0:T(8,128)(2,1)} %add_convert_fusion.1), channel_id=1, source_target_pairs={{0,2},{1,3},{2,0},{3,1},{4,6},{5,7},{6,4},{7,5},{8,10},{9,11},{10,... | collective-permute-start | bytes 1916936 | tf_op jit(solution)/shard_map/ppermute | solution.py:36
  366.1 21.4 %collective-permute-start.42 = (bf16[1,4,104,768]{3,2,1,0:T(8,128)(2,1)}, bf16[1,4,104,768]{3,2,1,0:T(8,128)(2,1)}, u32[]{:S(2)}, u32[]{:S(2)}) collective-permute-start(bf16[1,4,104,768]{3,2,1,0:T(8,128)(2,1)} %get-tuple-element.193), channel_id=1, source_target_pairs={{0,4},{1,5},{2,6},{3,7},{4,0},{5,1},{6,2},{7,3},{8,12},{9,13},{10,... | collective-permute-start | bytes 1916936 | tf_op jit(solution)/shard_map/ppermute | solution.py:36
  367.6 18.4 %collective-permute-start.41 = (bf16[2,96,768]{2,1,0:T(8,128)(2,1)S(1)}, bf16[2,96,768]{2,1,0:T(8,128)(2,1)}, u32[]{:S(2)}, u32[]{:S(2)}) collective-permute-start(bf16[2,96,768]{2,1,0:T(8,128)(2,1)S(1)} %get-tuple-element.185), channel_id=1, source_target_pairs={{0,24},{1,25},{2,26},{3,27},{4,28},{5,29},{6,30},{7,31},{8,16},{9,... | collective-permute-start | bytes 884744 | tf_op jit(solution)/shard_map/ppermute | solution.py:36
  373.1 23.4 %collective-permute-start.34 = (bf16[8,64,768]{2,1,0:T(8,128)(2,1)S(1)}, bf16[8,64,768]{2,1,0:T(8,128)(2,1)S(1)}, u32[]{:S(2)}, u32[]{:S(2)}) collective-permute-start(bf16[8,64,768]{2,1,0:T(8,128)(2,1)S(1)} %copy-done.56), channel_id=1, source_target_pairs={{0,1},{1,0},{2,3},{3,2},{4,5},{5,4},{6,7},{7,6},{8,9},{9,8},{10,11... | collective-permute-start | bytes 2359304 | tf_op jit(solution)/shard_map/ppermute | solution.py:36
  384.7 11.8 %collective-permute-start.33 = (bf16[8,64,768]{2,1,0:T(8,128)(2,1)}, bf16[8,64,768]{2,1,0:T(8,128)(2,1)S(1)}, u32[]{:S(2)}, u32[]{:S(2)}) collective-permute-start(bf16[8,64,768]{2,1,0:T(8,128)(2,1)} %all-to-all-done.3.a_ref), channel_id=1, source_target_pairs={{0,1},{1,0},{2,3},{3,2},{4,5},{5,4},{6,7},{7,6},{8,9},{9,8},{10,11... | collective-permute-start | bytes 2359304 | tf_op jit(solution)/shard_map/ppermute | solution.py:36
  389.6 18.5 %collective-permute-start.44 = (bf16[1,104,768]{2,1,0:T(8,128)(2,1)}, bf16[1,104,768]{2,1,0:T(8,128)(2,1)}, u32[]{:S(2)}, u32[]{:S(2)}) collective-permute-start(bf16[1,104,768]{2,1,0:T(8,128)(2,1)} %get-tuple-element.200), channel_id=1, source_target_pairs={{0,8},{1,9},{2,10},{3,11},{4,12},{5,13},{6,14},{7,15},{8,0},{9,1},... | collective-permute-start | bytes 479240 | tf_op jit(solution)/shard_map/ppermute | solution.py:36
  393.3 14.9 %collective-permute-start.45 = (bf16[1,104,768]{2,1,0:T(8,128)(2,1)}, bf16[1,104,768]{2,1,0:T(8,128)(2,1)}, u32[]{:S(2)}, u32[]{:S(2)}) collective-permute-start(bf16[1,104,768]{2,1,0:T(8,128)(2,1)} %get-tuple-element.201), channel_id=1, source_target_pairs={{0,16},{1,17},{2,18},{3,19},{4,20},{5,21},{6,22},{7,23},{8,24},{9,... | collective-permute-start | bytes 479240 | tf_op jit(solution)/shard_map/ppermute | solution.py:36
  394.2 14.0 %collective-permute-start.46 = (bf16[1,104,768]{2,1,0:T(8,128)(2,1)}, bf16[1,104,768]{2,1,0:T(8,128)(2,1)}, u32[]{:S(2)}, u32[]{:S(2)}) collective-permute-start(bf16[1,104,768]{2,1,0:T(8,128)(2,1)} %get-tuple-element.202), channel_id=1, source_target_pairs={{0,24},{1,25},{2,26},{3,27},{4,28},{5,29},{6,30},{7,31},{8,16},{9,... | collective-permute-start | bytes 479240 | tf_op jit(solution)/shard_map/ppermute | solution.py:36
  402.1 17.5 %collective-permute-start.36 = (bf16[8,64,768]{2,1,0:T(8,128)(2,1)S(1)}, bf16[8,64,768]{2,1,0:T(8,128)(2,1)S(1)}, u32[]{:S(2)}, u32[]{:S(2)}) collective-permute-start(bf16[8,64,768]{2,1,0:T(8,128)(2,1)S(1)} %all-to-all-done.4.a_ref), channel_id=1, source_target_pairs={{0,2},{1,3},{2,0},{3,1},{4,6},{5,7},{6,4},{7,5},{8,10},{9,11},{10,... | collective-permute-start | bytes 2359304 | tf_op jit(solution)/shard_map/ppermute | solution.py:36
  403.6 16.0 %all-to-all-start.5 = ((bf16[8,224,128]{2,1,0:T(8,128)(2,1)}), bf16[8,224,128]{2,1,0:T(8,128)(2,1)}, u32[]{:S(2)}, u32[]{:S(2)}) async-start(bf16[8,224,128]{2,1,0:T(8,128)(2,1)} %convert_add_fusion), calls=%async_computation.5 | async-start | bytes 917504 | tf_op jit(solution)/shard_map/all_to_all | solution.py:1141
  411.9 14.5 %collective-permute-start.37 = (bf16[8,64,768]{2,1,0:T(8,128)(2,1)S(1)}, bf16[8,64,768]{2,1,0:T(8,128)(2,1)S(1)}, u32[]{:S(2)}, u32[]{:S(2)}) collective-permute-start(bf16[8,64,768]{2,1,0:T(8,128)(2,1)S(1)} %all-to-all-done.4.a_ref), channel_id=1, source_target_pairs={{0,1},{1,0},{2,3},{3,2},{4,5},{5,4},{6,7},{7,6},{8,9},{9,8},{10,11... | collective-permute-start | bytes 2359304 | tf_op jit(solution)/shard_map/ppermute | solution.py:36
  419.6 7.7 %collective-permute-start.38 = (bf16[8,64,768]{2,1,0:T(8,128)(2,1)S(1)}, bf16[8,64,768]{2,1,0:T(8,128)(2,1)S(1)}, u32[]{:S(2)}, u32[]{:S(2)}) collective-permute-start(bf16[8,64,768]{2,1,0:T(8,128)(2,1)S(1)} %collective-permute-done.36.b_ref), channel_id=1, source_target_pairs={{0,1},{1,0},{2,3},{3,2},{4,5},{5,4},{6,7},{7,6},{8,9},{9,8},{10,11... | collective-permute-start | bytes 2359304 | tf_op jit(solution)/shard_map/ppermute | solution.py:36
  (126 other events, 733.7 us)

commit v3 on v2

--- a/solution.py
+++ b/solution.py
@@ -159,7 +159,7 @@
         out_specs=[cut(o) for o in outs] + [whole(o) for o in sums],
         out_shape=[*outs, *sums],
         cost_estimate=cost(size),
-        compiler_params=room(ROOM),
+        compiler_params=room(60),
         name=name,
     )(*head, *args, *consts)
 
@@ -192,7 +192,7 @@
     return start(copies)
 
 
-def load_rows(info, arrays, b_ref, sems):
+def load_rows(info, arrays, k, b_ref, sems):
     nz = arrays[0].shape[1]
     rows = D // (2 * nz)
     copies = []
@@ -200,15 +200,15 @@
         for z in range(nz):
             copies.append(
                 pltpu.make_async_copy(
-                    a.at[0, z, pl.ds(rows, 8), :], b_ref.at[info[0] ^ (2 * z + x)], sems.at[len(copies)]
+                    a.at[k, z, pl.ds(rows, b_ref.shape[1]), :], b_ref.at[info[0] ^ (2 * z + x)], sems.at[len(copies)]
                 )
             )
     return start(copies)
 
 
-def load_weight(info, arrays, w_ref, sems):
+def load_weight(info, arrays, k, w_ref, sems):
     if len(arrays) == 2:
-        return start([pltpu.make_async_copy(a.at[0], w_ref.at[i], sems.at[i]) for i, a in enumerate(arrays)])
+        return start([pltpu.make_async_copy(a.at[k], w_ref.at[i], sems.at[i]) for i, a in enumerate(arrays)])
     nz = arrays[0].shape[1]
     rows = D // (2 * nz)
     copies = []
@@ -217,7 +217,7 @@
             at = pl.multiple_of((info[0] ^ (2 * z + i % 2)) * rows, 16)
             copies.append(
                 pltpu.make_async_copy(
-                    a.at[0, z, pl.ds(0, rows), :], w_ref.at[i // 2, pl.ds(at, rows), :], sems.at[len(copies)]
+                    a.at[k, z, pl.ds(0, rows), :], w_ref.at[i // 2, pl.ds(at, rows), :], sems.at[len(copies)]
                 )
             )
     return start(copies)
@@ -236,10 +236,27 @@
 def gather_lines(local):
     k, rows, n = local.shape
     cur = local[:, None]
-    for masks in bit_groups(lax.axis_size("dp")):
+    *groups, last = bit_groups(lax.axis_size("dp"))
+    for masks in groups:
         parts = [cur] + [hop(cur, b, 0) for b in masks[1:]]
         cur = jnp.stack(parts, 2).reshape(k, -1, rows, n)
-    return cur, parts[1:]
+    return [cur] + [hop(cur, b, 0) for b in last[1:]]
+
+
+def gather_doubling(local, *others):
+    k, rows, n = local.shape
+    cur, got = local[:, None], []
+    bit = lax.axis_size("dp") // 2
+    while bit > 1:
+        got.append(hop(cur, bit, 0))
+        cur = jnp.stack([cur, got[-1]], 2).reshape(k, -1, rows, n)
+        bit //= 2
+    return cur, got
+
+
+def join_lines(parts):
+    k, _, rows, n = parts[0].shape
+    return jnp.stack(parts, 2).reshape(k, -1, rows, n)
 
 
 def gather_planes(cur, fast):
@@ -322,10 +339,14 @@
 
 
 def finish_lines(sums):
-    own, *send = sums
-    for z, piece in enumerate(send, 1):
-        own = own + hop(piece, 2 * z, 0).astype(F32)
-    return own
+    own, low, *high = sums
+    if len(high) != 2:
+        for z, piece in enumerate([low, *high], 1):
+            own = own + hop(piece, 2 * z, 0).astype(F32)
+        return own
+    got = hop(jnp.stack([low, high[1]]), 2, 0)
+    send = (high[0].astype(F32) + got[1].astype(F32)).astype(BF)
+    return own + got[0].astype(F32) + hop(send, 4, 0).astype(F32)
 
 
 def bias_rows(b, first, count, low, high):
@@ -341,12 +362,12 @@
     copies = load_pair(info, arrays, w_ref, w_sems)
     hw = nh * HS
     if len(arrays) == 2:
-        wait(load_rows(info, arrays, b_ref, b_sems))
+        wait(load_rows(info, arrays, 0, b_ref, b_sems))
         nd = b_ref.shape[0]
         w = 2 * HS // nd
 
         def bias_part(first):
-            return [b_ref[a, 0:1, h * w : h * w + w] for h in range(nh) for a in range(first, first + nd // 2)]
+            return [b_ref[a, h : h + 1, :w] for h in range(nh) for a in range(first, first + nd // 2)]
 
         q_part, v_part = (
             jnp.concatenate(bias_part(a), axis=1).astype(F32) for a in (0, nd // 2)
@@ -403,7 +424,7 @@
         [
             pltpu.SemaphoreType.DMA((count,)),
             pltpu.VMEM((4 * HS, n), F32),
-            pltpu.VMEM((count, 8, D), BF),
+            pltpu.VMEM((count, 16, D), BF),
             pltpu.SemaphoreType.DMA((count,)),
         ],
         "attn_fwd",
@@ -465,12 +486,12 @@
 
 def ffn_up_kernel(nh, nr, info, x_ref, b0_ref, b1_ref, *rest):
     *up, act_ref, slope_ref, up_ref, sems, r0_ref, r1_ref, r_sems = rest
-    copies = load_weight(info, up, up_ref, sems)
+    copies = load_weight(info, up, 0, up_ref, sems)
     fw = nr * HS
     x = x_ref[...]
     if len(up) == 4:
         for i, r_ref in enumerate((r0_ref, r1_ref)):
-            wait(load_rows(info, up[2 * i : 2 * i + 2], r_ref, r_sems))
+            wait(load_rows(info, up[2 * i : 2 * i + 2], 0, r_ref, r_sems))
         biases = [hidden_bias(r_ref, nr) for r_ref in (r0_ref, r1_ref)]
     else:
         biases = [bias_rows(b_ref[...].astype(F32), nh, nr, 0, HS) for b_ref in (b0_ref, b1_ref)]
@@ -485,9 +506,9 @@
             slope_ref[:, t] = (phi + pre * (jnp.exp(-0.5 * pre * pre) * (2 * np.pi) ** -0.5)).astype(BF)
 
 
-def product_kernel(info, a_ref, *rest):
+def product_kernel(k, info, a_ref, *rest):
     *w, out_ref, w_ref, sems = rest
-    wait(load_weight(info, w, w_ref, sems))
+    wait(load_weight(info, w, k, w_ref, sems))
     fw = w_ref.shape[2]
     out_ref[...] = (dot(a_ref[:, :fw], w_ref[0], 1, 1) + dot(a_ref[:, fw:], w_ref[1], 1, 1)).astype(out_ref.dtype)
 
@@ -628,7 +649,7 @@
 
 def ffn_back_kernel(info, g_ref, slope_ref, *rest):
     *down, dpre_ref, ub_ref, w_ref, sems = rest
-    copies = load_weight(info, down, w_ref, sems)
+    copies = load_weight(info, down, 1, w_ref, sems)
     fw = w_ref.shape[2]
     g = g_ref[...]
     ub_ref[...] = jnp.zeros(ub_ref.shape, F32)
@@ -649,7 +670,37 @@
         for y in range(2):
             s = slice(y * fw, (y + 1) * fw)
             g = dot(a0[...], b0[:, s], 0, 0) + dot(a1[...], b1[:, s], 0, 0)
-            store_grad(info, k, y, g, g_ref, outs)
+            if len(outs) == 2:
+                outs[y][k] = g.astype(BF)
+                continue
+            g_ref[...] = g
+            nz = outs[0].shape[1]
+            rows = D // (2 * nz)
+            for z in range(nz):
+                for x in range(2):
+                    at = pl.multiple_of((info[0] ^ (2 * z + x)) * rows, 8)
+                    piece = g_ref[pl.ds(at, rows), :].astype(BF)
+                    if k == 0:
+                        outs[y][x, z] = piece
+                    else:
+                        outs[2 + x][y, z] = piece
+
+
+def sum_half_kernel(a_ref, ga_ref, b_ref, gb_ref, keep_ref, sa_ref, sb_ref):
+    for k, (r, g, send_ref) in enumerate(((a_ref, ga_ref, sa_ref), (b_ref, gb_ref, sb_ref))):
+        for z in range(r.shape[1]):
+            keep_ref[k, z] = (r[0, z].astype(F32) + g[0, z].astype(F32)).astype(BF)
+            send_ref[z] = (r[1, z].astype(F32) + g[1, z].astype(F32)).astype(BF)
+
+
+def sum_last_kernel(keep_ref, a_ref, b_ref, own_ref, *send_refs):
+    for k, g in enumerate((a_ref, b_ref)):
+        for z in range(keep_ref.shape[1]):
+            total = keep_ref[k, z].astype(F32) + g[z].astype(F32)
+            if z == 0:
+                own_ref[k] = total
+            else:
+                send_refs[z - 1][k] = total.astype(BF)
 
 
 def ln1_back_kernel(part_ref, got_ref, dr2_ref, n_ref, s_ref, wide_ref, dr1_ref, low_ref, vec_ref):
@@ -795,6 +846,31 @@
     return jnp.pad(x, ((0, 0), (0, 128 - x.shape[1])))
 
 
+def vectors_kernel(sizes, info, a0, a1, wide_ref, narrow_ref, b_ref, sems):
+    rows, cr, nh, _ = sizes
+    wait(load_rows(info, [a0, a1], 0, b_ref, sems))
+    nd = b_ref.shape[0]
+    for out_ref, row, count, width in ((wide_ref, nh, 6, rows), (narrow_ref, nh + 6, 3, cr)):
+        out_ref[...] = jnp.zeros(out_ref.shape, F32)
+        for i in range(count):
+            cuts = [b_ref[a, row + i : row + i + 1, :width] for a in range(nd)]
+            out_ref[i : i + 1] = jnp.concatenate(cuts, axis=1).astype(F32)
+
+
+def matrices_kernel(info, a0, a1, sw_ref, pooler_ref, class_ref, b_ref, c_ref, sems):
+    copies = load_rows(info, [a0, a1], 0, b_ref, sems.at[0])
+    copies += load_rows(info, [a0, a1], 1, c_ref, sems.at[1])
+    wait(copies)
+    for a in range(b_ref.shape[0]):
+        for i in range(2):
+            at = slice(16 * a + 8 * i, 16 * a + 8 * i + 8)
+            pooler_ref[at] = b_ref[a, 8:16, 128 * i : 128 * i + 128].astype(F32)
+            class_ref[at] = b_ref[a, 8:16, 256 + 128 * i : 384 + 128 * i].astype(F32)
+        for i in range(6):
+            at = 96 * a + 16 * i
+            sw_ref[at : at + 16] = c_ref[a, :, 128 * i : 128 * i + 128]
+
+
 def unpack_kernel(sizes, in_ref, sw_ref, pooler_ref, class_ref, wide_ref, narrow_ref, bias_ref):
     rows, cr, nh, nr = sizes
     nd = in_ref.shape[0]
@@ -891,7 +967,7 @@
     rows, cr = D // nd, CW // nd
     nh, nr = qv_bias.shape[0], up_bias.shape[0]
     hw, fw = nh * HS, nr * HS
-    fast = rows % 16 == 0 and len(bit_groups(nd)) == 1
+    fast = nd == 8
     sizes = (rows, cr, nh, nr)
     seq = 2 * me + y
     length = lengths[seq]
@@ -921,41 +997,26 @@
 
     qo = jnp.concatenate([jnp.transpose(qkv_weight, (1, 0, 2)).reshape(rows, 3 * hw), out_weight.T], axis=1)
     if fast:
-        row = jnp.pad(qv_bias.reshape(1, -1), ((0, 7), (0, D - qv_bias.size)))
-        qo = jnp.concatenate([qo, row], axis=0)
-    qo_line, _ = gather_lines(qo[None])
+        vectors = [qv_bias]
+        vectors += [v[None] for v in (out_bias, norm1_gain, norm1_bias, down_bias, norm2_gain, norm2_bias)]
+        vectors += [v[None] for v in (student_bias, pool_query, pooler_bias)]
+        vectors = [jnp.pad(v, ((0, 0), (0, 128 - v.shape[1]))) for v in vectors]
+        vectors = jnp.concatenate([*vectors, jnp.zeros((7 - nh, 128), BF)], axis=0)
+        qo = jnp.concatenate([qo, jnp.pad(vectors, ((0, 0), (0, D - 128)))], axis=0)
+    qo_line = join_lines(gather_lines(qo[None]))
     tokens = deal(after(hidden_in, qo_line))
     w_qo = gather_planes(qo_line, fast)
     w_qo = (w_qo[:2], w_qo[2:]) if fast else (w_qo[:1], w_qo[1:])
-    up_pack = up_weight
+    up_pack, down_pack = up_weight, down_weight.T
     if fast:
         row = jnp.pad(up_bias.reshape(1, -1), ((0, 7), (0, D - up_bias.size)))
-        up_pack = jnp.concatenate([up_weight, row], axis=0)
-    up_line, up_got = gather_lines(after(up_pack, qo_line)[None])
-    w_up = gather_planes(up_line, fast)
-    down_line, down_got = gather_lines(after(down_weight.T, up_line)[None])
-    small = jnp.concatenate(
-        [student_weight, pooler_weight]
-        + [
-            lanes(v)
-            for v in (
-                class_weight,
-                out_bias,
-                norm1_gain,
-                norm1_bias,
-                down_bias,
-                norm2_gain,
-                norm2_bias,
-                student_bias,
-                pool_query,
-                pooler_bias,
-                qv_bias,
-                up_bias,
-            )
-        ],
-        axis=0,
-    )
-    small = jnp.pad(small, ((0, -small.shape[0] % 16), (0, 0)))
+        cls = lanes(class_weight)
+        more = jnp.concatenate([pooler_weight[:8], pooler_weight[8:], cls[:8], cls[8:]], axis=1)
+        more = jnp.pad(more, ((0, 0), (0, D - 512)))
+        up_pack = jnp.concatenate([up_pack, row, more], axis=0)
+        more = jnp.concatenate([student_weight[16 * i : 16 * i + 16] for i in range(6)], axis=1)
+        down_pack = jnp.concatenate([down_pack, more], axis=0)
+    f_line, f_got = gather_doubling(after(jnp.stack([up_pack, down_pack]), qo_line))
     class_b = lanes(class_bias.astype(F32))
     cot = deal(cotangent)
 
@@ -968,7 +1029,7 @@
     ).astype(BF)
     aux_own = aux[:half]
 
-    sib = hop(after(tokens, w_qo, up_got), 0, 1)
+    sib = hop(after(tokens, w_qo, f_got[0]), 0, 1)
     n = 2 * half
     biases = [aux, aux]
     if not fast:
@@ -978,20 +1039,53 @@
         piece = jnp.pad(piece, ((0, 16 - nh), (0, 0)))
         biases = [piece, hop(piece, 0, 2)]
     proj0, w0, ctx0, lse0 = attn_fwd(nh, info, tokens, sib, biases[0], aux, w_qo[0])
-    small = lax.all_to_all(jnp.broadcast_to(after(small, ctx0)[None], (nd, *small.shape)), "dp", 0, 0, tiled=True)
-    student_w, pooler_f, class_f, wide, narrow, bias_near = call(
-        functools.partial(unpack_kernel, sizes),
-        [sds((D, CW), BF), sds((CW, CW)), sds((CW, CW)), sds((8, D)), sds((8, CW)), sds((16, 128))],
-        [small],
-        name="unpack",
-    )
-    bias_near = bias_near.astype(BF)
-    bias_far = bias_near if fast else hop(bias_near, 0, 2)
-    proj1, w1, ctx1, lse1 = attn_fwd(nh, info, tokens, sib, biases[1], after(aux, down_got, ctx0), w_qo[1])
-    w_down = gather_planes(after(down_line, ctx0), fast)
-
     if fast:
-        ctx1 = after(ctx1, w_up, w_down[1:3], student_w)
+        wide, narrow = call(
+            functools.partial(vectors_kernel, sizes),
+            [sds((8, D)), sds((8, CW))],
+            [info, *w_qo[0]],
+            [SMEM, ANY, ANY],
+            [pltpu.VMEM((nd, 16, D), BF), pltpu.SemaphoreType.DMA((nd,))],
+            "vectors",
+        )
+        bias_near = bias_far = aux
+    else:
+        small = jnp.concatenate(
+            [student_weight, pooler_weight]
+            + [
+                lanes(v)
+                for v in (
+                    class_weight,
+                    out_bias,
+                    norm1_gain,
+                    norm1_bias,
+                    down_bias,
+                    norm2_gain,
+                    norm2_bias,
+                    student_bias,
+                    pool_query,
+                    pooler_bias,
+                    qv_bias,
+                    up_bias,
+                )
+            ],
+            axis=0,
+        )
+        small = jnp.pad(small, ((0, -small.shape[0] % 16), (0, 0)))
+        small = lax.all_to_all(jnp.broadcast_to(small[None], (nd, *small.shape)), "dp", 0, 0, tiled=True)
+        student_w, pooler_f, class_f, wide, narrow, bias_near = call(
+            functools.partial(unpack_kernel, sizes),
+            [sds((D, CW), BF), sds((CW, CW)), sds((CW, CW)), sds((8, D)), sds((8, CW)), sds((16, 128))],
+            [small],
+            name="unpack",
+        )
+        bias_near = bias_near.astype(BF)
+        bias_far = hop(bias_near, 0, 2)
+    proj1, w1, ctx1, lse1 = attn_fwd(nh, info, tokens, sib, biases[1], after(aux, ctx0), w_qo[1])
+    w_ffn = gather_planes(f_line, fast)
+
+    if fast:
+            ctx1 = after(ctx1, wide)
 
     def out(first, kind):
         return call(
@@ -1008,34 +1102,44 @@
         [wide],
         name="ln1",
     )
-    first_sib = hop(first_low, 0, 1)
+    first_sib = hop(after(first_low, w_ffn), 0, 1)
+
+    if fast:
+        student_w, pooler_f, class_f = call(
+            matrices_kernel,
+            [sds((D, CW), BF), sds((CW, CW)), sds((CW, CW))],
+            [info, *w_ffn[:2]],
+            [SMEM, ANY, ANY],
+            [pltpu.VMEM((nd, 16, D), BF)] * 2 + [pltpu.SemaphoreType.DMA((2, nd))],
+            "matrices",
+        )
 
     def ffn_up(x):
         return call(
             functools.partial(ffn_up_kernel, nh, nr),
             [sds((half, 2 * fw), BF), sds((half, 2 * fw), BF)],
-            [info, x, bias_near, bias_far, *w_up],
-            [SMEM] + [None] * 3 + [ANY] * len(w_up),
-            weight_scratch(w_up)
+            [info, x, bias_near, bias_far, *w_ffn],
+            [SMEM] + [None] * 3 + [ANY] * len(w_ffn),
+            weight_scratch(w_ffn)
             + [pltpu.VMEM((max(nd, 8), 8, D), BF)] * 2
             + [pltpu.SemaphoreType.DMA((nd,))],
             "ffn_up",
         )
 
-    def product(a, w, kind):
+    def product(a, k, kind):
         return call(
-            product_kernel,
+            functools.partial(product_kernel, k),
             [sds((half, D), kind)],
-            [info, a, *w],
-            [SMEM, None] + [ANY] * len(w),
-            weight_scratch(w),
+            [info, a, *w_ffn],
+            [SMEM, None] + [ANY] * len(w_ffn),
+            weight_scratch(w_ffn),
             "product",
         )[0]
 
     act, slope = ffn_up(first_low)
     act_sib, slope_sib = ffn_up(after(first_sib, act))
-    ffn_got = hop(product(act_sib, w_down, BF), 0, 1)
-    ffn_part = product(act, w_down, F32)
+    ffn_got = hop(product(act_sib, 1, BF), 0, 1)
+    ffn_part = product(act, 1, F32)
     second_low, n2, s2, student, pool_logit, stat = by_rows(
         ln2_kernel,
         [sds((half, D), BF), sds((half, D)), sds((half, 1)), sds((half, CW)), sds((half, CW))],
@@ -1070,16 +1174,16 @@
         return call(
             ffn_back_kernel,
             [sds((half, 2 * fw), BF), sds((8, 2 * fw))],
-            [info, g, s, *w_down],
-            [SMEM, None, None] + [ANY] * len(w_down),
-            weight_scratch(w_down),
+            [info, g, s, *w_ffn],
+            [SMEM, None, None] + [ANY] * len(w_ffn),
+            weight_scratch(w_ffn),
             "ffn_back",
         )
 
     dpre, ub0 = ffn_back(dffn, slope)
     dpre_sib, ub1 = ffn_back(after(dffn_sib, dpre, hidden_a), slope_sib)
-    dfirst_got = hop(product(dpre_sib, w_up, BF), 0, 1)
-    dfirst_part = product(dpre, w_up, F32)
+    dfirst_got = hop(product(dpre_sib, 0, BF), 0, 1)
+    dfirst_part = product(dpre, 0, F32)
     f_grads = call(
         ffn_grad_kernel,
         grad_outs(2, 2, nd, rows, fast),
@@ -1098,7 +1202,9 @@
     )
     dattn_sib = hop(dattn, 0, 1)
     dattn_sib = after(dattn_sib, f_grads, hidden_b)
-    f_parts = sum_planes(f_grads)
+    if fast:
+        up_keep, up_send, down_keep, down_send = f_grads
+        up_got, down_got = hop(up_send, 0, 2), hop(down_send, 1, 0)
     count = rows + 2 * cr + 9 + 4 * nr + 2 * total
     (small_g,) = call(
         functools.partial(pack_grads_kernel, sizes),
@@ -1129,23 +1235,39 @@
         nh, proj0, w0, aux, ctx0, dattn, after(dattn_sib, g1, far_grad), lse0
     )
     if fast:
-        g0, f_parts[1], f_parts[2], far_got = lax.optimization_barrier((g0, f_parts[1], f_parts[2], far_got))
-        far_part = (far_grad[0].astype(F32) + far_got.astype(F32)).astype(BF)
+        g0, up_got, down_got = lax.optimization_barrier((g0, up_got, down_got))
     tok_send, tok_own = call(
         token_grad_kernel, [sds((half, D), BF), sds((half, D))], [g0, g1, w0, w1, dr1], name="token_grad"
     )
     near_grad = qkv_grad(g0, ctx0, g0_sum)
     tok_sum = after((tok_own + hop(tok_send, 0, 1).astype(F32)).astype(BF), near_grad)
     input_a = undeal(tok_sum)
-    f_sums = sum_blocks(f_parts)
-    small_g = lax.all_to_all(after(small_y.astype(BF), input_a), "dp", 0, 0, tiled=True).astype(F32).sum(0)
-    hidden_out = place(after(hidden_a, f_sums), hidden_b)
-    input_grad = place(input_a, hop(after(input_a, hidden_out), 0, 2))
-    f_sum = finish_lines(f_sums) if fast else sum_lines(f_parts)
+    if fast:
+        block_ = (nd // 2, rows, D)
+        f_keep, up_half, down_half = call(
+            sum_half_kernel,
+            [sds((2, *block_), BF), sds(block_, BF), sds(block_, BF)],
+            [up_keep, up_got, down_keep, down_got],
+            name="grad_half",
+        )
+        f_sums = call(
+            sum_last_kernel,
+            [sds((2, rows, D))] + [sds((2, rows, D), BF)] * (nd // 2 - 1),
+            [f_keep, hop(up_half, 1, 0), hop(down_half, 0, 2)],
+            name="grad_sum",
+        )
+        f_sum = finish_lines(f_sums)
+        far_part = (far_grad[0].astype(F32) + far_got.astype(F32)).astype(BF)
+        qo_own = (near_grad[0], hop(near_grad[1], 1, 0), hop(far_part, 0, 2))
+    else:
+        qo_own = ()
+        f_sums = f_sum = sum_lines(f_grads)
+    hidden_out = place(hidden_a, hidden_b)
+    input_b = hop(after(input_a, hidden_out, f_sums, qo_own[1:]), 0, 2)
+    small_g = lax.all_to_all(after(small_y.astype(BF), input_b), "dp", 0, 0, tiled=True).astype(F32).sum(0)
+    input_grad = place(input_a, input_b)
     up_sum, down_sum = f_sum
     if fast:
-        qo_own = (near_grad[0], hop(near_grad[1], 1, 0), hop(far_part, 0, 2))
-        qo_own = (after(qo_own[0], f_sum), *qo_own[1:])
         qo_sum = finish_lines(sum_blocks(qo_own))[0]
     else:
         qo_sum = sum_lines([*near_grad, *far_grad])[0]

time: 443 us -> 426 us (0.962)
  starting transfers between devices: 94.4 us -> 72.1 us
  Pallas kernels: 130 us -> 143 us
  waiting for transfers between devices: 122 us -> 113 us
  other arithmetic: 16.2 us -> 21.5 us
    ppermute x47 -> x39, starting transfers between devices: 55.7 us -> 35.1 us  [hop(): return lax.ppermute(x, AXES, pairs)]
    unnamed x279 -> x216, local copies, waits for them, and re-layouts: 59.7 us -> 44.4 us
    ppermute x47 -> x39, waiting for transfers between devices: 122 us -> 112 us  [hop(): return lax.ppermute(x, AXES, pairs)]
    pallas_call x4, Pallas kernels: 14.6 us -> 24 us  [by_rows(): pl.pallas_call(kernel, grid=(n // RB,), in_specs=[SMEM] * len(head) + [cu...]
    pad x13 -> x10, local copies, waits for them, and re-layouts: 0.09 us -> 6.64 us  [body(): vectors = [jnp.pad(v, ((0, 0), (0, 128 - v.shape[1]))) for v in vectors]]
    pallas_call x22 -> x24, Pallas kernels: 106 us -> 109 us  [call(): pl.pallas_call(kernel, in_specs=specs, out_specs=[pl.BlockSpec(memory_spa...]
  transfers between devices with their start and end apart: 53 -> 44, of which waited for: 20 -> 17; matrix products, arithmetic and copies ran while one was open for 6% -> 8% of each run, Pallas kernels for 26% -> 30%
where the time goes in v3:
time: 426 us; the launch traced here: 420 us
  Pallas kernels  143 us (34%)
  waiting for transfers between devices  113 us (27%)
  starting transfers between devices  72.1 us (17%)
  local copies, waits for them, and re-layouts  67.4 us (16%)
  other arithmetic  21.5 us (5%)
    ppermute x39, waiting for transfers between devices, hop(): return lax.ppermute(x, AXES, pairs)  112 us
    pallas_call x24, Pallas kernels, call(): pl.pallas_call(kernel, in_specs=specs, out_specs=[pl.BlockSpec(memory_spa...  109 us
    unnamed x216, local copies, waits for them, and re-layouts  44.4 us
    ppermute x39, starting transfers between devices, hop(): return lax.ppermute(x, AXES, pairs)  35.1 us
    pallas_call x4, Pallas kernels, by_rows(): pl.pallas_call(kernel, grid=(n // RB,), in_specs=[SMEM] * len(head) + [cu...  24 us
    all_to_all x2, starting transfers between devices, deal(): return lax.all_to_all(x, 'dp', 0, 0, tiled=True).reshape(half, D)  22.3 us
    all_to_all x2, starting transfers between devices, undeal(): return lax.all_to_all(x.reshape(nd, hp, D), 'dp', 0, 0, tiled=True)  10.2 us
    pallas_call x2, Pallas kernels, place(): pl.pallas_call(place_kernel, grid=(nd,), in_specs=[SMEM] + [one] * 4, out...  9.4 us
  transfers between devices with their start and end apart: 44, of which 17 were waited for; matrix products, arithmetic and copies ran while one was open for 8% of the time, Pallas kernels for 30%

profile of v3, /device:TPU:0, one launch (start us, length us, event | category | flops | bytes accessed | tf_op | source)
XLA Modules:
  0.0 420.1 jit_solution(18122626798344589395)
XLA Ops:
  10.4 3.0 collective-permute-start
  13.4 2.6 collective-permute-start.1
  20.7 8.6 %collective-permute-done.1 = bf16[1,1,112,768]{3,2,1,0:T(8,128)(2,1)} collective-permute-done((bf16[1,1,112,768]{3,2,1,0:T(8,128)(2,1)}, bf16[1,1,112,768]{3,2,1,0:T(8,128)(2,1)}, u32[]{:S(2)}, u32[]{:S(2)}) %collective-permute-start.1) | collective-permute-done | bytes 172064 | tf_op jit(solution)/shard_map/ppermute | solution.py:36
  29.3 1.9 maximum_bitcast_fusion.rest_0_.a0
  32.2 6.2 %all-to-all-start = ((bf16[8,64,768]{2,1,0:T(8,128)(2,1)}), bf16[8,64,768]{2,1,0:T(8,128)(2,1)S(1)}, u32[]{:S(2)}, u32[]{:S(2)}) async-start(bf16[8,64,768]{2,1,0:T(8,128)(2,1)} %dynamic-slice_bitcast_fusion.1), calls=%async_computation | async-start | bytes 1572864 | tf_op jit(solution)/shard_map/all_to_all | solution.py:979
  38.4 1.3 constant_dynamic-update-slice_fusion.1
  41.8 2.1 collective-permute-start.3
  43.9 1.5 collective-permute-start.4
  45.4 2.9 collective-permute-start.6
  48.4 24.0 %collective-permute-done.6 = bf16[2,1,112,768]{3,2,0,1:T(8,128)(2,1)S(1)} collective-permute-done((bf16[2,1,112,768]{3,2,0,1:T(8,128)(2,1)S(1)}, bf16[2,1,112,768]{3,2,0,1:T(8,128)(2,1)S(1)}, u32[]{:S(2)}, u32[]{:S(2)}) %collective-permute-start.6) | collective-permute-done | bytes 344096 | tf_op jit(solution)/shard_map/ppermute | solution.py:36
  75.6 3.8 collective-permute-done.5.rest_1_
  82.6 6.6 %collective-permute-done.9 = bf16[2,2,112,768]{3,2,0,1:T(8,128)(2,1)} collective-permute-done((bf16[2,2,112,768]{3,2,0,1:T(8,128)(2,1)}, bf16[2,2,112,768]{3,2,0,1:T(8,128)(2,1)}, u32[]{:S(2)}, u32[]{:S(2)}) %collective-permute-start.9) | collective-permute-done | bytes 688160 | tf_op jit(solution)/shard_map/ppermute | solution.py:36
  90.6 2.0 collective-permute-start.10
  92.6 1.5 collective-permute-start.11
  94.2 12.6 %attn_fwd.2 = (bf16[1024,640]{1,0:T(8,128)(2,1)S(1)}, bf16[768,768]{1,0:T(8,128)(2,1)S(1)}, bf16[1024,256]{1,0:T(8,128)(2,1)S(1)}, f32[8,1024]{1,0:T(8,128)S(1)}) custom-call(s32[4]{0:T(128)S(1)} %pad_add_fusion.info, bf16[512,768]{1,0:T(8,128)(2,1)S(1)} %bitcast.122, bf16[512,768]{1,0:T(8,128)(2,1)S(1)} %collective-permute-done.7.sib_ref.x1, ...), custom_call_target="tpu_custom_call" | custom-call | flops 11000000512 | bytes 6520848 | tf_op jit(solution)/shard_map/attn_fwd/pallas_call | solution.py:124
  107.9 12.8 %attn_fwd.3 = (bf16[1024,640]{1,0:T(8,128)(2,1)S(1)}, bf16[768,768]{1,0:T(8,128)(2,1)S(1)}, bf16[1024,256]{1,0:T(8,128)(2,1)S(1)}, f32[8,1024]{1,0:T(8,128)S(1)}) custom-call(s32[4]{0:T(128)S(1)} %pad_add_fusion.info, bf16[512,768]{1,0:T(8,128)(2,1)S(1)} %bitcast.123, bf16[512,768]{1,0:T(8,128)(2,1)S(1)} %collective-permute-done.7.sib_ref.x1, ...), custom_call_target="tpu_custom_call" | custom-call | flops 11000000512 | bytes 6520848 | tf_op jit(solution)/shard_map/attn_fwd/pallas_call | solution.py:124
  125.1 5.1 %ln1.1 = (f32[512,768]{1,0:T(8,128)}, bf16[512,768]{1,0:T(8,128)(2,1)}, f32[512,768]{1,0:T(8,128)}, f32[512,1]{1,0:T(8,128)}, f32[1,128]{1,0:T(1,128)}) custom-call(f32[512,768]{1,0:T(8,128)} %copy-done.10, bf16[512,768]{1,0:T(8,128)(2,1)} %copy-done.92, bf16[512,768]{1,0:T(8,128)(2,1)} %bitcast.124, bf16[512,128]{1,0:T(8,128)(2,1)} %slice.159.aux_ref, ...), custom_call_target="tpu_custom_call" | custom-call | bytes 3301376 | tf_op jit(solution)/shard_map/ln1/pallas_call | solution.py:155
  130.2 21.5 %collective-permute-done.11.rest_2_ = bf16[2,4,112,768]{3,2,1,0:T(8,128)(2,1)} collective-permute-done((bf16[2,4,112,768]{3,2,1,0:T(8,128)(2,1)S(1)}, bf16[2,4,112,768]{3,2,1,0:T(8,128)(2,1)}, u32[]{:S(2)}, u32[]{:S(2)}) %collective-permute-start.11) | collective-permute-done | bytes 1376288 | tf_op jit(solution)/shard_map/ppermute | solution.py:36
  151.7 2.1 dynamic-slice_bitcast_fusion
  153.9 16.1 %all-to-all-start.1 = ((bf16[8,64,768]{2,1,0:T(8,128)(2,1)}), bf16[8,64,768]{2,1,0:T(8,128)(2,1)}, u32[]{:S(2)}, u32[]{:S(2)}) async-start(bf16[8,64,768]{2,1,0:T(8,128)(2,1)} %dynamic-slice_bitcast_fusion), calls=%async_computation.1 | async-start | bytes 1572864 | tf_op jit(solution)/shard_map/all_to_all | solution.py:979
  171.1 6.1 %ffn_up.2 = (bf16[512,1536]{1,0:T(8,128)(2,1)S(1)}, bf16[512,1536]{1,0:T(8,128)(2,1)S(1)}) custom-call(s32[4]{0:T(128)S(1)} %pad_add_fusion.info, bf16[512,768]{1,0:T(8,128)(2,1)S(1)} %copy-done.29, bf16[1024,128]{1,0:T(8,128)(2,1)S(1)} %copy-done.9, bf16[1024,128]{1,0:T(8,128)(2,1)S(1)} %copy-done.9, bf16[2,4,112,768]{3,2,1,0:T(8,128)(2,1)S(1)} %bitcast.112, ...), custom_call_target="tpu_custom_call" | custom-call | bytes 9961488 | tf_op jit(solution)/shard_map/ffn_up/pallas_call | solution.py:124
  179.6 6.7 %ffn_up.3 = (bf16[512,1536]{1,0:T(8,128)(2,1)S(1)}, bf16[512,1536]{1,0:T(8,128)(2,1)S(1)}) custom-call(s32[4]{0:T(128)S(1)} %pad_add_fusion.info, bf16[512,768]{1,0:T(8,128)(2,1)} %collective-permute-done.13.x_ref.first2, bf16[1024,128]{1,0:T(8,128)(2,1)S(1)} %copy-done.9, bf16[1024,128]{1,0:T(8,128)(2,1)S(1)} %copy-done.9, ...), custom_call_target="tpu_custom_call" | custom-call | bytes 9961488 | tf_op jit(solution)/shard_map/ffn_up/pallas_call | solution.py:124
  187.5 5.9 %product.5 = bf16[512,768]{1,0:T(8,128)(2,1)} custom-call(s32[4]{0:T(128)S(1)} %pad_add_fusion.info, bf16[512,1536]{1,0:T(8,128)(2,1)S(1)} %get-tuple-element.124.a_ref.act2, bf16[2,4,112,768]{3,2,1,0:T(8,128)(2,1)S(1)} %bitcast.114, bf16[2,4,112,768]{3,2,1,0:T(8,128)(2,1)S(1)} %collective-permute-done.10.rest_1_.a1, ...), custom_call_target="tpu_custom_call" | custom-call | bytes 7864336 | tf_op jit(solution)/shard_map/product/pallas_call | solution.py:124
  195.8 1.4 copy-done.12
  197.2 5.0 %product.4.part_ref = f32[512,768]{1,0:T(8,128)S(1)} custom-call(s32[4]{0:T(128)S(1)} %pad_add_fusion.info, bf16[512,1536]{1,0:T(8,128)(2,1)S(1)} %copy-done.12, bf16[2,4,112,768]{3,2,1,0:T(8,128)(2,1)S(1)} %bitcast.116, bf16[2,4,112,768]{3,2,1,0:T(8,128)(2,1)S(1)} %collective-permute-done.10.rest_1_.a1, ...), custom_call_target="tpu_custom_call" | custom-call | bytes 8650768 | tf_op jit(solution)/shard_map/product/pallas_call | solution.py:124
  203.4 5.9 %ln2.1 = (bf16[512,768]{1,0:T(8,128)(2,1)}, f32[512,768]{1,0:T(8,128)}, f32[512,1]{1,0:T(8,128)}, f32[512,128]{1,0:T(8,128)}, f32[512,128]{1,0:T(8,128)}, /*index=5*/f32[8,128]{1,0:T(8,128)}) custom-call(f32[512,768]{1,0:T(8,128)} %copy-done.21, bf16[512,768]{1,0:T(8,128)(2,1)} %collective-permute-done.14.got_ref, f32[512,768]{1,0:T(8,128)} %get-tuple-element.126.first_ref, ...), custom_call_target="tpu_custom_call" | custom-call | bytes 4288512 | tf_op jit(solution)/shard_map/ln2/pallas_call | solution.py:155
  209.3 5.8 %all-to-all-start.2 = ((bf16[8,64,768]{2,1,0:T(8,128)(2,1)}), bf16[8,64,768]{2,1,0:T(8,128)(2,1)}, u32[]{:S(2)}, u32[]{:S(2)}) async-start(bf16[8,64,768]{2,1,0:T(8,128)(2,1)} %bitcast.131), calls=%async_computation.2 | async-start | bytes 1572864 | tf_op jit(solution)/shard_map/all_to_all | solution.py:982
  216.9 7.4 %head.1 = (f32[512,768]{1,0:T(8,128)}, bf16[512,768]{1,0:T(8,128)(2,1)}, f32[768,128]{1,0:T(8,128)}, f32[128,128]{1,0:T(8,128)}, f32[128,128]{1,0:T(8,128)}, /*i...) custom-call(s32[4]{0:T(128)} %copy-done.65, f32[512,128]{1,0:T(8,128)} %get-tuple-element.130.st_ref, ...), custom_call_target="tpu_custom_call" | custom-call | bytes 4037632 | tf_op jit(solution)/shard_map/head/pallas_call | solution.py:155
  225.8 1.4 copy-done.45
  227.2 5.0 %ffn_back.2 = (bf16[512,1536]{1,0:T(8,128)(2,1)S(1)}, f32[8,1536]{1,0:T(8,128)S(1)}) custom-call(s32[4]{0:T(128)S(1)} %copy-done.66, bf16[512,768]{1,0:T(8,128)(2,1)S(1)} %copy-done.34, bf16[512,1536]{1,0:T(8,128)(2,1)S(1)} %copy-done.45, bf16[2,4,112,768]{3,2,1,0:T(8,128)(2,1)S(1)} %bitcast.117, ...), custom_call_target="tpu_custom_call" | custom-call | bytes 9486352 | tf_op jit(solution)/shard_map/ffn_back/pallas_call | solution.py:124
  234.4 1.6 all-to-all-done.2.a_ref
  238.0 1.4 copy-done.43
  239.4 5.0 %ffn_back.3 = (bf16[512,1536]{1,0:T(8,128)(2,1)S(1)}, f32[8,1536]{1,0:T(8,128)S(1)}) custom-call(s32[4]{0:T(128)S(1)} %copy-done.66, bf16[512,768]{1,0:T(8,128)(2,1)S(1)} %copy-done.37, bf16[512,1536]{1,0:T(8,128)(2,1)S(1)} %copy-done.43, bf16[2,4,112,768]{3,2,1,0:T(8,128)(2,1)S(1)} %bitcast.118, ...), custom_call_target="tpu_custom_call" | custom-call | bytes 9486352 | tf_op jit(solution)/shard_map/ffn_back/pallas_call | solution.py:124
  244.5 5.0 %product.7 = bf16[512,768]{1,0:T(8,128)(2,1)S(1)} custom-call(s32[4]{0:T(128)S(1)} %copy-done.66, bf16[512,1536]{1,0:T(8,128)(2,1)S(1)} %get-tuple-element.146.a_ref.dpre2, bf16[2,4,112,768]{3,2,1,0:T(8,128)(2,1)S(1)} %bitcast.119, bf16[2,4,112,768]{3,2,1,0:T(8,128)(2,1)S(1)} %collective-permute-done.10.rest_1_.a1, ...), custom_call_target="tpu_custom_call" | custom-call | bytes 7864336 | tf_op jit(solution)/shard_map/product/pallas_call | solution.py:124
  249.6 5.0 %product.6.part_ref = f32[512,768]{1,0:T(8,128)S(1)} custom-call(s32[4]{0:T(128)S(1)} %copy-done.66, bf16[512,1536]{1,0:T(8,128)(2,1)S(1)} %copy-done.17, bf16[2,4,112,768]{3,2,1,0:T(8,128)(2,1)S(1)} %bitcast.120, bf16[2,4,112,768]{3,2,1,0:T(8,128)(2,1)S(1)} %collective-permute-done.10.rest_1_.a1, bf16[2,4,112,768]{3,2,1,0:T(8,128)(2,1)} %collective-permute-done.11.rest_2_, ...), custom_call_target="tpu_custom_call" | custom-call | bytes 8650768 | tf_op jit(solution)/shard_map/product/pallas_call | solution.py:124
  256.9 5.6 %ln1_back.1 = (f32[512,768]{1,0:T(8,128)}, bf16[512,768]{1,0:T(8,128)(2,1)}, f32[8,768]{1,0:T(8,128)}) custom-call(f32[512,768]{1,0:T(8,128)} %copy-done.22, bf16[512,768]{1,0:T(8,128)(2,1)} %copy-done.93, f32[512,768]{1,0:T(8,128)} %get-tuple-element.148.dr2_ref, f32[512,768]{1,0:T(8,128)} %get-tuple-element.149.n_ref, f32[512,1]{1,0:T(8,128)} %get-tuple-element.150.s_ref, ...), custom_call_target="tpu_custom_call" | custom-call | bytes 5531648 | tf_op jit(solution)/shard_map/ln1_back/pallas_call | solution.py:155
  264.8 1.4 collective-permute-done.21
  269.8 7.0 %ffn_grad.1 = (bf16[2,4,96,768]{3,2,1,0:T(8,128)(2,1)S(1)}, bf16[2,4,96,768]{3,2,1,0:T(8,128)(2,1)S(1)}, bf16[2,4,96,768]{3,2,1,0:T(8,128)(2,1)S(1)}, bf16[2,4,96,768]{3,2,1,0:T(8,128)(2,1)S(1)}) custom-call(s32[4]{0:T(128)S(1)} %copy-done.66, bf16[512,768]{1,0:T(8,128)(2,1)S(1)} %copy-done.30, bf16[512,768]{1,0:T(8,128)(2,1)} %collective-permute-done.13.x_ref.first2, ...), custom_call_target="tpu_custom_call" | custom-call | bytes 14155792 | tf_op jit(solution)/shard_map/ffn_grad/pallas_call | solution.py:124
  277.8 1.4 collective-permute-start.25
  280.2 8.7 %attn_bwd.2 = (bf16[1024,640]{1,0:T(8,128)(2,1)S(1)}, f32[8,640]{1,0:T(8,128)S(1)}) custom-call(bf16[1024,640]{1,0:T(8,128)(2,1)S(1)} %copy-done.85, bf16[768,768]{1,0:T(8,128)(2,1)S(1)} %copy-done.7, bf16[1024,128]{1,0:T(8,128)(2,1)S(1)} %copy-done.9, bf16[1024,256]{1,0:T(8,128)(2,1)S(1)} %copy-done.26, bf16[512,768]{1,0:T(8,128)(2,1)S(1)} %copy-done.33, ...), custom_call_target="tpu_custom_call" | custom-call | flops 11000000512 | bytes 6213632 | tf_op jit(solution)/shard_map/attn_bwd/pallas_call | solution.py:124
  288.9 3.3 qkv_grad.2
  292.3 8.5 %attn_bwd.3 = (bf16[1024,640]{1,0:T(8,128)(2,1)S(1)}, f32[8,640]{1,0:T(8,128)S(1)}) custom-call(bf16[1024,640]{1,0:T(8,128)(2,1)S(1)} %copy-done.83, bf16[768,768]{1,0:T(8,128)(2,1)S(1)} %copy-done.5, bf16[1024,128]{1,0:T(8,128)(2,1)S(1)} %copy-done.9, bf16[1024,256]{1,0:T(8,128)(2,1)S(1)} %copy-done.24, bf16[512,768]{1,0:T(8,128)(2,1)S(1)} %copy-done.33, ...), custom_call_target="tpu_custom_call" | custom-call | flops 11000000512 | bytes 6213632 | tf_op jit(solution)/shard_map/attn_bwd/pallas_call | solution.py:124
  300.8 4.1 collective-permute-done.24.ga_ref
  305.4 2.9 token_grad.1
  308.4 1.5 grad_half.1
  310.9 1.4 collective-permute-start.27
  314.1 2.5 qkv_grad.3
  317.8 4.4 %all-to-all-start.3 = ((bf16[8,64,768]{2,1,0:T(8,128)(2,1)}), bf16[8,64,768]{2,1,0:T(8,128)(2,1)S(1)}, u32[]{:S(2)}, u32[]{:S(2)}) async-start(bf16[8,64,768]{2,1,0:T(8,128)(2,1)} %bitcast.134), calls=%async_computation.3 | async-start | bytes 1572864 | tf_op jit(solution)/shard_map/all_to_all | solution.py:982
  322.2 8.6 %collective-permute-done.27.a_ref = bf16[4,96,768]{2,1,0:T(8,128)(2,1)} collective-permute-done((bf16[4,96,768]{2,1,0:T(8,128)(2,1)}, bf16[4,96,768]{2,1,0:T(8,128)(2,1)}, u32[]{:S(2)}, u32[]{:S(2)}) %collective-permute-start.27) | collective-permute-done | bytes 589856 | tf_op jit(solution)/shard_map/ppermute | solution.py:36
  330.8 1.6 grad_sum.2
  333.9 2.9 collective-permute-start.29
  336.8 10.6 %collective-permute-done.30 = bf16[1,4,104,768]{3,2,1,0:T(8,128)(2,1)} collective-permute-done((bf16[1,4,104,768]{3,2,1,0:T(8,128)(2,1)}, bf16[1,4,104,768]{3,2,1,0:T(8,128)(2,1)}, u32[]{:S(2)}, u32[]{:S(2)}) %collective-permute-start.30) | collective-permute-done | bytes 639008 | tf_op jit(solution)/shard_map/ppermute | solution.py:36
  351.5 1.5 collective-permute-start.38
  353.0 9.7 %collective-permute-done.29.refs_1_ = bf16[1,4,104,768]{3,2,1,0:T(8,128)(2,1)S(1)} collective-permute-done((bf16[1,4,104,768]{3,2,1,0:T(8,128)(2,1)S(1)}, bf16[1,4,104,768]{3,2,1,0:T(8,128)(2,1)S(1)}, u32[]{:S(2)}, u32[]{:S(2)}) %collective-permute-start.29) | collective-permute-done | bytes 639008 | tf_op jit(solution)/shard_map/ppermute | solution.py:36
  362.7 1.6 collective-permute-done.31.refs_2_
  365.6 5.6 %place.2 = bf16[8,2,2,64,768]{4,3,2,1,0:T(8,128)(2,1)} custom-call(s32[4]{0:T(128)S(1)} %copy-done.66, bf16[8,64,768]{2,1,0:T(8,128)(2,1)} %all-to-all-done.2.a_ref, bf16[8,64,768]{2,1,0:T(8,128)(2,1)S(1)} %copy-done.50, bf16[8,64,768]{2,1,0:T(8,128)(2,1)S(1)} %collective-permute-done.16.c_ref, bf16[8,64,768]{2,1,0:T(8,128)(2,1)S(1)} %collective-permute-done.17.d_ref), custom_call_target="tpu_custom_call" | custom-call | bytes 6000000 | tf_op jit(solution)/shard_map/place/pallas_call | solution.py:986
  374.8 1.6 fusion.8
  376.4 2.4 collective-permute-start.36
  379.6 9.3 %collective-permute-done.32.b_ref = bf16[8,64,768]{2,1,0:T(8,128)(2,1)S(1)} collective-permute-done((bf16[8,64,768]{2,1,0:T(8,128)(2,1)S(1)}, bf16[8,64,768]{2,1,0:T(8,128)(2,1)S(1)}, u32[]{:S(2)}, u32[]{:S(2)}) %collective-permute-start.32) | collective-permute-done | bytes 786464 | tf_op jit(solution)/shard_map/ppermute | solution.py:36
  388.9 4.5 %all-to-all-start.4 = ((bf16[8,224,128]{2,1,0:T(8,128)(2,1)}), bf16[8,224,128]{2,1,0:T(8,128)(2,1)}, u32[]{:S(2)}, u32[]{:S(2)}) async-start(bf16[8,224,128]{2,1,0:T(8,128)(2,1)} %convert_add_fusion), calls=%async_computation.4 | async-start | bytes 917504 | tf_op jit(solution)/shard_map/all_to_all | solution.py:1267
  395.9 1.8 copy.58
  397.7 1.8 copy.59
  400.2 1.6 copy.60
  409.6 3.8 place.3
  (340 shorter events, 88.8 us)
Async XLA Ops:
  0.7 30.6 %copy-start = (bf16[16,128,768]{2,1,0:T(8,128)(2,1)S(1)}, bf16[16,128,768]{2,1,0:T(8,128)(2,1)}, u32[]{:S(2)}) copy-start(bf16[16,128,768]{2,1,0:T(8,128)(2,1)} %param.23) | copy-start | bytes 9437188
  10.4 10.3 %collective-permute-start = (bf16[1,1,112,768]{3,2,1,0:T(8,128)(2,1)}, bf16[1,1,112,768]{3,2,1,0:T(8,128)(2,1)S(1)}, u32[]{:S(2)}, u32[]{:S(2)}) collective-permute-start(bf16[1,1,112,768]{3,2,1,0:T(8,128)(2,1)} %get-tuple-element.248), channel_id=1, source_target_pairs={{0,8},{1,9},{2,10},{3,11},{4,12},{5,13},{6,14},{7,15},{8,0},{9,1},... | collective-permute-start | bytes 516104 | tf_op jit(solution)/shard_map/ppermute | solution.py:36
  13.4 15.9 %collective-permute-start.1 = (bf16[1,1,112,768]{3,2,1,0:T(8,128)(2,1)}, bf16[1,1,112,768]{3,2,1,0:T(8,128)(2,1)}, u32[]{:S(2)}, u32[]{:S(2)}) collective-permute-start(bf16[1,1,112,768]{3,2,1,0:T(8,128)(2,1)} %get-tuple-element.248), channel_id=1, source_target_pairs={{0,16},{1,17},{2,18},{3,19},{4,20},{5,21},{6,22},{7,23},{8,24},{9,... | collective-permute-start | bytes 516104 | tf_op jit(solution)/shard_map/ppermute | solution.py:36
  16.0 13.3 %collective-permute-start.2 = (bf16[1,1,112,768]{3,2,1,0:T(8,128)(2,1)}, bf16[1,1,112,768]{3,2,1,0:T(8,128)(2,1)}, u32[]{:S(2)}, u32[]{:S(2)}) collective-permute-start(bf16[1,1,112,768]{3,2,1,0:T(8,128)(2,1)} %get-tuple-element.248), channel_id=1, source_target_pairs={{0,24},{1,25},{2,26},{3,27},{4,28},{5,29},{6,30},{7,31},{8,16},{9,... | collective-permute-start | bytes 516104 | tf_op jit(solution)/shard_map/ppermute | solution.py:36
  20.4 11.8 %copy-start.97 = (bf16[16,768]{1,0:T(8,128)(2,1)}, bf16[16,768]{1,0:T(8,128)(2,1)S(1)}, u32[]{:S(2)}) copy-start(bf16[16,768]{1,0:T(8,128)(2,1)S(1)} %constant_dynamic-update-slice_fusion.2) | copy-start | bytes 73732
  32.2 47.2 %all-to-all-start = ((bf16[8,64,768]{2,1,0:T(8,128)(2,1)}), bf16[8,64,768]{2,1,0:T(8,128)(2,1)S(1)}, u32[]{:S(2)}, u32[]{:S(2)}) async-start(bf16[8,64,768]{2,1,0:T(8,128)(2,1)} %dynamic-slice_bitcast_fusion.1), calls=%async_computation | async-start | bytes 1572864 | tf_op jit(solution)/shard_map/all_to_all | solution.py:979
  41.8 31.8 %copy-start.102 = (s32[16]{0:T(128)S(1)}, s32[16]{0:T(128)}, u32[]{:S(2)}) copy-start(s32[16]{0:T(128)} %param.25) | copy-start | bytes 196
  41.8 32.4 %copy-start.100 = (s32[16]{0:T(128)S(1)}, s32[16]{0:T(128)}, u32[]{:S(2)}) copy-start(s32[16]{0:T(128)} %param.26) | copy-start | bytes 196
  41.8 32.9 %collective-permute-start.3 = (bf16[1,4,112,768]{3,2,1,0:T(8,128)(2,1)S(1)}, bf16[1,4,112,768]{3,2,1,0:T(8,128)(2,1)S(1)}, u32[]{:S(2)}, u32[]{:S(2)}) collective-permute-start(bf16[1,4,112,768]{3,2,1,0:T(8,128)(2,1)S(1)} %copy-done.39), channel_id=1, source_target_pairs={{0,4},{1,5},{2,6},{3,7},{4,0},{5,1},{6,2},{7,3},{8,12},{9,13},{10,... | collective-permute-start | bytes 2064392 | tf_op jit(solution)/shard_map/ppermute | solution.py:36
  43.9 30.9 %collective-permute-start.4 = (bf16[1,4,112,768]{3,2,1,0:T(8,128)(2,1)S(1)}, bf16[1,4,112,768]{3,2,1,0:T(8,128)(2,1)S(1)}, u32[]{:S(2)}, u32[]{:S(2)}) collective-permute-start(bf16[1,4,112,768]{3,2,1,0:T(8,128)(2,1)S(1)} %copy-done.39), channel_id=1, source_target_pairs={{0,2},{1,3},{2,0},{3,1},{4,6},{5,7},{6,4},{7,5},{8,10},{9,11},{10,... | collective-permute-start | bytes 2064392 | tf_op jit(solution)/shard_map/ppermute | solution.py:36
  45.4 34.0 %collective-permute-start.5 = (bf16[1,4,112,768]{3,2,1,0:T(8,128)(2,1)S(1)}, bf16[1,4,112,768]{3,2,1,0:T(8,128)(2,1)S(1)}, u32[]{:S(2)}, u32[]{:S(2)}) collective-permute-start(bf16[1,4,112,768]{3,2,1,0:T(8,128)(2,1)S(1)} %copy-done.39), channel_id=1, source_target_pairs={{0,6},{1,7},{2,4},{3,5},{4,2},{5,3},{6,0},{7,1},{8,14},{9,15},{10,... | collective-permute-start | bytes 2064392 | tf_op jit(solution)/shard_map/ppermute | solution.py:36
  45.4 26.9 %collective-permute-start.6 = (bf16[2,1,112,768]{3,2,0,1:T(8,128)(2,1)S(1)}, bf16[2,1,112,768]{3,2,0,1:T(8,128)(2,1)S(1)}, u32[]{:S(2)}, u32[]{:S(2)}) collective-permute-start(bf16[2,1,112,768]{3,2,0,1:T(8,128)(2,1)S(1)} %bitcast.135), channel_id=1, source_target_pairs={{0,16},{1,17},{2,18},{3,19},{4,20},{5,21},{6,22},{7,23},{8,24},{9,... | collective-permute-start | bytes 1032200 | tf_op jit(solution)/shard_map/ppermute | solution.py:36
  73.5 15.6 %collective-permute-start.9 = (bf16[2,2,112,768]{3,2,0,1:T(8,128)(2,1)}, bf16[2,2,112,768]{3,2,0,1:T(8,128)(2,1)}, u32[]{:S(2)}, u32[]{:S(2)}) collective-permute-start(bf16[2,2,112,768]{3,2,0,1:T(8,128)(2,1)} %get-tuple-element.244), channel_id=1, source_target_pairs={{0,8},{1,9},{2,10},{3,11},{4,12},{5,13},{6,14},{7,15},{8,0},{9,1},... | collective-permute-start | bytes 2064392 | tf_op jit(solution)/shard_map/ppermute | solution.py:36
  74.7 14.5 %copy-start.57 = (bf16[1,4,112,768]{3,2,1,0:T(8,128)(2,1)}, bf16[1,4,112,768]{3,2,1,0:T(8,128)(2,1)S(1)}, u32[]{:S(2)}) copy-start(bf16[1,4,112,768]{3,2,1,0:T(8,128)(2,1)S(1)} %collective-permute-done.3.rest_1_.a1) | copy-start | bytes 2064388
  79.4 11.0 %copy-start.78 = (bf16[1,4,112,768]{3,2,1,0:T(8,128)(2,1)}, bf16[1,4,112,768]{3,2,1,0:T(8,128)(2,1)S(1)}, u32[]{:S(2)}) copy-start(bf16[1,4,112,768]{3,2,1,0:T(8,128)(2,1)S(1)} %collective-permute-done.5.rest_1_) | copy-start | bytes 2064388
  79.4 28.4 %copy-start.2 = (bf16[8,64,768]{2,1,0:T(8,128)(2,1)}, bf16[8,64,768]{2,1,0:T(8,128)(2,1)S(1)}, u32[]{:S(2)}) copy-start(bf16[8,64,768]{2,1,0:T(8,128)(2,1)S(1)} %all-to-all-done) | copy-start | bytes 2359300
  79.4 14.7 %collective-permute-start.7 = (bf16[512,768]{1,0:T(8,128)(2,1)S(1)}, bf16[512,768]{1,0:T(8,128)(2,1)S(1)}, u32[]{:S(2)}, u32[]{:S(2)}) collective-permute-start(bf16[512,768]{1,0:T(8,128)(2,1)S(1)} %bitcast.121), channel_id=1, source_target_pairs={{0,1},{1,0},{2,3},{3,2},{4,5},{5,4},{6,7},{7,6},{8,9},{9,8},{10,11... | collective-permute-start | bytes 2359304 | tf_op jit(solution)/shard_map/ppermute | solution.py:36
  80.6 115.1 %copy-start.65 = (s32[4]{0:T(128)}, s32[4]{0:T(128)S(1)}, u32[]{:S(2)}) copy-start(s32[4]{0:T(128)S(1)} %pad_add_fusion.info) | copy-start | bytes 52
  81.5 40.3 %copy-start.8 = (bf16[1024,128]{1,0:T(8,128)(2,1)}, bf16[1024,128]{1,0:T(8,128)(2,1)S(1)}, u32[]{:S(2)}) copy-start(bf16[1024,128]{1,0:T(8,128)(2,1)S(1)} %select_convert_fusion.bias_ref.aux_ref.b0_ref.b1_ref) | copy-start | bytes 786436
  90.6 17.3 %copy-start.77 = (bf16[1,4,112,768]{3,2,1,0:T(8,128)(2,1)S(1)}, bf16[1,4,112,768]{3,2,1,0:T(8,128)(2,1)}, u32[]{:S(2)}) copy-start(bf16[1,4,112,768]{3,2,1,0:T(8,128)(2,1)} %copy-done.76) | copy-start | bytes 2064388
  90.6 17.3 %copy-start.79 = (bf16[1,4,112,768]{3,2,1,0:T(8,128)(2,1)S(1)}, bf16[1,4,112,768]{3,2,1,0:T(8,128)(2,1)}, u32[]{:S(2)}) copy-start(bf16[1,4,112,768]{3,2,1,0:T(8,128)(2,1)} %copy-done.78) | copy-start | bytes 2064388
  90.6 39.6 %collective-permute-start.10 = (bf16[2,4,112,768]{3,2,1,0:T(8,128)(2,1)S(1)}, bf16[2,4,112,768]{3,2,1,0:T(8,128)(2,1)S(1)}, u32[]{:S(2)}, u32[]{:S(2)}) collective-permute-start(bf16[2,4,112,768]{3,2,1,0:T(8,128)(2,1)S(1)} %bitcast.109), channel_id=1, source_target_pairs={{0,4},{1,5},{2,6},{3,7},{4,0},{5,1},{6,2},{7,3},{8,12},{9,13},{10,... | collective-permute-start | bytes 4128776 | tf_op jit(solution)/shard_map/ppermute | solution.py:36
  92.6 59.1 %collective-permute-start.11 = (bf16[2,4,112,768]{3,2,1,0:T(8,128)(2,1)S(1)}, bf16[2,4,112,768]{3,2,1,0:T(8,128)(2,1)}, u32[]{:S(2)}, u32[]{:S(2)}) collective-permute-start(bf16[2,4,112,768]{3,2,1,0:T(8,128)(2,1)S(1)} %bitcast.110), channel_id=1, source_target_pairs={{0,2},{1,3},{2,0},{3,1},{4,6},{5,7},{6,4},{7,5},{8,10},{9,11},{10,... | collective-permute-start | bytes 4128776 | tf_op jit(solution)/shard_map/ppermute | solution.py:36
  94.1 57.6 %collective-permute-start.12 = (bf16[2,4,112,768]{3,2,1,0:T(8,128)(2,1)S(1)}, bf16[2,4,112,768]{3,2,1,0:T(8,128)(2,1)}, u32[]{:S(2)}, u32[]{:S(2)}) collective-permute-start(bf16[2,4,112,768]{3,2,1,0:T(8,128)(2,1)S(1)} %bitcast.111), channel_id=1, source_target_pairs={{0,6},{1,7},{2,4},{3,5},{4,2},{5,3},{6,0},{7,1},{8,14},{9,15},{10,... | collective-permute-start | bytes 4128776 | tf_op jit(solution)/shard_map/ppermute | solution.py:36
  94.2 13.7 %copy-start.31 = (bf16[512,768]{1,0:T(8,128)(2,1)}, bf16[512,768]{1,0:T(8,128)(2,1)S(1)}, u32[]{:S(2)}) copy-start(bf16[512,768]{1,0:T(8,128)(2,1)S(1)} %collective-permute-done.7.sib_ref.x1) | copy-start | bytes 2359300
  107.8 12.9 %copy-start.86 = (f32[8,1024]{1,0:T(8,128)}, f32[8,1024]{1,0:T(8,128)S(1)}, u32[]{:S(2)}) copy-start(f32[8,1024]{1,0:T(8,128)S(1)} %get-tuple-element.172.lse_ref) | copy-start | bytes 98308
  107.8 14.6 %copy-start.4 = (bf16[768,768]{1,0:T(8,128)(2,1)}, bf16[768,768]{1,0:T(8,128)(2,1)S(1)}, u32[]{:S(2)}) copy-start(bf16[768,768]{1,0:T(8,128)(2,1)S(1)} %get-tuple-element.118.w0_ref.w_ref) | copy-start | bytes 3538948
  107.8 14.6 %copy-start.23 = (bf16[1024,256]{1,0:T(8,128)(2,1)}, bf16[1024,256]{1,0:T(8,128)(2,1)S(1)}, u32[]{:S(2)}) copy-start(bf16[1024,256]{1,0:T(8,128)(2,1)S(1)} %get-tuple-element.113.c0_ref.ctx_ref) | copy-start | bytes 1572868
  121.8 2.4 collective-permute-start.8
  151.7 27.9 %collective-permute-start.13 = (bf16[512,768]{1,0:T(8,128)(2,1)}, bf16[512,768]{1,0:T(8,128)(2,1)}, u32[]{:S(2)}, u32[]{:S(2)}) collective-permute-start(bf16[512,768]{1,0:T(8,128)(2,1)} %get-tuple-element.122.x_ref.first), channel_id=1, source_target_pairs={{0,1},{1,0},{2,3},{3,2},{4,5},{5,4},{6,7},{7,6},{8,9},{9,8},{10,11... | collective-permute-start | bytes 2359304 | tf_op jit(solution)/shard_map/ppermute | solution.py:36
  151.7 18.3 %copy-start.9 = (bf16[1024,128]{1,0:T(8,128)(2,1)S(1)}, bf16[1024,128]{1,0:T(8,128)(2,1)}, u32[]{:S(2)}) copy-start(bf16[1024,128]{1,0:T(8,128)(2,1)} %copy-done.8) | copy-start | bytes 786436
  153.9 41.9 %all-to-all-start.1 = ((bf16[8,64,768]{2,1,0:T(8,128)(2,1)}), bf16[8,64,768]{2,1,0:T(8,128)(2,1)}, u32[]{:S(2)}, u32[]{:S(2)}) async-start(bf16[8,64,768]{2,1,0:T(8,128)(2,1)} %dynamic-slice_bitcast_fusion), calls=%async_computation.1 | async-start | bytes 1572864 | tf_op jit(solution)/shard_map/all_to_all | solution.py:979
  193.5 9.9 %collective-permute-start.14 = (bf16[512,768]{1,0:T(8,128)(2,1)}, bf16[512,768]{1,0:T(8,128)(2,1)}, u32[]{:S(2)}, u32[]{:S(2)}) collective-permute-start(bf16[512,768]{1,0:T(8,128)(2,1)} %product.5), channel_id=1, source_target_pairs={{0,1},{1,0},{2,3},{3,2},{4,5},{5,4},{6,7},{7,6},{8,9},{9,8},{10,11... | collective-permute-start | bytes 2359304 | tf_op jit(solution)/shard_map/ppermute | solution.py:36
  209.3 26.7 %all-to-all-start.2 = ((bf16[8,64,768]{2,1,0:T(8,128)(2,1)}), bf16[8,64,768]{2,1,0:T(8,128)(2,1)}, u32[]{:S(2)}, u32[]{:S(2)}) async-start(bf16[8,64,768]{2,1,0:T(8,128)(2,1)} %bitcast.131), calls=%async_computation.2 | async-start | bytes 1572864 | tf_op jit(solution)/shard_map/all_to_all | solution.py:982
  215.1 1.2 collective-permute-start.18
  224.3 9.1 %collective-permute-start.19 = (bf16[512,768]{1,0:T(8,128)(2,1)}, bf16[512,768]{1,0:T(8,128)(2,1)S(1)}, u32[]{:S(2)}, u32[]{:S(2)}) collective-permute-start(bf16[512,768]{1,0:T(8,128)(2,1)} %get-tuple-element.141.g_ref.dffn), channel_id=1, source_target_pairs={{0,1},{1,0},{2,3},{3,2},{4,5},{5,4},{6,7},{7,6},{8,9},{9,8},{10,11... | collective-permute-start | bytes 2359304 | tf_op jit(solution)/shard_map/ppermute | solution.py:36
  236.0 19.7 %collective-permute-start.15 = (bf16[8,64,768]{2,1,0:T(8,128)(2,1)}, bf16[8,64,768]{2,1,0:T(8,128)(2,1)S(1)}, u32[]{:S(2)}, u32[]{:S(2)}) collective-permute-start(bf16[8,64,768]{2,1,0:T(8,128)(2,1)} %all-to-all-done.2.a_ref), channel_id=1, source_target_pairs={{0,2},{1,3},{2,0},{3,1},{4,6},{5,7},{6,4},{7,5},{8,10},{9,11},{10,... | collective-permute-start | bytes 2359304 | tf_op jit(solution)/shard_map/ppermute | solution.py:36
  249.5 6.2 %collective-permute-start.20 = (bf16[512,768]{1,0:T(8,128)(2,1)S(1)}, bf16[512,768]{1,0:T(8,128)(2,1)S(1)}, u32[]{:S(2)}, u32[]{:S(2)}) collective-permute-start(bf16[512,768]{1,0:T(8,128)(2,1)S(1)} %product.7), channel_id=1, source_target_pairs={{0,1},{1,0},{2,3},{3,2},{4,5},{5,4},{6,7},{7,6},{8,9},{9,8},{10,11... | collective-permute-start | bytes 2359304 | tf_op jit(solution)/shard_map/ppermute | solution.py:36
  264.2 2.0 collective-permute-start.21
  264.7 14.5 %collective-permute-start.23 = (bf16[512,768]{1,0:T(8,128)(2,1)}, bf16[512,768]{1,0:T(8,128)(2,1)S(1)}, u32[]{:S(2)}, u32[]{:S(2)}) collective-permute-start(bf16[512,768]{1,0:T(8,128)(2,1)} %get-tuple-element.158.da_ref.da), channel_id=1, source_target_pairs={{0,1},{1,0},{2,3},{3,2},{4,5},{5,4},{6,7},{7,6},{8,9},{9,8},{10,11... | collective-permute-start | bytes 2359304 | tf_op jit(solution)/shard_map/ppermute | solution.py:36
  266.3 12.9 %collective-permute-start.22 = (bf16[8,224,128]{2,1,0:T(8,128)(2,1)S(1)}, bf16[8,224,128]{2,1,0:T(8,128)(2,1)S(1)}, u32[]{:S(2)}, u32[]{:S(2)}) collective-permute-start(bf16[8,224,128]{2,1,0:T(8,128)(2,1)S(1)} %fusion), channel_id=1, source_target_pairs={{0,2},{1,3},{2,0},{3,1},{4,6},{5,7},{6,4},{7,5},{8,10},{9,11},{10,... | collective-permute-start | bytes 1376264 | tf_op jit(solution)/shard_map/ppermute | solution.py:36
  276.9 28.0 %collective-permute-start.24 = (bf16[2,4,96,768]{3,2,1,0:T(8,128)(2,1)S(1)}, bf16[2,4,96,768]{3,2,1,0:T(8,128)(2,1)S(1)}, u32[]{:S(2)}, u32[]{:S(2)}) collective-permute-start(bf16[2,4,96,768]{3,2,1,0:T(8,128)(2,1)S(1)} %get-tuple-element.160), channel_id=1, source_target_pairs={{0,2},{1,3},{2,0},{3,1},{4,6},{5,7},{6,4},{7,5},{8,10},{9,11},{10,... | collective-permute-start | bytes 3538952 | tf_op jit(solution)/shard_map/ppermute | solution.py:36
  277.8 27.7 %collective-permute-start.25 = (bf16[2,4,96,768]{3,2,1,0:T(8,128)(2,1)S(1)}, bf16[2,4,96,768]{3,2,1,0:T(8,128)(2,1)S(1)}, u32[]{:S(2)}, u32[]{:S(2)}) collective-permute-start(bf16[2,4,96,768]{3,2,1,0:T(8,128)(2,1)S(1)} %get-tuple-element.162), channel_id=1, source_target_pairs={{0,4},{1,5},{2,6},{3,7},{4,0},{5,1},{6,2},{7,3},{8,12},{9,13},{10,... | collective-permute-start | bytes 3538952 | tf_op jit(solution)/shard_map/ppermute | solution.py:36
  292.3 13.2 %copy-start.41 = (f32[512,768]{1,0:T(8,128)S(1)}, f32[512,768]{1,0:T(8,128)}, u32[]{:S(2)}) copy-start(f32[512,768]{1,0:T(8,128)} %get-tuple-element.175.dr1_ref) | copy-start | bytes 4718596
  308.3 8.3 %collective-permute-start.26 = (bf16[512,768]{1,0:T(8,128)(2,1)S(1)}, bf16[512,768]{1,0:T(8,128)(2,1)S(1)}, u32[]{:S(2)}, u32[]{:S(2)}) collective-permute-start(bf16[512,768]{1,0:T(8,128)(2,1)S(1)} %get-tuple-element.177), channel_id=1, source_target_pairs={{0,1},{1,0},{2,3},{3,2},{4,5},{5,4},{6,7},{7,6},{8,9},{9,8},{10,11... | collective-permute-start | bytes 2359304 | tf_op jit(solution)/shard_map/ppermute | solution.py:36
  310.9 19.9 %collective-permute-start.27 = (bf16[4,96,768]{2,1,0:T(8,128)(2,1)}, bf16[4,96,768]{2,1,0:T(8,128)(2,1)}, u32[]{:S(2)}, u32[]{:S(2)}) collective-permute-start(bf16[4,96,768]{2,1,0:T(8,128)(2,1)} %get-tuple-element.185), channel_id=1, source_target_pairs={{0,4},{1,5},{2,6},{3,7},{4,0},{5,1},{6,2},{7,3},{8,12},{9,13},{10,... | collective-permute-start | bytes 1769480 | tf_op jit(solution)/shard_map/ppermute | solution.py:36
  312.3 18.5 %collective-permute-start.28 = (bf16[4,96,768]{2,1,0:T(8,128)(2,1)}, bf16[4,96,768]{2,1,0:T(8,128)(2,1)}, u32[]{:S(2)}, u32[]{:S(2)}) collective-permute-start(bf16[4,96,768]{2,1,0:T(8,128)(2,1)} %get-tuple-element.186), channel_id=1, source_target_pairs={{0,2},{1,3},{2,0},{3,1},{4,6},{5,7},{6,4},{7,5},{8,10},{9,11},{10,... | collective-permute-start | bytes 1769480 | tf_op jit(solution)/shard_map/ppermute | solution.py:36
  313.5 33.9 %collective-permute-start.30 = (bf16[1,4,104,768]{3,2,1,0:T(8,128)(2,1)}, bf16[1,4,104,768]{3,2,1,0:T(8,128)(2,1)}, u32[]{:S(2)}, u32[]{:S(2)}) collective-permute-start(bf16[1,4,104,768]{3,2,1,0:T(8,128)(2,1)} %get-tuple-element.170), channel_id=1, source_target_pairs={{0,4},{1,5},{2,6},{3,7},{4,0},{5,1},{6,2},{7,3},{8,12},{9,13},{10,... | collective-permute-start | bytes 1916936 | tf_op jit(solution)/shard_map/ppermute | solution.py:36
  317.8 13.0 %copy-start.47 = (bf16[2,4,96,768]{3,2,1,0:T(8,128)(2,1)S(1)}, bf16[2,4,96,768]{3,2,1,0:T(8,128)(2,1)}, u32[]{:S(2)}) copy-start(bf16[2,4,96,768]{3,2,1,0:T(8,128)(2,1)} %copy-done.46) | copy-start | bytes 3538948
  317.8 53.4 %all-to-all-start.3 = ((bf16[8,64,768]{2,1,0:T(8,128)(2,1)}), bf16[8,64,768]{2,1,0:T(8,128)(2,1)S(1)}, u32[]{:S(2)}, u32[]{:S(2)}) async-start(bf16[8,64,768]{2,1,0:T(8,128)(2,1)} %bitcast.134), calls=%async_computation.3 | async-start | bytes 1572864 | tf_op jit(solution)/shard_map/all_to_all | solution.py:982
  330.8 16.5 %copy-start.60 = (bf16[1,4,104,768]{3,2,1,0:T(8,128)(2,1)S(1)}, bf16[1,4,104,768]{3,2,1,0:T(8,128)(2,1)}, u32[]{:S(2)}) copy-start(bf16[1,4,104,768]{3,2,1,0:T(8,128)(2,1)} %copy-done.59) | copy-start | bytes 1916932
  333.3 17.3 %collective-permute-start.37 = (bf16[2,2,96,768]{3,2,1,0:T(8,128)(2,1)S(1)}, bf16[2,2,96,768]{3,2,1,0:T(8,128)(2,1)S(1)}, u32[]{:S(2)}, u32[]{:S(2)}) collective-permute-start(bf16[2,2,96,768]{3,2,1,0:T(8,128)(2,1)S(1)} %pad_maximum_fusion.2), channel_id=1, source_target_pairs={{0,8},{1,9},{2,10},{3,11},{4,12},{5,13},{6,14},{7,15},{8,0},{9,1},... | collective-permute-start | bytes 1769480 | tf_op jit(solution)/shard_map/ppermute | solution.py:36
  333.3 32.2 %collective-permute-start.16 = (bf16[8,64,768]{2,1,0:T(8,128)(2,1)}, bf16[8,64,768]{2,1,0:T(8,128)(2,1)S(1)}, u32[]{:S(2)}, u32[]{:S(2)}) collective-permute-start(bf16[8,64,768]{2,1,0:T(8,128)(2,1)} %all-to-all-done.2.a_ref), channel_id=1, source_target_pairs={{0,1},{1,0},{2,3},{3,2},{4,5},{5,4},{6,7},{7,6},{8,9},{9,8},{10,11... | collective-permute-start | bytes 2359304 | tf_op jit(solution)/shard_map/ppermute | solution.py:36
  333.3 32.2 %collective-permute-start.17 = (bf16[8,64,768]{2,1,0:T(8,128)(2,1)S(1)}, bf16[8,64,768]{2,1,0:T(8,128)(2,1)S(1)}, u32[]{:S(2)}, u32[]{:S(2)}) collective-permute-start(bf16[8,64,768]{2,1,0:T(8,128)(2,1)S(1)} %copy-done.50), channel_id=1, source_target_pairs={{0,1},{1,0},{2,3},{3,2},{4,5},{5,4},{6,7},{7,6},{8,9},{9,8},{10,11... | collective-permute-start | bytes 2359304 | tf_op jit(solution)/shard_map/ppermute | solution.py:36
  333.9 28.8 %collective-permute-start.29 = (bf16[1,4,104,768]{3,2,1,0:T(8,128)(2,1)S(1)}, bf16[1,4,104,768]{3,2,1,0:T(8,128)(2,1)S(1)}, u32[]{:S(2)}, u32[]{:S(2)}) collective-permute-start(bf16[1,4,104,768]{3,2,1,0:T(8,128)(2,1)S(1)} %copy-done.81), channel_id=1, source_target_pairs={{0,4},{1,5},{2,6},{3,7},{4,0},{5,1},{6,2},{7,3},{8,12},{9,13},{10,... | collective-permute-start | bytes 1916936 | tf_op jit(solution)/shard_map/ppermute | solution.py:36
  348.6 15.7 %collective-permute-start.31 = (bf16[1,4,104,768]{3,2,1,0:T(8,128)(2,1)S(1)}, bf16[1,4,104,768]{3,2,1,0:T(8,128)(2,1)S(1)}, u32[]{:S(2)}, u32[]{:S(2)}) collective-permute-start(bf16[1,4,104,768]{3,2,1,0:T(8,128)(2,1)S(1)} %add_convert_fusion.1), channel_id=1, source_target_pairs={{0,2},{1,3},{2,0},{3,1},{4,6},{5,7},{6,4},{7,5},{8,10},{9,11},{10,... | collective-permute-start | bytes 1916936 | tf_op jit(solution)/shard_map/ppermute | solution.py:36
  350.6 14.7 %copy-start.94 = (bf16[2,2,96,768]{3,2,1,0:T(8,128)(2,1)}, bf16[2,2,96,768]{3,2,1,0:T(8,128)(2,1)S(1)}, u32[]{:S(2)}) copy-start(bf16[2,2,96,768]{3,2,1,0:T(8,128)(2,1)S(1)} %collective-permute-done.37) | copy-start | bytes 1769476
  351.5 22.1 %collective-permute-start.38 = (bf16[2,96,768]{2,1,0:T(8,128)(2,1)}, bf16[2,96,768]{2,1,0:T(8,128)(2,1)}, u32[]{:S(2)}, u32[]{:S(2)}) collective-permute-start(bf16[2,96,768]{2,1,0:T(8,128)(2,1)} %fusion.1), channel_id=1, source_target_pairs={{0,16},{1,17},{2,18},{3,19},{4,20},{5,21},{6,22},{7,23},{8,24},{9,... | collective-permute-start | bytes 884744 | tf_op jit(solution)/shard_map/ppermute | solution.py:36
  365.3 9.5 %collective-permute-start.35 = (bf16[2,1,104,768]{3,2,1,0:T(8,128)(2,1)}, bf16[2,1,104,768]{3,2,1,0:T(8,128)(2,1)}, u32[]{:S(2)}, u32[]{:S(2)}) collective-permute-start(bf16[2,1,104,768]{3,2,1,0:T(8,128)(2,1)} %pad_maximum_fusion.4), channel_id=1, source_target_pairs={{0,8},{1,9},{2,10},{3,11},{4,12},{5,13},{6,14},{7,15},{8,0},{9,1},... | collective-permute-start | bytes 958472 | tf_op jit(solution)/shard_map/ppermute | solution.py:36
  371.2 17.7 %collective-permute-start.32 = (bf16[8,64,768]{2,1,0:T(8,128)(2,1)S(1)}, bf16[8,64,768]{2,1,0:T(8,128)(2,1)S(1)}, u32[]{:S(2)}, u32[]{:S(2)}) collective-permute-start(bf16[8,64,768]{2,1,0:T(8,128)(2,1)S(1)} %all-to-all-done.3.a_ref), channel_id=1, source_target_pairs={{0,2},{1,3},{2,0},{3,1},{4,6},{5,7},{6,4},{7,5},{8,10},{9,11},{10,... | collective-permute-start | bytes 2359304 | tf_op jit(solution)/shard_map/ppermute | solution.py:36
  376.4 17.0 %collective-permute-start.36 = (bf16[1,104,768]{2,1,0:T(8,128)(2,1)}, bf16[1,104,768]{2,1,0:T(8,128)(2,1)}, u32[]{:S(2)}, u32[]{:S(2)}) collective-permute-start(bf16[1,104,768]{2,1,0:T(8,128)(2,1)} %fusion.8), channel_id=1, source_target_pairs={{0,16},{1,17},{2,18},{3,19},{4,20},{5,21},{6,22},{7,23},{8,24},{9,... | collective-permute-start | bytes 479240 | tf_op jit(solution)/shard_map/ppermute | solution.py:36
  379.6 23.6 %collective-permute-start.33 = (bf16[8,64,768]{2,1,0:T(8,128)(2,1)S(1)}, bf16[8,64,768]{2,1,0:T(8,128)(2,1)S(1)}, u32[]{:S(2)}, u32[]{:S(2)}) collective-permute-start(bf16[8,64,768]{2,1,0:T(8,128)(2,1)S(1)} %all-to-all-done.3.a_ref), channel_id=1, source_target_pairs={{0,1},{1,0},{2,3},{3,2},{4,5},{5,4},{6,7},{7,6},{8,9},{9,8},{10,11... | collective-permute-start | bytes 2359304 | tf_op jit(solution)/shard_map/ppermute | solution.py:36
  388.9 24.5 %all-to-all-start.4 = ((bf16[8,224,128]{2,1,0:T(8,128)(2,1)}), bf16[8,224,128]{2,1,0:T(8,128)(2,1)}, u32[]{:S(2)}, u32[]{:S(2)}) async-start(bf16[8,224,128]{2,1,0:T(8,128)(2,1)} %convert_add_fusion), calls=%async_computation.4 | async-start | bytes 917504 | tf_op jit(solution)/shard_map/all_to_all | solution.py:1267
  393.4 10.8 %collective-permute-start.34 = (bf16[8,64,768]{2,1,0:T(8,128)(2,1)S(1)}, bf16[8,64,768]{2,1,0:T(8,128)(2,1)S(1)}, u32[]{:S(2)}, u32[]{:S(2)}) collective-permute-start(bf16[8,64,768]{2,1,0:T(8,128)(2,1)S(1)} %collective-permute-done.32.b_ref), channel_id=1, source_target_pairs={{0,1},{1,0},{2,3},{3,2},{4,5},{5,4},{6,7},{7,6},{8,9},{9,8},{10,11... | collective-permute-start | bytes 2359304 | tf_op jit(solution)/shard_map/ppermute | solution.py:36
  (83 other events, 329.4 us)

commit v4 on v3

--- a/solution.py
+++ b/solution.py
@@ -1003,8 +1003,9 @@
         vectors = [jnp.pad(v, ((0, 0), (0, 128 - v.shape[1]))) for v in vectors]
         vectors = jnp.concatenate([*vectors, jnp.zeros((7 - nh, 128), BF)], axis=0)
         qo = jnp.concatenate([qo, jnp.pad(vectors, ((0, 0), (0, D - 128)))], axis=0)
-    qo_line = join_lines(gather_lines(qo[None]))
-    tokens = deal(after(hidden_in, qo_line))
+    qo_got = gather_lines(qo[None])
+    qo_line = join_lines(qo_got)
+    tokens = deal(after(hidden_in, qo_got[1:]))
     w_qo = gather_planes(qo_line, fast)
     w_qo = (w_qo[:2], w_qo[2:]) if fast else (w_qo[:1], w_qo[1:])
     up_pack, down_pack = up_weight, down_weight.T
@@ -1016,9 +1017,9 @@
         up_pack = jnp.concatenate([up_pack, row, more], axis=0)
         more = jnp.concatenate([student_weight[16 * i : 16 * i + 16] for i in range(6)], axis=1)
         down_pack = jnp.concatenate([down_pack, more], axis=0)
-    f_line, f_got = gather_doubling(after(jnp.stack([up_pack, down_pack]), qo_line))
+    f_line, f_got = gather_doubling(after(jnp.stack([up_pack, down_pack]), qo_got[1:]))
     class_b = lanes(class_bias.astype(F32))
-    cot = deal(cotangent)
+    cot = deal(after(cotangent, f_got))
 
     index = jnp.arange(half, dtype=jnp.int32)
     position = (index // hp) * pd + index % hp
@@ -1102,7 +1103,7 @@
         [wide],
         name="ln1",
     )
-    first_sib = hop(after(first_low, w_ffn), 0, 1)
+    first_sib = hop(after(first_low, w_ffn, cot), 0, 1)
 
     if fast:
         student_w, pooler_f, class_f = call(
@@ -1144,7 +1145,7 @@
         ln2_kernel,
         [sds((half, D), BF), sds((half, D)), sds((half, 1)), sds((half, CW)), sds((half, CW))],
         [sds((8, 128))],
-        [ffn_part, ffn_got, after(first, cot), aux_own],
+        [ffn_part, ffn_got, first, aux_own],
         [wide, narrow, student_w],
         name="ln2",
     )
@@ -1230,7 +1231,7 @@
     g1, g1_sum = attn_bwd(nh, proj1, w1, aux, ctx1, dattn, after(dattn_sib, small_y), lse1)
     far_grad = qkv_grad(g1, ctx1, g1_sum)
     if fast:
-        far_got = hop(far_grad[1], 1, 0)
+        far_got = [hop(g, 0, 2) for g in far_grad]
     g0, g0_sum = attn_bwd(
         nh, proj0, w0, aux, ctx0, dattn, after(dattn_sib, g1, far_grad), lse0
     )
@@ -1257,8 +1258,8 @@
             name="grad_sum",
         )
         f_sum = finish_lines(f_sums)
-        far_part = (far_grad[0].astype(F32) + far_got.astype(F32)).astype(BF)
-        qo_own = (near_grad[0], hop(near_grad[1], 1, 0), hop(far_part, 0, 2))
+        near_part = (near_grad[1].astype(F32) + far_got[1].astype(F32)).astype(BF)
+        qo_own = (near_grad[0], far_got[0], hop(near_part, 1, 0))
     else:
         qo_own = ()
         f_sums = f_sum = sum_lines(f_grads)

time: 426 us -> 413 us (0.969)
  starting transfers between devices: 72.1 us -> 59.3 us
  Pallas kernels: 143 us -> 154 us
  waiting for transfers between devices: 113 us -> 104 us
    ppermute x39, waiting for transfers between devices: 112 us -> 85.8 us  [hop(): return lax.ppermute(x, AXES, pairs)]
    all_to_all x2, waiting for transfers between devices: 0.01 us -> 16.3 us  [deal(): return lax.all_to_all(x, 'dp', 0, 0, tiled=True).reshape(half, D)]
    pallas_call x24, Pallas kernels: 109 us -> 121 us  [call(): pl.pallas_call(kernel, in_specs=specs, out_specs=[pl.BlockSpec(memory_spa...]
    all_to_all x2, starting transfers between devices: 22.3 us -> 11.7 us  [deal(): return lax.all_to_all(x, 'dp', 0, 0, tiled=True).reshape(half, D)]
    unnamed x216 -> x214, local copies, waits for them, and re-layouts: 44.4 us -> 44.5 us
  transfers between devices with their start and end apart: 44 -> 44, of which waited for: 17 -> 18; matrix products, arithmetic and copies ran while one was open for 8% -> 9% of each run, Pallas kernels for 30% -> 31%
where the time goes in v4:
time: 413 us; the launch traced here: 407 us
  Pallas kernels  154 us (37%)
  waiting for transfers between devices  104 us (25%)
  local copies, waits for them, and re-layouts  68.2 us (17%)
  starting transfers between devices  59.3 us (14%)
  other arithmetic  19.4 us (5%)
    pallas_call x24, Pallas kernels, call(): pl.pallas_call(kernel, in_specs=specs, out_specs=[pl.BlockSpec(memory_spa...  121 us
    ppermute x39, waiting for transfers between devices, hop(): return lax.ppermute(x, AXES, pairs)  85.8 us
    unnamed x214, local copies, waits for them, and re-layouts  44.5 us
    ppermute x39, starting transfers between devices, hop(): return lax.ppermute(x, AXES, pairs)  33.3 us
    pallas_call x4, Pallas kernels, by_rows(): pl.pallas_call(kernel, grid=(n // RB,), in_specs=[SMEM] * len(head) + [cu...  24.2 us
    all_to_all x2, waiting for transfers between devices, deal(): return lax.all_to_all(x, 'dp', 0, 0, tiled=True).reshape(half, D)  16.3 us
    all_to_all x2, starting transfers between devices, deal(): return lax.all_to_all(x, 'dp', 0, 0, tiled=True).reshape(half, D)  11.7 us
    all_to_all x2, starting transfers between devices, undeal(): return lax.all_to_all(x.reshape(nd, hp, D), 'dp', 0, 0, tiled=True)  10.2 us
  transfers between devices with their start and end apart: 44, of which 18 were waited for; matrix products, arithmetic and copies ran while one was open for 9% of the time, Pallas kernels for 31%

profile of v4, /device:TPU:0, one launch (start us, length us, event | category | flops | bytes accessed | tf_op | source)
XLA Modules:
  0.0 407.1 jit_solution(13485155665392650133)
XLA Ops:
  10.5 3.0 collective-permute-start
  13.5 2.6 collective-permute-start.1
  21.2 8.1 %collective-permute-done.1 = bf16[1,1,112,768]{3,2,1,0:T(8,128)(2,1)S(1)} collective-permute-done((bf16[1,1,112,768]{3,2,1,0:T(8,128)(2,1)}, bf16[1,1,112,768]{3,2,1,0:T(8,128)(2,1)S(1)}, u32[]{:S(2)}, u32[]{:S(2)}) %collective-permute-start.1) | collective-permute-done | bytes 172064 | tf_op jit(solution)/shard_map/ppermute | solution.py:36
  30.3 6.3 %all-to-all-start = ((bf16[8,64,768]{2,1,0:T(8,128)(2,1)}), bf16[8,64,768]{2,1,0:T(8,128)(2,1)S(1)}, u32[]{:S(2)}, u32[]{:S(2)}) async-start(bf16[8,64,768]{2,1,0:T(8,128)(2,1)} %dynamic-slice_bitcast_fusion.1), calls=%async_computation | async-start | bytes 1572864 | tf_op jit(solution)/shard_map/all_to_all | solution.py:979
  38.7 3.0 collective-permute-start.6
  42.8 1.5 collective-permute-start.3
  44.4 1.5 collective-permute-start.4
  46.4 24.1 %collective-permute-done.6 = bf16[2,1,112,768]{3,2,0,1:T(8,128)(2,1)S(1)} collective-permute-done((bf16[2,1,112,768]{3,2,0,1:T(8,128)(2,1)S(1)}, bf16[2,1,112,768]{3,2,0,1:T(8,128)(2,1)S(1)}, u32[]{:S(2)}, u32[]{:S(2)}) %collective-permute-start.6) | collective-permute-done | bytes 344096 | tf_op jit(solution)/shard_map/ppermute | solution.py:36
  73.2 4.6 %collective-permute-done.5.rest_1_ = bf16[1,4,112,768]{3,2,1,0:T(8,128)(2,1)S(1)} collective-permute-done((bf16[1,4,112,768]{3,2,1,0:T(8,128)(2,1)S(1)}, bf16[1,4,112,768]{3,2,1,0:T(8,128)(2,1)S(1)}, u32[]{:S(2)}, u32[]{:S(2)}) %collective-permute-start.5) | collective-permute-done | bytes 688160 | tf_op jit(solution)/shard_map/ppermute | solution.py:36
  82.6 4.7 %collective-permute-done.9 = bf16[2,2,112,768]{3,2,0,1:T(8,128)(2,1)} collective-permute-done((bf16[2,2,112,768]{3,2,0,1:T(8,128)(2,1)}, bf16[2,2,112,768]{3,2,0,1:T(8,128)(2,1)}, u32[]{:S(2)}, u32[]{:S(2)}) %collective-permute-start.9) | collective-permute-done | bytes 688160 | tf_op jit(solution)/shard_map/ppermute | solution.py:36
  88.7 2.0 collective-permute-start.10
  90.7 1.5 collective-permute-start.11
  92.2 2.1 dynamic-slice_bitcast_fusion
  94.3 5.4 %all-to-all-start.1 = ((bf16[8,64,768]{2,1,0:T(8,128)(2,1)}), bf16[8,64,768]{2,1,0:T(8,128)(2,1)}, u32[]{:S(2)}, u32[]{:S(2)}) async-start(bf16[8,64,768]{2,1,0:T(8,128)(2,1)} %dynamic-slice_bitcast_fusion), calls=%async_computation.1 | async-start | bytes 1572864 | tf_op jit(solution)/shard_map/all_to_all | solution.py:979
  102.8 13.3 %attn_fwd.2 = (bf16[1024,640]{1,0:T(8,128)(2,1)S(1)}, bf16[768,768]{1,0:T(8,128)(2,1)S(1)}, bf16[1024,256]{1,0:T(8,128)(2,1)S(1)}, f32[8,1024]{1,0:T(8,128)S(1)}) custom-call(s32[4]{0:T(128)S(1)} %pad_add_fusion.info, bf16[512,768]{1,0:T(8,128)(2,1)S(1)} %bitcast.122, bf16[512,768]{1,0:T(8,128)(2,1)} %collective-permute-done.7.sib_ref.x1, ...), custom_call_target="tpu_custom_call" | custom-call | flops 11000000512 | bytes 6520848 | tf_op jit(solution)/shard_map/attn_fwd/pallas_call | solution.py:124
  117.2 14.0 %attn_fwd.3 = (bf16[1024,640]{1,0:T(8,128)(2,1)S(1)}, bf16[768,768]{1,0:T(8,128)(2,1)S(1)}, bf16[1024,256]{1,0:T(8,128)(2,1)S(1)}, f32[8,1024]{1,0:T(8,128)S(1)}) custom-call(s32[4]{0:T(128)S(1)} %pad_add_fusion.info, bf16[512,768]{1,0:T(8,128)(2,1)S(1)} %bitcast.123, bf16[512,768]{1,0:T(8,128)(2,1)} %collective-permute-done.7.sib_ref.x1, ...), custom_call_target="tpu_custom_call" | custom-call | flops 11000000512 | bytes 6520848 | tf_op jit(solution)/shard_map/attn_fwd/pallas_call | solution.py:124
  135.4 5.1 %ln1.1 = (f32[512,768]{1,0:T(8,128)}, bf16[512,768]{1,0:T(8,128)(2,1)}, f32[512,768]{1,0:T(8,128)}, f32[512,1]{1,0:T(8,128)}, f32[1,128]{1,0:T(1,128)}) custom-call(f32[512,768]{1,0:T(8,128)} %copy-done.10, bf16[512,768]{1,0:T(8,128)(2,1)} %collective-permute-done.8.got_ref, bf16[512,768]{1,0:T(8,128)(2,1)} %bitcast.124, bf16[512,128]{1,0:T(8,128)(2,1)} %slice.159.aux_ref, ...), custom_call_target="tpu_custom_call" | custom-call | bytes 3301376 | tf_op jit(solution)/shard_map/ln1/pallas_call | solution.py:155
  140.5 16.3 %all-to-all-done.1 = bf16[8,64,768]{2,1,0:T(8,128)(2,1)} async-done(((bf16[8,64,768]{2,1,0:T(8,128)(2,1)}), bf16[8,64,768]{2,1,0:T(8,128)(2,1)}, u32[]{:S(2)}, u32[]{:S(2)}) %all-to-all-start.1) | async-done | bytes 786464 | tf_op jit(solution)/shard_map/all_to_all | solution.py:979
  157.9 16.2 %ffn_up.2 = (bf16[512,1536]{1,0:T(8,128)(2,1)S(1)}, bf16[512,1536]{1,0:T(8,128)(2,1)S(1)}) custom-call(s32[4]{0:T(128)S(1)} %pad_add_fusion.info, bf16[512,768]{1,0:T(8,128)(2,1)S(1)} %copy-done.28, bf16[1024,128]{1,0:T(8,128)(2,1)S(1)} %copy-done.9, bf16[1024,128]{1,0:T(8,128)(2,1)S(1)} %copy-done.9, bf16[2,4,112,768]{3,2,1,0:T(8,128)(2,1)S(1)} %bitcast.112, ...), custom_call_target="tpu_custom_call" | custom-call | bytes 9961488 | tf_op jit(solution)/shard_map/ffn_up/pallas_call | solution.py:124
  175.4 6.1 %ffn_up.3 = (bf16[512,1536]{1,0:T(8,128)(2,1)S(1)}, bf16[512,1536]{1,0:T(8,128)(2,1)S(1)}) custom-call(s32[4]{0:T(128)S(1)} %pad_add_fusion.info, bf16[512,768]{1,0:T(8,128)(2,1)S(1)} %collective-permute-done.13.x_ref.first2, bf16[1024,128]{1,0:T(8,128)(2,1)S(1)} %copy-done.9, bf16[1024,128]{1,0:T(8,128)(2,1)S(1)} %copy-done.9, ...), custom_call_target="tpu_custom_call" | custom-call | bytes 9961488 | tf_op jit(solution)/shard_map/ffn_up/pallas_call | solution.py:124
  182.7 5.0 %product.5 = bf16[512,768]{1,0:T(8,128)(2,1)S(1)} custom-call(s32[4]{0:T(128)S(1)} %pad_add_fusion.info, bf16[512,1536]{1,0:T(8,128)(2,1)S(1)} %get-tuple-element.125.a_ref.act2, bf16[2,4,112,768]{3,2,1,0:T(8,128)(2,1)S(1)} %bitcast.114, bf16[2,4,112,768]{3,2,1,0:T(8,128)(2,1)S(1)} %collective-permute-done.10.rest_1_.a1, ...), custom_call_target="tpu_custom_call" | custom-call | bytes 7864336 | tf_op jit(solution)/shard_map/product/pallas_call | solution.py:124
  190.9 5.0 %product.4.part_ref = f32[512,768]{1,0:T(8,128)S(1)} custom-call(s32[4]{0:T(128)S(1)} %pad_add_fusion.info, bf16[512,1536]{1,0:T(8,128)(2,1)S(1)} %get-tuple-element.121.a_ref.act, bf16[2,4,112,768]{3,2,1,0:T(8,128)(2,1)S(1)} %bitcast.116, bf16[2,4,112,768]{3,2,1,0:T(8,128)(2,1)S(1)} %collective-permute-done.10.rest_1_.a1, ...), custom_call_target="tpu_custom_call" | custom-call | bytes 8650768 | tf_op jit(solution)/shard_map/product/pallas_call | solution.py:124
  197.9 5.9 %ln2.1 = (bf16[512,768]{1,0:T(8,128)(2,1)}, f32[512,768]{1,0:T(8,128)}, f32[512,1]{1,0:T(8,128)}, f32[512,128]{1,0:T(8,128)}, f32[512,128]{1,0:T(8,128)}, /*index=5*/f32[8,128]{1,0:T(8,128)}) custom-call(f32[512,768]{1,0:T(8,128)} %copy-done.20, bf16[512,768]{1,0:T(8,128)(2,1)} %copy-done.87, f32[512,768]{1,0:T(8,128)} %get-tuple-element.126.first_ref, ...), custom_call_target="tpu_custom_call" | custom-call | bytes 4288512 | tf_op jit(solution)/shard_map/ln2/pallas_call | solution.py:155
  203.9 6.4 %all-to-all-start.2 = ((bf16[8,64,768]{2,1,0:T(8,128)(2,1)}), bf16[8,64,768]{2,1,0:T(8,128)(2,1)}, u32[]{:S(2)}, u32[]{:S(2)}) async-start(bf16[8,64,768]{2,1,0:T(8,128)(2,1)} %bitcast.131), calls=%async_computation.2 | async-start | bytes 1572864 | tf_op jit(solution)/shard_map/all_to_all | solution.py:982
  212.1 7.4 %head.1 = (f32[512,768]{1,0:T(8,128)}, bf16[512,768]{1,0:T(8,128)(2,1)}, f32[768,128]{1,0:T(8,128)}, f32[128,128]{1,0:T(8,128)}, f32[128,128]{1,0:T(8,128)}, /*i...) custom-call(s32[4]{0:T(128)} %copy-done.60, f32[512,128]{1,0:T(8,128)} %get-tuple-element.130.st_ref, ...), custom_call_target="tpu_custom_call" | custom-call | bytes 4037632 | tf_op jit(solution)/shard_map/head/pallas_call | solution.py:155
  220.9 1.4 copy-done.44
  222.3 5.0 %ffn_back.2 = (bf16[512,1536]{1,0:T(8,128)(2,1)S(1)}, f32[8,1536]{1,0:T(8,128)S(1)}) custom-call(s32[4]{0:T(128)S(1)} %copy-done.61, bf16[512,768]{1,0:T(8,128)(2,1)S(1)} %copy-done.33, bf16[512,1536]{1,0:T(8,128)(2,1)S(1)} %copy-done.44, bf16[2,4,112,768]{3,2,1,0:T(8,128)(2,1)S(1)} %bitcast.117, ...), custom_call_target="tpu_custom_call" | custom-call | bytes 9486352 | tf_op jit(solution)/shard_map/ffn_back/pallas_call | solution.py:124
  229.4 1.4 all-to-all-done.2.a_ref
  230.7 1.5 collective-permute-start.15
  233.4 1.4 copy-done.42
  234.8 5.0 %ffn_back.3 = (bf16[512,1536]{1,0:T(8,128)(2,1)S(1)}, f32[8,1536]{1,0:T(8,128)S(1)}) custom-call(s32[4]{0:T(128)S(1)} %copy-done.61, bf16[512,768]{1,0:T(8,128)(2,1)S(1)} %copy-done.36, bf16[512,1536]{1,0:T(8,128)(2,1)S(1)} %copy-done.42, bf16[2,4,112,768]{3,2,1,0:T(8,128)(2,1)S(1)} %bitcast.118, ...), custom_call_target="tpu_custom_call" | custom-call | bytes 9486352 | tf_op jit(solution)/shard_map/ffn_back/pallas_call | solution.py:124
  239.9 5.0 %product.7 = bf16[512,768]{1,0:T(8,128)(2,1)S(1)} custom-call(s32[4]{0:T(128)S(1)} %copy-done.61, bf16[512,1536]{1,0:T(8,128)(2,1)S(1)} %get-tuple-element.146.a_ref.dpre2, bf16[2,4,112,768]{3,2,1,0:T(8,128)(2,1)S(1)} %bitcast.119, bf16[2,4,112,768]{3,2,1,0:T(8,128)(2,1)S(1)} %collective-permute-done.10.rest_1_.a1, ...), custom_call_target="tpu_custom_call" | custom-call | bytes 7864336 | tf_op jit(solution)/shard_map/product/pallas_call | solution.py:124
  244.9 5.0 %product.6.part_ref = f32[512,768]{1,0:T(8,128)S(1)} custom-call(s32[4]{0:T(128)S(1)} %copy-done.61, bf16[512,1536]{1,0:T(8,128)(2,1)S(1)} %copy-done.16, bf16[2,4,112,768]{3,2,1,0:T(8,128)(2,1)S(1)} %bitcast.120, bf16[2,4,112,768]{3,2,1,0:T(8,128)(2,1)S(1)} %collective-permute-done.10.rest_1_.a1, bf16[2,4,112,768]{3,2,1,0:T(8,128)(2,1)} %collective-permute-done.11.rest_2_, ...), custom_call_target="tpu_custom_call" | custom-call | bytes 8650768 | tf_op jit(solution)/shard_map/product/pallas_call | solution.py:124
  252.3 5.8 %ln1_back.1 = (f32[512,768]{1,0:T(8,128)}, bf16[512,768]{1,0:T(8,128)(2,1)}, f32[8,768]{1,0:T(8,128)}) custom-call(f32[512,768]{1,0:T(8,128)} %copy-done.21, bf16[512,768]{1,0:T(8,128)(2,1)} %copy-done.88, f32[512,768]{1,0:T(8,128)} %get-tuple-element.148.dr2_ref, f32[512,768]{1,0:T(8,128)} %get-tuple-element.149.n_ref, f32[512,1]{1,0:T(8,128)} %get-tuple-element.150.s_ref, ...), custom_call_target="tpu_custom_call" | custom-call | bytes 5531648 | tf_op jit(solution)/shard_map/ln1_back/pallas_call | solution.py:155
  260.4 1.4 collective-permute-done.21
  264.7 6.2 %ffn_grad.1 = (bf16[2,4,96,768]{3,2,1,0:T(8,128)(2,1)S(1)}, bf16[2,4,96,768]{3,2,1,0:T(8,128)(2,1)S(1)}, bf16[2,4,96,768]{3,2,1,0:T(8,128)(2,1)S(1)}, bf16[2,4,96,768]{3,2,1,0:T(8,128)(2,1)S(1)}) custom-call(s32[4]{0:T(128)S(1)} %copy-done.61, bf16[512,768]{1,0:T(8,128)(2,1)S(1)} %copy-done.29, bf16[512,768]{1,0:T(8,128)(2,1)S(1)} %copy-done.31, ...), custom_call_target="tpu_custom_call" | custom-call | bytes 14155792 | tf_op jit(solution)/shard_map/ffn_grad/pallas_call | solution.py:124
  271.0 1.6 collective-permute-start.24
  272.6 1.4 collective-permute-start.25
  276.2 8.7 %attn_bwd.2 = (bf16[1024,640]{1,0:T(8,128)(2,1)S(1)}, f32[8,640]{1,0:T(8,128)S(1)}) custom-call(bf16[1024,640]{1,0:T(8,128)(2,1)S(1)} %copy-done.80, bf16[768,768]{1,0:T(8,128)(2,1)S(1)} %copy-done.7, bf16[1024,128]{1,0:T(8,128)(2,1)S(1)} %copy-done.9, bf16[1024,256]{1,0:T(8,128)(2,1)S(1)} %copy-done.25, bf16[512,768]{1,0:T(8,128)(2,1)S(1)} %copy-done.32, ...), custom_call_target="tpu_custom_call" | custom-call | flops 11000000512 | bytes 6213632 | tf_op jit(solution)/shard_map/attn_bwd/pallas_call | solution.py:124
  284.9 4.1 qkv_grad.2
  289.1 8.5 %attn_bwd.3 = (bf16[1024,640]{1,0:T(8,128)(2,1)S(1)}, f32[8,640]{1,0:T(8,128)S(1)}) custom-call(bf16[1024,640]{1,0:T(8,128)(2,1)S(1)} %copy-done.78, bf16[768,768]{1,0:T(8,128)(2,1)S(1)} %copy-done.5, bf16[1024,128]{1,0:T(8,128)(2,1)S(1)} %copy-done.9, bf16[1024,256]{1,0:T(8,128)(2,1)S(1)} %copy-done.23, bf16[512,768]{1,0:T(8,128)(2,1)S(1)} %copy-done.32, ...), custom_call_target="tpu_custom_call" | custom-call | flops 11000000512 | bytes 6213632 | tf_op jit(solution)/shard_map/attn_bwd/pallas_call | solution.py:124
  297.6 2.4 collective-permute-done.24.ga_ref
  300.3 2.9 token_grad.1
  303.2 1.5 grad_half.1
  304.7 1.4 collective-permute-start.27
  306.6 1.5 collective-permute-start.30
  308.1 3.1 qkv_grad.3
  312.2 3.8 all-to-all-start.3
  316.0 8.4 %collective-permute-done.27.a_ref = bf16[4,96,768]{2,1,0:T(8,128)(2,1)} collective-permute-done((bf16[4,96,768]{2,1,0:T(8,128)(2,1)}, bf16[4,96,768]{2,1,0:T(8,128)(2,1)}, u32[]{:S(2)}, u32[]{:S(2)}) %collective-permute-start.27) | collective-permute-done | bytes 589856 | tf_op jit(solution)/shard_map/ppermute | solution.py:36
  324.4 1.6 grad_sum.2
  328.7 7.5 %collective-permute-done.30 = bf16[1,4,104,768]{3,2,1,0:T(8,128)(2,1)} collective-permute-done((bf16[1,4,104,768]{3,2,1,0:T(8,128)(2,1)}, bf16[1,4,104,768]{3,2,1,0:T(8,128)(2,1)}, u32[]{:S(2)}, u32[]{:S(2)}) %collective-permute-start.30) | collective-permute-done | bytes 639008 | tf_op jit(solution)/shard_map/ppermute | solution.py:36
  338.2 6.0 %collective-permute-done.37 = bf16[2,2,96,768]{3,2,1,0:T(8,128)(2,1)S(1)} collective-permute-done((bf16[2,2,96,768]{3,2,1,0:T(8,128)(2,1)S(1)}, bf16[2,2,96,768]{3,2,1,0:T(8,128)(2,1)S(1)}, u32[]{:S(2)}, u32[]{:S(2)}) %collective-permute-start.37) | collective-permute-done | bytes 589856 | tf_op jit(solution)/shard_map/ppermute | solution.py:36
  345.1 1.7 collective-permute-start.38
  346.8 2.3 collective-permute-done.29.refs_1_
  349.1 3.4 collective-permute-done.31.refs_2_
  353.5 5.6 %place.2 = bf16[8,2,2,64,768]{4,3,2,1,0:T(8,128)(2,1)} custom-call(s32[4]{0:T(128)S(1)} %copy-done.61, bf16[8,64,768]{2,1,0:T(8,128)(2,1)} %all-to-all-done.2.a_ref, bf16[8,64,768]{2,1,0:T(8,128)(2,1)S(1)} %copy-done.47, bf16[8,64,768]{2,1,0:T(8,128)(2,1)S(1)} %collective-permute-done.16.c_ref, bf16[8,64,768]{2,1,0:T(8,128)(2,1)S(1)} %collective-permute-done.17.d_ref), custom_call_target="tpu_custom_call" | custom-call | bytes 6000000 | tf_op jit(solution)/shard_map/place/pallas_call | solution.py:986
  362.4 2.9 collective-permute-done.35
  366.1 1.5 collective-permute-start.36
  368.5 7.7 %collective-permute-done.32.b_ref = bf16[8,64,768]{2,1,0:T(8,128)(2,1)S(1)} collective-permute-done((bf16[8,64,768]{2,1,0:T(8,128)(2,1)S(1)}, bf16[8,64,768]{2,1,0:T(8,128)(2,1)S(1)}, u32[]{:S(2)}, u32[]{:S(2)}) %collective-permute-start.32) | collective-permute-done | bytes 786464 | tf_op jit(solution)/shard_map/ppermute | solution.py:36
  376.2 4.1 %all-to-all-start.4 = ((bf16[8,224,128]{2,1,0:T(8,128)(2,1)}), bf16[8,224,128]{2,1,0:T(8,128)(2,1)}, u32[]{:S(2)}, u32[]{:S(2)}) async-start(bf16[8,224,128]{2,1,0:T(8,128)(2,1)} %convert_add_fusion), calls=%async_computation.4 | async-start | bytes 917504 | tf_op jit(solution)/shard_map/all_to_all | solution.py:1268
  382.9 1.8 copy.58
  384.7 1.8 copy.59
  387.3 1.6 copy.60
  396.6 3.8 place.3
  (338 shorter events, 91.8 us)
Async XLA Ops:
  0.7 28.6 %copy-start = (bf16[16,128,768]{2,1,0:T(8,128)(2,1)S(1)}, bf16[16,128,768]{2,1,0:T(8,128)(2,1)}, u32[]{:S(2)}) copy-start(bf16[16,128,768]{2,1,0:T(8,128)(2,1)} %param.23) | copy-start | bytes 9437188
  10.5 10.7 %collective-permute-start = (bf16[1,1,112,768]{3,2,1,0:T(8,128)(2,1)}, bf16[1,1,112,768]{3,2,1,0:T(8,128)(2,1)S(1)}, u32[]{:S(2)}, u32[]{:S(2)}) collective-permute-start(bf16[1,1,112,768]{3,2,1,0:T(8,128)(2,1)} %get-tuple-element.248), channel_id=1, source_target_pairs={{0,8},{1,9},{2,10},{3,11},{4,12},{5,13},{6,14},{7,15},{8,0},{9,1},... | collective-permute-start | bytes 516104 | tf_op jit(solution)/shard_map/ppermute | solution.py:36
  13.5 15.8 %collective-permute-start.1 = (bf16[1,1,112,768]{3,2,1,0:T(8,128)(2,1)}, bf16[1,1,112,768]{3,2,1,0:T(8,128)(2,1)S(1)}, u32[]{:S(2)}, u32[]{:S(2)}) collective-permute-start(bf16[1,1,112,768]{3,2,1,0:T(8,128)(2,1)} %get-tuple-element.248), channel_id=1, source_target_pairs={{0,16},{1,17},{2,18},{3,19},{4,20},{5,21},{6,22},{7,23},{8,24},{9,... | collective-permute-start | bytes 516104 | tf_op jit(solution)/shard_map/ppermute | solution.py:36
  16.1 13.2 %collective-permute-start.2 = (bf16[1,1,112,768]{3,2,1,0:T(8,128)(2,1)}, bf16[1,1,112,768]{3,2,1,0:T(8,128)(2,1)}, u32[]{:S(2)}, u32[]{:S(2)}) collective-permute-start(bf16[1,1,112,768]{3,2,1,0:T(8,128)(2,1)} %get-tuple-element.248), channel_id=1, source_target_pairs={{0,24},{1,25},{2,26},{3,27},{4,28},{5,29},{6,30},{7,31},{8,16},{9,... | collective-permute-start | bytes 516104 | tf_op jit(solution)/shard_map/ppermute | solution.py:36
  30.2 11.4 %copy-start.89 = (bf16[1,1,1,112,768]{4,3,2,1,0:T(8,128)(2,1)S(1)}, bf16[1,1,1,112,768]{4,3,2,1,0:T(8,128)(2,1)}, u32[]{:S(2)}) copy-start(bf16[1,1,1,112,768]{4,3,2,1,0:T(8,128)(2,1)} %get-tuple-element.247) | copy-start | bytes 516100
  30.3 47.5 %all-to-all-start = ((bf16[8,64,768]{2,1,0:T(8,128)(2,1)}), bf16[8,64,768]{2,1,0:T(8,128)(2,1)S(1)}, u32[]{:S(2)}, u32[]{:S(2)}) async-start(bf16[8,64,768]{2,1,0:T(8,128)(2,1)} %dynamic-slice_bitcast_fusion.1), calls=%async_computation | async-start | bytes 1572864 | tf_op jit(solution)/shard_map/all_to_all | solution.py:979
  38.7 31.8 %collective-permute-start.6 = (bf16[2,1,112,768]{3,2,0,1:T(8,128)(2,1)S(1)}, bf16[2,1,112,768]{3,2,0,1:T(8,128)(2,1)S(1)}, u32[]{:S(2)}, u32[]{:S(2)}) collective-permute-start(bf16[2,1,112,768]{3,2,0,1:T(8,128)(2,1)S(1)} %bitcast.135), channel_id=1, source_target_pairs={{0,16},{1,17},{2,18},{3,19},{4,20},{5,21},{6,22},{7,23},{8,24},{9,... | collective-permute-start | bytes 1032200 | tf_op jit(solution)/shard_map/ppermute | solution.py:36
  41.6 30.0 %copy-start.99 = (s32[16]{0:T(128)S(1)}, s32[16]{0:T(128)}, u32[]{:S(2)}) copy-start(s32[16]{0:T(128)} %param.26) | copy-start | bytes 196
  42.8 39.7 %copy-start.38 = (bf16[1,4,112,768]{3,2,1,0:T(8,128)(2,1)}, bf16[1,4,112,768]{3,2,1,0:T(8,128)(2,1)S(1)}, u32[]{:S(2)}) copy-start(bf16[1,4,112,768]{3,2,1,0:T(8,128)(2,1)S(1)} %maximum_bitcast_fusion.rest_0_.a0) | copy-start | bytes 2064388
  42.8 29.4 %collective-permute-start.3 = (bf16[1,4,112,768]{3,2,1,0:T(8,128)(2,1)S(1)}, bf16[1,4,112,768]{3,2,1,0:T(8,128)(2,1)S(1)}, u32[]{:S(2)}, u32[]{:S(2)}) collective-permute-start(bf16[1,4,112,768]{3,2,1,0:T(8,128)(2,1)S(1)} %maximum_bitcast_fusion.rest_0_.a0), channel_id=1, source_target_pairs={{0,4},{1,5},{2,6},{3,7},{4,0},{5,1},{6,2},{7,3},{8,12},{9,13},{10,... | collective-permute-start | bytes 2064392 | tf_op jit(solution)/shard_map/ppermute | solution.py:36
  44.4 27.9 %collective-permute-start.4 = (bf16[1,4,112,768]{3,2,1,0:T(8,128)(2,1)S(1)}, bf16[1,4,112,768]{3,2,1,0:T(8,128)(2,1)S(1)}, u32[]{:S(2)}, u32[]{:S(2)}) collective-permute-start(bf16[1,4,112,768]{3,2,1,0:T(8,128)(2,1)S(1)} %maximum_bitcast_fusion.rest_0_.a0), channel_id=1, source_target_pairs={{0,2},{1,3},{2,0},{3,1},{4,6},{5,7},{6,4},{7,5},{8,10},{9,11},{10,... | collective-permute-start | bytes 2064392 | tf_op jit(solution)/shard_map/ppermute | solution.py:36
  45.9 31.9 %collective-permute-start.5 = (bf16[1,4,112,768]{3,2,1,0:T(8,128)(2,1)S(1)}, bf16[1,4,112,768]{3,2,1,0:T(8,128)(2,1)S(1)}, u32[]{:S(2)}, u32[]{:S(2)}) collective-permute-start(bf16[1,4,112,768]{3,2,1,0:T(8,128)(2,1)S(1)} %maximum_bitcast_fusion.rest_0_.a0), channel_id=1, source_target_pairs={{0,6},{1,7},{2,4},{3,5},{4,2},{5,3},{6,0},{7,1},{8,14},{9,15},{10,... | collective-permute-start | bytes 2064392 | tf_op jit(solution)/shard_map/ppermute | solution.py:36
  71.7 15.6 %collective-permute-start.9 = (bf16[2,2,112,768]{3,2,0,1:T(8,128)(2,1)}, bf16[2,2,112,768]{3,2,0,1:T(8,128)(2,1)}, u32[]{:S(2)}, u32[]{:S(2)}) collective-permute-start(bf16[2,2,112,768]{3,2,0,1:T(8,128)(2,1)} %get-tuple-element.244), channel_id=1, source_target_pairs={{0,8},{1,9},{2,10},{3,11},{4,12},{5,13},{6,14},{7,15},{8,0},{9,1},... | collective-permute-start | bytes 2064392 | tf_op jit(solution)/shard_map/ppermute | solution.py:36
  72.3 15.0 %copy-start.54 = (bf16[1,4,112,768]{3,2,1,0:T(8,128)(2,1)}, bf16[1,4,112,768]{3,2,1,0:T(8,128)(2,1)S(1)}, u32[]{:S(2)}) copy-start(bf16[1,4,112,768]{3,2,1,0:T(8,128)(2,1)S(1)} %collective-permute-done.3.rest_1_.a1) | copy-start | bytes 2064388
  77.8 10.7 %copy-start.73 = (bf16[1,4,112,768]{3,2,1,0:T(8,128)(2,1)}, bf16[1,4,112,768]{3,2,1,0:T(8,128)(2,1)S(1)}, u32[]{:S(2)}) copy-start(bf16[1,4,112,768]{3,2,1,0:T(8,128)(2,1)S(1)} %collective-permute-done.5.rest_1_) | copy-start | bytes 2064388
  77.8 39.4 %copy-start.2 = (bf16[8,64,768]{2,1,0:T(8,128)(2,1)}, bf16[8,64,768]{2,1,0:T(8,128)(2,1)S(1)}, u32[]{:S(2)}) copy-start(bf16[8,64,768]{2,1,0:T(8,128)(2,1)S(1)} %all-to-all-done) | copy-start | bytes 2359300
  77.8 21.9 %collective-permute-start.7 = (bf16[512,768]{1,0:T(8,128)(2,1)S(1)}, bf16[512,768]{1,0:T(8,128)(2,1)}, u32[]{:S(2)}, u32[]{:S(2)}) collective-permute-start(bf16[512,768]{1,0:T(8,128)(2,1)S(1)} %bitcast.121), channel_id=1, source_target_pairs={{0,1},{1,0},{2,3},{3,2},{4,5},{5,4},{6,7},{7,6},{8,9},{9,8},{10,11... | collective-permute-start | bytes 2359304 | tf_op jit(solution)/shard_map/ppermute | solution.py:36
  78.6 110.9 %copy-start.60 = (s32[4]{0:T(128)}, s32[4]{0:T(128)S(1)}, u32[]{:S(2)}) copy-start(s32[4]{0:T(128)S(1)} %pad_add_fusion.info) | copy-start | bytes 52
  88.7 51.8 %collective-permute-start.10 = (bf16[2,4,112,768]{3,2,1,0:T(8,128)(2,1)S(1)}, bf16[2,4,112,768]{3,2,1,0:T(8,128)(2,1)S(1)}, u32[]{:S(2)}, u32[]{:S(2)}) collective-permute-start(bf16[2,4,112,768]{3,2,1,0:T(8,128)(2,1)S(1)} %bitcast.109), channel_id=1, source_target_pairs={{0,4},{1,5},{2,6},{3,7},{4,0},{5,1},{6,2},{7,3},{8,12},{9,13},{10,... | collective-permute-start | bytes 4128776 | tf_op jit(solution)/shard_map/ppermute | solution.py:36
  90.7 66.1 %collective-permute-start.11 = (bf16[2,4,112,768]{3,2,1,0:T(8,128)(2,1)S(1)}, bf16[2,4,112,768]{3,2,1,0:T(8,128)(2,1)}, u32[]{:S(2)}, u32[]{:S(2)}) collective-permute-start(bf16[2,4,112,768]{3,2,1,0:T(8,128)(2,1)S(1)} %bitcast.110), channel_id=1, source_target_pairs={{0,2},{1,3},{2,0},{3,1},{4,6},{5,7},{6,4},{7,5},{8,10},{9,11},{10,... | collective-permute-start | bytes 4128776 | tf_op jit(solution)/shard_map/ppermute | solution.py:36
  92.2 64.6 %collective-permute-start.12 = (bf16[2,4,112,768]{3,2,1,0:T(8,128)(2,1)S(1)}, bf16[2,4,112,768]{3,2,1,0:T(8,128)(2,1)}, u32[]{:S(2)}, u32[]{:S(2)}) collective-permute-start(bf16[2,4,112,768]{3,2,1,0:T(8,128)(2,1)S(1)} %bitcast.111), channel_id=1, source_target_pairs={{0,6},{1,7},{2,4},{3,5},{4,2},{5,3},{6,0},{7,1},{8,14},{9,15},{10,... | collective-permute-start | bytes 4128776 | tf_op jit(solution)/shard_map/ppermute | solution.py:36
  94.3 62.5 %all-to-all-start.1 = ((bf16[8,64,768]{2,1,0:T(8,128)(2,1)}), bf16[8,64,768]{2,1,0:T(8,128)(2,1)}, u32[]{:S(2)}, u32[]{:S(2)}) async-start(bf16[8,64,768]{2,1,0:T(8,128)(2,1)} %dynamic-slice_bitcast_fusion), calls=%async_computation.1 | async-start | bytes 1572864 | tf_op jit(solution)/shard_map/all_to_all | solution.py:979
  102.8 14.4 %copy-start.72 = (bf16[1,4,112,768]{3,2,1,0:T(8,128)(2,1)S(1)}, bf16[1,4,112,768]{3,2,1,0:T(8,128)(2,1)}, u32[]{:S(2)}) copy-start(bf16[1,4,112,768]{3,2,1,0:T(8,128)(2,1)} %copy-done.71) | copy-start | bytes 2064388
  102.8 14.4 %copy-start.74 = (bf16[1,4,112,768]{3,2,1,0:T(8,128)(2,1)S(1)}, bf16[1,4,112,768]{3,2,1,0:T(8,128)(2,1)}, u32[]{:S(2)}) copy-start(bf16[1,4,112,768]{3,2,1,0:T(8,128)(2,1)} %copy-done.73) | copy-start | bytes 2064388
  117.2 14.0 %copy-start.81 = (f32[8,1024]{1,0:T(8,128)}, f32[8,1024]{1,0:T(8,128)S(1)}, u32[]{:S(2)}) copy-start(f32[8,1024]{1,0:T(8,128)S(1)} %get-tuple-element.172.lse_ref) | copy-start | bytes 98308
  117.2 16.4 %copy-start.4 = (bf16[768,768]{1,0:T(8,128)(2,1)}, bf16[768,768]{1,0:T(8,128)(2,1)S(1)}, u32[]{:S(2)}) copy-start(bf16[768,768]{1,0:T(8,128)(2,1)S(1)} %get-tuple-element.118.w0_ref.w_ref) | copy-start | bytes 3538948
  117.2 16.4 %copy-start.22 = (bf16[1024,256]{1,0:T(8,128)(2,1)}, bf16[1024,256]{1,0:T(8,128)(2,1)S(1)}, u32[]{:S(2)}) copy-start(bf16[1024,256]{1,0:T(8,128)(2,1)S(1)} %get-tuple-element.113.c0_ref.ctx_ref) | copy-start | bytes 1572868
  132.9 2.5 collective-permute-start.8
  156.8 18.6 %collective-permute-start.13 = (bf16[512,768]{1,0:T(8,128)(2,1)}, bf16[512,768]{1,0:T(8,128)(2,1)S(1)}, u32[]{:S(2)}, u32[]{:S(2)}) collective-permute-start(bf16[512,768]{1,0:T(8,128)(2,1)} %get-tuple-element.123.x_ref.first), channel_id=1, source_target_pairs={{0,1},{1,0},{2,3},{3,2},{4,5},{5,4},{6,7},{7,6},{8,9},{9,8},{10,11... | collective-permute-start | bytes 2359304 | tf_op jit(solution)/shard_map/ppermute | solution.py:36
  175.4 14.2 %copy-start.11 = (bf16[512,1536]{1,0:T(8,128)(2,1)}, bf16[512,1536]{1,0:T(8,128)(2,1)S(1)}, u32[]{:S(2)}) copy-start(bf16[512,1536]{1,0:T(8,128)(2,1)S(1)} %get-tuple-element.121.a_ref.act) | copy-start | bytes 4718596
  187.7 9.3 %collective-permute-start.14 = (bf16[512,768]{1,0:T(8,128)(2,1)S(1)}, bf16[512,768]{1,0:T(8,128)(2,1)S(1)}, u32[]{:S(2)}, u32[]{:S(2)}) collective-permute-start(bf16[512,768]{1,0:T(8,128)(2,1)S(1)} %product.5), channel_id=1, source_target_pairs={{0,1},{1,0},{2,3},{3,2},{4,5},{5,4},{6,7},{7,6},{8,9},{9,8},{10,11... | collective-permute-start | bytes 2359304 | tf_op jit(solution)/shard_map/ppermute | solution.py:36
  203.9 26.9 %all-to-all-start.2 = ((bf16[8,64,768]{2,1,0:T(8,128)(2,1)}), bf16[8,64,768]{2,1,0:T(8,128)(2,1)}, u32[]{:S(2)}, u32[]{:S(2)}) async-start(bf16[8,64,768]{2,1,0:T(8,128)(2,1)} %bitcast.131), calls=%async_computation.2 | async-start | bytes 1572864 | tf_op jit(solution)/shard_map/all_to_all | solution.py:982
  210.3 1.2 collective-permute-start.18
  219.5 9.0 %collective-permute-start.19 = (bf16[512,768]{1,0:T(8,128)(2,1)}, bf16[512,768]{1,0:T(8,128)(2,1)S(1)}, u32[]{:S(2)}, u32[]{:S(2)}) collective-permute-start(bf16[512,768]{1,0:T(8,128)(2,1)} %get-tuple-element.141.g_ref.dffn), channel_id=1, source_target_pairs={{0,1},{1,0},{2,3},{3,2},{4,5},{5,4},{6,7},{7,6},{8,9},{9,8},{10,11... | collective-permute-start | bytes 2359304 | tf_op jit(solution)/shard_map/ppermute | solution.py:36
  230.7 20.3 %collective-permute-start.15 = (bf16[8,64,768]{2,1,0:T(8,128)(2,1)}, bf16[8,64,768]{2,1,0:T(8,128)(2,1)S(1)}, u32[]{:S(2)}, u32[]{:S(2)}) collective-permute-start(bf16[8,64,768]{2,1,0:T(8,128)(2,1)} %all-to-all-done.2.a_ref), channel_id=1, source_target_pairs={{0,2},{1,3},{2,0},{3,1},{4,6},{5,7},{6,4},{7,5},{8,10},{9,11},{10,... | collective-permute-start | bytes 2359304 | tf_op jit(solution)/shard_map/ppermute | solution.py:36
  244.9 6.2 %collective-permute-start.20 = (bf16[512,768]{1,0:T(8,128)(2,1)S(1)}, bf16[512,768]{1,0:T(8,128)(2,1)S(1)}, u32[]{:S(2)}, u32[]{:S(2)}) collective-permute-start(bf16[512,768]{1,0:T(8,128)(2,1)S(1)} %product.7), channel_id=1, source_target_pairs={{0,1},{1,0},{2,3},{3,2},{4,5},{5,4},{6,7},{7,6},{8,9},{9,8},{10,11... | collective-permute-start | bytes 2359304 | tf_op jit(solution)/shard_map/ppermute | solution.py:36
  252.3 10.1 %copy-start.19 = (bf16[512,1536]{1,0:T(8,128)(2,1)S(1)}, bf16[512,1536]{1,0:T(8,128)(2,1)}, u32[]{:S(2)}) copy-start(bf16[512,1536]{1,0:T(8,128)(2,1)} %copy-done.18) | copy-start | bytes 4718596
  252.3 10.1 %copy-start.29 = (bf16[512,768]{1,0:T(8,128)(2,1)S(1)}, bf16[512,768]{1,0:T(8,128)(2,1)}, u32[]{:S(2)}) copy-start(bf16[512,768]{1,0:T(8,128)(2,1)} %get-tuple-element.123.x_ref.first) | copy-start | bytes 2359300
  259.7 2.0 collective-permute-start.21
  260.3 13.7 %collective-permute-start.23 = (bf16[512,768]{1,0:T(8,128)(2,1)}, bf16[512,768]{1,0:T(8,128)(2,1)S(1)}, u32[]{:S(2)}, u32[]{:S(2)}) collective-permute-start(bf16[512,768]{1,0:T(8,128)(2,1)} %get-tuple-element.158.da_ref.da), channel_id=1, source_target_pairs={{0,1},{1,0},{2,3},{3,2},{4,5},{5,4},{6,7},{7,6},{8,9},{9,8},{10,11... | collective-permute-start | bytes 2359304 | tf_op jit(solution)/shard_map/ppermute | solution.py:36
  261.8 13.4 %collective-permute-start.22 = (bf16[8,224,128]{2,1,0:T(8,128)(2,1)S(1)}, bf16[8,224,128]{2,1,0:T(8,128)(2,1)S(1)}, u32[]{:S(2)}, u32[]{:S(2)}) collective-permute-start(bf16[8,224,128]{2,1,0:T(8,128)(2,1)S(1)} %fusion), channel_id=1, source_target_pairs={{0,2},{1,3},{2,0},{3,1},{4,6},{5,7},{6,4},{7,5},{8,10},{9,11},{10,... | collective-permute-start | bytes 1376264 | tf_op jit(solution)/shard_map/ppermute | solution.py:36
  264.7 11.5 %copy-start.32 = (bf16[512,768]{1,0:T(8,128)(2,1)S(1)}, bf16[512,768]{1,0:T(8,128)(2,1)}, u32[]{:S(2)}) copy-start(bf16[512,768]{1,0:T(8,128)(2,1)} %get-tuple-element.158.da_ref.da) | copy-start | bytes 2359300
  264.7 11.5 %copy-start.80 = (bf16[1024,640]{1,0:T(8,128)(2,1)S(1)}, bf16[1024,640]{1,0:T(8,128)(2,1)}, u32[]{:S(2)}) copy-start(bf16[1024,640]{1,0:T(8,128)(2,1)} %copy-done.79) | copy-start | bytes 3932164
  271.0 29.0 %collective-permute-start.24 = (bf16[2,4,96,768]{3,2,1,0:T(8,128)(2,1)S(1)}, bf16[2,4,96,768]{3,2,1,0:T(8,128)(2,1)S(1)}, u32[]{:S(2)}, u32[]{:S(2)}) collective-permute-start(bf16[2,4,96,768]{3,2,1,0:T(8,128)(2,1)S(1)} %get-tuple-element.160), channel_id=1, source_target_pairs={{0,2},{1,3},{2,0},{3,1},{4,6},{5,7},{6,4},{7,5},{8,10},{9,11},{10,... | collective-permute-start | bytes 3538952 | tf_op jit(solution)/shard_map/ppermute | solution.py:36
  272.6 27.7 %collective-permute-start.25 = (bf16[2,4,96,768]{3,2,1,0:T(8,128)(2,1)S(1)}, bf16[2,4,96,768]{3,2,1,0:T(8,128)(2,1)S(1)}, u32[]{:S(2)}, u32[]{:S(2)}) collective-permute-start(bf16[2,4,96,768]{3,2,1,0:T(8,128)(2,1)S(1)} %get-tuple-element.162), channel_id=1, source_target_pairs={{0,4},{1,5},{2,6},{3,7},{4,0},{5,1},{6,2},{7,3},{8,12},{9,13},{10,... | collective-permute-start | bytes 3538952 | tf_op jit(solution)/shard_map/ppermute | solution.py:36
  289.0 11.2 %copy-start.40 = (f32[512,768]{1,0:T(8,128)S(1)}, f32[512,768]{1,0:T(8,128)}, u32[]{:S(2)}) copy-start(f32[512,768]{1,0:T(8,128)} %get-tuple-element.175.dr1_ref) | copy-start | bytes 4718596
  303.1 8.0 %collective-permute-start.26 = (bf16[512,768]{1,0:T(8,128)(2,1)S(1)}, bf16[512,768]{1,0:T(8,128)(2,1)S(1)}, u32[]{:S(2)}, u32[]{:S(2)}) collective-permute-start(bf16[512,768]{1,0:T(8,128)(2,1)S(1)} %get-tuple-element.177), channel_id=1, source_target_pairs={{0,1},{1,0},{2,3},{3,2},{4,5},{5,4},{6,7},{7,6},{8,9},{9,8},{10,11... | collective-permute-start | bytes 2359304 | tf_op jit(solution)/shard_map/ppermute | solution.py:36
  304.7 19.7 %collective-permute-start.27 = (bf16[4,96,768]{2,1,0:T(8,128)(2,1)}, bf16[4,96,768]{2,1,0:T(8,128)(2,1)}, u32[]{:S(2)}, u32[]{:S(2)}) collective-permute-start(bf16[4,96,768]{2,1,0:T(8,128)(2,1)} %get-tuple-element.185), channel_id=1, source_target_pairs={{0,4},{1,5},{2,6},{3,7},{4,0},{5,1},{6,2},{7,3},{8,12},{9,13},{10,... | collective-permute-start | bytes 1769480 | tf_op jit(solution)/shard_map/ppermute | solution.py:36
  306.0 18.3 %collective-permute-start.28 = (bf16[4,96,768]{2,1,0:T(8,128)(2,1)}, bf16[4,96,768]{2,1,0:T(8,128)(2,1)}, u32[]{:S(2)}, u32[]{:S(2)}) collective-permute-start(bf16[4,96,768]{2,1,0:T(8,128)(2,1)} %get-tuple-element.186), channel_id=1, source_target_pairs={{0,2},{1,3},{2,0},{3,1},{4,6},{5,7},{6,4},{7,5},{8,10},{9,11},{10,... | collective-permute-start | bytes 1769480 | tf_op jit(solution)/shard_map/ppermute | solution.py:36
  306.6 29.7 %collective-permute-start.30 = (bf16[1,4,104,768]{3,2,1,0:T(8,128)(2,1)}, bf16[1,4,104,768]{3,2,1,0:T(8,128)(2,1)}, u32[]{:S(2)}, u32[]{:S(2)}) collective-permute-start(bf16[1,4,104,768]{3,2,1,0:T(8,128)(2,1)} %get-tuple-element.170), channel_id=1, source_target_pairs={{0,2},{1,3},{2,0},{3,1},{4,6},{5,7},{6,4},{7,5},{8,10},{9,11},{10,... | collective-permute-start | bytes 1916936 | tf_op jit(solution)/shard_map/ppermute | solution.py:36
  312.2 46.9 %all-to-all-start.3 = ((bf16[8,64,768]{2,1,0:T(8,128)(2,1)}), bf16[8,64,768]{2,1,0:T(8,128)(2,1)S(1)}, u32[]{:S(2)}, u32[]{:S(2)}) async-start(bf16[8,64,768]{2,1,0:T(8,128)(2,1)} %bitcast.134), calls=%async_computation.3 | async-start | bytes 1572864 | tf_op jit(solution)/shard_map/all_to_all | solution.py:982
  326.8 17.4 %collective-permute-start.37 = (bf16[2,2,96,768]{3,2,1,0:T(8,128)(2,1)S(1)}, bf16[2,2,96,768]{3,2,1,0:T(8,128)(2,1)S(1)}, u32[]{:S(2)}, u32[]{:S(2)}) collective-permute-start(bf16[2,2,96,768]{3,2,1,0:T(8,128)(2,1)S(1)} %pad_maximum_fusion.2), channel_id=1, source_target_pairs={{0,8},{1,9},{2,10},{3,11},{4,12},{5,13},{6,14},{7,15},{8,0},{9,1},... | collective-permute-start | bytes 1769480 | tf_op jit(solution)/shard_map/ppermute | solution.py:36
  327.3 26.2 %collective-permute-start.16 = (bf16[8,64,768]{2,1,0:T(8,128)(2,1)}, bf16[8,64,768]{2,1,0:T(8,128)(2,1)S(1)}, u32[]{:S(2)}, u32[]{:S(2)}) collective-permute-start(bf16[8,64,768]{2,1,0:T(8,128)(2,1)} %all-to-all-done.2.a_ref), channel_id=1, source_target_pairs={{0,1},{1,0},{2,3},{3,2},{4,5},{5,4},{6,7},{7,6},{8,9},{9,8},{10,11... | collective-permute-start | bytes 2359304 | tf_op jit(solution)/shard_map/ppermute | solution.py:36
  327.3 26.2 %collective-permute-start.17 = (bf16[8,64,768]{2,1,0:T(8,128)(2,1)S(1)}, bf16[8,64,768]{2,1,0:T(8,128)(2,1)S(1)}, u32[]{:S(2)}, u32[]{:S(2)}) collective-permute-start(bf16[8,64,768]{2,1,0:T(8,128)(2,1)S(1)} %copy-done.47), channel_id=1, source_target_pairs={{0,1},{1,0},{2,3},{3,2},{4,5},{5,4},{6,7},{7,6},{8,9},{9,8},{10,11... | collective-permute-start | bytes 2359304 | tf_op jit(solution)/shard_map/ppermute | solution.py:36
  327.8 21.2 %collective-permute-start.29 = (bf16[1,4,104,768]{3,2,1,0:T(8,128)(2,1)S(1)}, bf16[1,4,104,768]{3,2,1,0:T(8,128)(2,1)S(1)}, u32[]{:S(2)}, u32[]{:S(2)}) collective-permute-start(bf16[1,4,104,768]{3,2,1,0:T(8,128)(2,1)S(1)} %copy-done.76), channel_id=1, source_target_pairs={{0,2},{1,3},{2,0},{3,1},{4,6},{5,7},{6,4},{7,5},{8,10},{9,11},{10,... | collective-permute-start | bytes 1916936 | tf_op jit(solution)/shard_map/ppermute | solution.py:36
  337.4 15.0 %collective-permute-start.31 = (bf16[1,4,104,768]{3,2,1,0:T(8,128)(2,1)S(1)}, bf16[1,4,104,768]{3,2,1,0:T(8,128)(2,1)S(1)}, u32[]{:S(2)}, u32[]{:S(2)}) collective-permute-start(bf16[1,4,104,768]{3,2,1,0:T(8,128)(2,1)S(1)} %add_convert_fusion.1), channel_id=1, source_target_pairs={{0,4},{1,5},{2,6},{3,7},{4,0},{5,1},{6,2},{7,3},{8,12},{9,13},{10,... | collective-permute-start | bytes 1916936 | tf_op jit(solution)/shard_map/ppermute | solution.py:36
  345.1 16.2 %collective-permute-start.38 = (bf16[2,96,768]{2,1,0:T(8,128)(2,1)}, bf16[2,96,768]{2,1,0:T(8,128)(2,1)}, u32[]{:S(2)}, u32[]{:S(2)}) collective-permute-start(bf16[2,96,768]{2,1,0:T(8,128)(2,1)} %fusion.1), channel_id=1, source_target_pairs={{0,16},{1,17},{2,18},{3,19},{4,20},{5,21},{6,22},{7,23},{8,24},{9,... | collective-permute-start | bytes 884744 | tf_op jit(solution)/shard_map/ppermute | solution.py:36
  352.8 12.5 %collective-permute-start.35 = (bf16[2,1,104,768]{3,2,1,0:T(8,128)(2,1)S(1)}, bf16[2,1,104,768]{3,2,1,0:T(8,128)(2,1)S(1)}, u32[]{:S(2)}, u32[]{:S(2)}) collective-permute-start(bf16[2,1,104,768]{3,2,1,0:T(8,128)(2,1)S(1)} %pad_maximum_fusion.4), channel_id=1, source_target_pairs={{0,8},{1,9},{2,10},{3,11},{4,12},{5,13},{6,14},{7,15},{8,0},{9,1},... | collective-permute-start | bytes 958472 | tf_op jit(solution)/shard_map/ppermute | solution.py:36
  359.1 17.0 %collective-permute-start.32 = (bf16[8,64,768]{2,1,0:T(8,128)(2,1)S(1)}, bf16[8,64,768]{2,1,0:T(8,128)(2,1)S(1)}, u32[]{:S(2)}, u32[]{:S(2)}) collective-permute-start(bf16[8,64,768]{2,1,0:T(8,128)(2,1)S(1)} %all-to-all-done.3.a_ref), channel_id=1, source_target_pairs={{0,2},{1,3},{2,0},{3,1},{4,6},{5,7},{6,4},{7,5},{8,10},{9,11},{10,... | collective-permute-start | bytes 2359304 | tf_op jit(solution)/shard_map/ppermute | solution.py:36
  366.1 14.3 %collective-permute-start.36 = (bf16[1,104,768]{2,1,0:T(8,128)(2,1)}, bf16[1,104,768]{2,1,0:T(8,128)(2,1)}, u32[]{:S(2)}, u32[]{:S(2)}) collective-permute-start(bf16[1,104,768]{2,1,0:T(8,128)(2,1)} %fusion.8), channel_id=1, source_target_pairs={{0,16},{1,17},{2,18},{3,19},{4,20},{5,21},{6,22},{7,23},{8,24},{9,... | collective-permute-start | bytes 479240 | tf_op jit(solution)/shard_map/ppermute | solution.py:36
  368.5 21.8 %collective-permute-start.33 = (bf16[8,64,768]{2,1,0:T(8,128)(2,1)S(1)}, bf16[8,64,768]{2,1,0:T(8,128)(2,1)S(1)}, u32[]{:S(2)}, u32[]{:S(2)}) collective-permute-start(bf16[8,64,768]{2,1,0:T(8,128)(2,1)S(1)} %all-to-all-done.3.a_ref), channel_id=1, source_target_pairs={{0,1},{1,0},{2,3},{3,2},{4,5},{5,4},{6,7},{7,6},{8,9},{9,8},{10,11... | collective-permute-start | bytes 2359304 | tf_op jit(solution)/shard_map/ppermute | solution.py:36
  376.2 24.2 %all-to-all-start.4 = ((bf16[8,224,128]{2,1,0:T(8,128)(2,1)}), bf16[8,224,128]{2,1,0:T(8,128)(2,1)}, u32[]{:S(2)}, u32[]{:S(2)}) async-start(bf16[8,224,128]{2,1,0:T(8,128)(2,1)} %convert_add_fusion), calls=%async_computation.4 | async-start | bytes 917504 | tf_op jit(solution)/shard_map/all_to_all | solution.py:1268
  380.3 10.9 %collective-permute-start.34 = (bf16[8,64,768]{2,1,0:T(8,128)(2,1)S(1)}, bf16[8,64,768]{2,1,0:T(8,128)(2,1)S(1)}, u32[]{:S(2)}, u32[]{:S(2)}) collective-permute-start(bf16[8,64,768]{2,1,0:T(8,128)(2,1)S(1)} %collective-permute-done.32.b_ref), channel_id=1, source_target_pairs={{0,1},{1,0},{2,3},{3,2},{4,5},{5,4},{6,7},{7,6},{8,9},{9,8},{10,11... | collective-permute-start | bytes 2359304 | tf_op jit(solution)/shard_map/ppermute | solution.py:36
  396.6 10.3 %copy-start.1 = (bf16[16,128,768]{2,1,0:T(8,128)(2,1)S(1)}, bf16[16,128,768]{2,1,0:T(8,128)(2,1)}, u32[]{:S(2)}) copy-start(bf16[16,128,768]{2,1,0:T(8,128)(2,1)} %param.23) | copy-start | bytes 9437188
  (82 other events, 298.6 us)
